TPU v7x, 128 devices: a whole 4x4x4 slice. The times are simulated.
128 devices in a mesh: req: 8 (over x, z_lo), blk: 16 (over y, z_hi, core).
Axes of the slice: x: 4, y: 4, z: 4 (z_hi: 2, z_lo: 2; z = z_hi * 2 + z_lo), core: 2. Of those that a mesh axis runs over, the one named last changes fastest.
Arguments:
- new_states: bfloat16 [4096, 1024], P('req'), may hold values from -50 to 50
- encoder_out: bfloat16 [4096, 1024], P('req'), may hold values from -90 to 90
- cache_in: bfloat16 [8, 4096, 2048], P(None, 'blk', 'req'), may hold values from -90 to 90
- slot_order: int32 [8], replicated, may hold values from 0 to 7, each once
- new_lengths: int32 [8], replicated, may hold values from 1 to 512, 2560 in all
- cache_lengths: int32 [8], replicated, may hold values from 1 to 4096, 16384 in all
- enc_lengths: int32 [8], replicated, may hold values from 1 to 512, 3072 in all
- bucket_of: int32 [4608], replicated, may hold values from 0 to 31, as said below
- rel_bias: float32 [32, 16], replicated, may hold values from -4 to 4
- norm_gain: float32 [3, 1024], replicated, may hold values from 0.25 to 1.75
- self_q: bfloat16 [1024, 1024], P('req', 'blk'), may hold values from -0.09375 to 0.09375
- self_kv: bfloat16 [1024, 2, 1024], P('req', None, 'blk'), may hold values from -0.1875 to 0.1875
- self_out: bfloat16 [1024, 1024], P('blk', 'req'), may hold values from -0.1875 to 0.1875
- cross_q: bfloat16 [1024, 1024], P('req', 'blk'), may hold values from -0.09375 to 0.09375
- cross_kv: bfloat16 [1024, 2, 1024], P('req', None, 'blk'), may hold values from -0.1875 to 0.1875
- cross_out: bfloat16 [1024, 1024], P('blk', 'req'), may hold values from -0.1875 to 0.1875
- ff_in: bfloat16 [1024, 2, 2816], P('req', None, 'blk'), may hold values from -0.1875 to 0.1875
- ff_out: bfloat16 [2816, 1024], P('blk', 'req'), may hold values from -0.109375 to 0.109375
Outputs:
- layer_out: bfloat16 [4096, 1024], P('req')
- cache_out: bfloat16 [8, 4096, 2048], P('req', None, 'blk')
Inputs may be any that keep to these rules, and one draw needn't show every extreme that they name: Slot s holds request slot_order[s]; every request is held once. `new_lengths`: they sum to 2560 and the most is 512. `cache_lengths`: they sum to 16384 and the most is 4096. `enc_lengths`: they sum to 3072 and the most is 512. `bucket_of`: non-decreasing in the distance, 0 at distance 0 and 31 at distance 4608 - 1.
All inputs are finite; a program needn't handle non-finite values.
Results may differ from a plain program's by a relative error of at most 0.035.
Values may be sent and summed in bfloat16 or wider, within the bound.
A program may use at most 128 MiB of HBM per device.

v0:
```python
import jax
import jax.numpy as jnp
from jax import lax
from jax.sharding import PartitionSpec as P

H = 16
HD = 64


EPSILON = 1e-06
NEG_FILL = -1e30


def rms_rows(row_block, gain):
    mean_square = jnp.mean(row_block * row_block, axis=-1, keepdims=True)
    return (row_block * lax.rsqrt(mean_square + EPSILON) * gain).astype(jnp.bfloat16)


def softmax_rows(scores):
    row_top = jnp.max(scores, axis=-1, keepdims=True)
    weights = jnp.exp(scores - row_top)
    return (weights / jnp.sum(weights, axis=-1, keepdims=True)).astype(jnp.bfloat16)


def pick_lengths(table, own_slots):
    matches = own_slots[:, None] == jnp.arange(table.shape[0], dtype=jnp.int32)[None, :]
    return jnp.sum(jnp.where(matches, table[None, :], 0), axis=1)


def shifted_bias(bias_dist, base, row_count, col_count):
    heads_here, span_len = bias_dist.shape
    line_len = row_count + col_count - 1
    steps = jnp.arange(line_len + 1, dtype=jnp.int32)
    line = bias_dist[:, jnp.clip(base + row_count - 1 - steps, 0, span_len - 1)]
    tiled = jnp.broadcast_to(line[:, None, :], (heads_here, row_count, line_len + 1))
    flat = tiled.reshape(heads_here, row_count * (line_len + 1))[:, : row_count * line_len]
    skewed = flat.reshape(heads_here, row_count, line_len)
    return skewed[:, :, row_count - 1 : row_count - 1 + col_count]


def row_total(left, weight):
    term = jnp.dot(left, weight, preferred_element_type=jnp.float32)
    return lax.psum(term.astype(jnp.bfloat16), "blk").astype(jnp.float32)


def cached_scores(queries, key_rows, first_col, old_len, bias_dist):
    col_ids = first_col + jnp.arange(key_rows.shape[0], dtype=jnp.int32)[None, :]
    scores = jnp.einsum("qhe,khe->hqk", queries, key_rows, preferred_element_type=jnp.float32)
    scores = scores + shifted_bias(
        bias_dist, old_len - first_col, queries.shape[0], key_rows.shape[0]
    )
    return jnp.where((col_ids < old_len)[None], scores, NEG_FILL)


def fresh_scores(queries, fresh_keys, fresh_len, bias_dist):
    row_ids = jnp.arange(queries.shape[0], dtype=jnp.int32)[:, None]
    col_ids = jnp.arange(fresh_keys.shape[0], dtype=jnp.int32)[None, :]
    scores = jnp.einsum("qhe,khe->hqk", queries, fresh_keys, preferred_element_type=jnp.float32)
    scores = scores + shifted_bias(bias_dist, 0, queries.shape[0], fresh_keys.shape[0])
    admitted = (col_ids <= row_ids) & (col_ids < fresh_len)
    return jnp.where(admitted[None], scores, NEG_FILL)


def self_padded(
    queries, key_rows, value_rows, fresh_keys, fresh_values, old_len, fresh_len, bias_dist
):
    scores = jnp.concatenate(
        [
            cached_scores(queries, key_rows, 0, old_len, bias_dist),
            fresh_scores(queries, fresh_keys, fresh_len, bias_dist),
        ],
        axis=2,
    )
    weights = softmax_rows(scores)
    value_all = jnp.concatenate([value_rows, fresh_values], axis=0)
    return jnp.einsum(
        "hqk,khe->qhe", weights, value_all, preferred_element_type=jnp.float32
    ).astype(jnp.bfloat16)


def self_attend(queries, key_value, cache_dec, slot_old, slot_new, bias_dist, heads_dev):
    req_dev, cache_len = (cache_dec.shape[0], cache_dec.shape[1])
    cache_split = cache_dec.reshape(req_dev, cache_len, heads_dev, 2, -1)

    def one_request(request):
        queries_one, pair_one, cache_one, old_len, fresh_len = request
        return self_padded(
            queries_one,
            cache_one[:, :, 0],
            cache_one[:, :, 1],
            pair_one[:, 0],
            pair_one[:, 1],
            old_len,
            fresh_len,
            bias_dist,
        )

    return lax.map(one_request, (queries, key_value, cache_split, slot_old, slot_new))


def cross_attend(queries, key_value, slot_enc):
    scores = jnp.einsum(
        "rqhe,rkhe->rhqk", queries, key_value[:, :, 0], preferred_element_type=jnp.float32
    )
    col_ids = jnp.arange(key_value.shape[1], dtype=jnp.int32)
    scores = jnp.where(
        col_ids[None, None, None, :] < slot_enc[:, None, None, None], scores, NEG_FILL
    )
    weights = softmax_rows(scores)
    return jnp.einsum(
        "rhqk,rkhe->rqhe", weights, key_value[:, :, 1], preferred_element_type=jnp.float32
    ).astype(jnp.bfloat16)


def add_branch(residual, left, weight, gain):
    residual = residual + row_total(left, weight)
    normed = rms_rows(residual, gain)
    return (residual, normed)


def per_device(
    new_states,
    encoder_out,
    cache_in,
    slot_order,
    new_lengths,
    cache_lengths,
    enc_lengths,
    bucket_of,
    rel_bias,
    norm_gain,
    self_q,
    self_kv,
    self_out,
    cross_q,
    cross_kv,
    cross_out,
    ff_in,
    ff_out,
):
    blk_count = lax.axis_size("blk")
    heads_dev = H // blk_count
    width_dev = heads_dev * HD
    req_dev = cache_in.shape[0] // lax.axis_size("req")
    own_slots = lax.dynamic_slice_in_dim(slot_order, lax.axis_index("req") * req_dev, req_dev, 0)
    slot_new = pick_lengths(new_lengths, own_slots)
    slot_old = pick_lengths(cache_lengths, own_slots)
    slot_enc = pick_lengths(enc_lengths, own_slots)
    ordered = jnp.take(cache_in, slot_order, axis=0)
    cache_dec = lax.all_to_all(
        lax.all_to_all(ordered, "req", split_axis=0, concat_axis=2, tiled=True),
        "blk",
        split_axis=2,
        concat_axis=1,
        tiled=True,
    )
    onehot = (bucket_of[:, None] == jnp.arange(rel_bias.shape[0], dtype=jnp.int32)[None, :]).astype(
        jnp.float32
    )
    own_bias = lax.dynamic_slice_in_dim(rel_bias, lax.axis_index("blk") * heads_dev, heads_dev, 1)
    bias_dist = jnp.dot(onehot, own_bias, precision=lax.Precision.HIGHEST).T
    gathered = (
        lax.all_gather(self_q, "req", axis=0, tiled=True),
        lax.all_gather(self_kv, "req", axis=0, tiled=True),
        lax.all_gather(self_out, "req", axis=1, tiled=True),
        lax.all_gather(cross_q, "req", axis=0, tiled=True),
        lax.all_gather(cross_kv, "req", axis=0, tiled=True),
        lax.all_gather(cross_out, "req", axis=1, tiled=True),
        lax.all_gather(ff_in, "req", axis=0, tiled=True),
        lax.all_gather(ff_out, "req", axis=1, tiled=True),
    )
    wq_self, wkv_self, wo_self, wq_cross, wkv_cross, wo_cross, w_in, w_out = gathered
    states_full = new_states.astype(jnp.float32)
    normed = rms_rows(states_full, norm_gain[0])
    residual = states_full
    self_cat = jnp.concatenate([wq_self, wkv_self.reshape(wkv_self.shape[0], -1)], axis=1)
    projected = (
        jnp.dot(normed, self_cat, preferred_element_type=jnp.float32)
        .astype(jnp.bfloat16)
        .reshape(req_dev, -1, 3, heads_dev, HD)
    )
    context = self_attend(
        projected[:, :, 0], projected[:, :, 1:], cache_dec, slot_old, slot_new, bias_dist, heads_dev
    )
    residual, normed = add_branch(residual, context.reshape(-1, width_dev), wo_self, norm_gain[1])
    queries = (
        jnp.dot(normed, wq_cross, preferred_element_type=jnp.float32)
        .astype(jnp.bfloat16)
        .reshape(req_dev, -1, heads_dev, HD)
    )
    cross_pair = wkv_cross.reshape(wkv_cross.shape[0], -1)
    key_value = (
        jnp.dot(encoder_out, cross_pair, preferred_element_type=jnp.float32)
        .astype(jnp.bfloat16)
        .reshape(req_dev, -1, 2, heads_dev, HD)
    )
    context = cross_attend(queries, key_value, slot_enc)
    residual, normed = add_branch(residual, context.reshape(-1, width_dev), wo_cross, norm_gain[2])
    ff_dev = w_in.shape[2]
    gate_up = jnp.dot(normed, w_in.reshape(w_in.shape[0], -1), preferred_element_type=jnp.float32)
    hidden = (jax.nn.gelu(gate_up[:, :ff_dev], approximate=True) * gate_up[:, ff_dev:]).astype(
        jnp.bfloat16
    )
    layer_out = (residual + row_total(hidden, w_out)).astype(jnp.bfloat16)
    return (layer_out, cache_dec)


def solution(mesh):
    in_specs = (
        P("req", None),
        P("req", None),
        P(None, "blk", "req"),
        P(),
        P(),
        P(),
        P(),
        P(),
        P(),
        P(),
        P("req", "blk"),
        P("req", None, "blk"),
        P("blk", "req"),
        P("req", "blk"),
        P("req", None, "blk"),
        P("blk", "req"),
        P("req", None, "blk"),
        P("blk", "req"),
    )
    out_specs = (P("req", None), P("req", None, "blk"))
    return jax.shard_map(
        per_device, mesh=mesh, in_specs=in_specs, out_specs=out_specs, check_vma=False
    )
```

profile of v0, /device:TPU:33, one launch (start us, length us, event | category | flops | bytes accessed | tf_op | source)
XLA Modules:
  0.0 833.5 jit_solution(8196994682831234726)
XLA Ops:
  9.3 1.1 broadcast_select_fusion
  10.4 5.2 all-to-all-start
  16.2 1.3 select_reduce_fusion.1
  18.3 1.0 convolution_reduce_fusion
  19.3 24.1 %gather_fusion.1 = f32[4608]{0:T(1024)S(1)} fusion(f32[4608]{0:T(1024)S(1)} %convolution_reduce_fusion, s32[5120]{0:T(1024)S(1)} %pad_clamp_fusion), kind=kCustom, calls=%fused_computation.1 | custom fusion | bytes 55296 | tf_op jit(solution)/shard_map/while/body/eval_jaxpr/gather | solution.py:34
  43.4 1.1 broadcast_bitcast_fusion
  44.5 35.9 %copy.40 = f32[1,1,512,4608]{3,1,2,0:T(1,128)} copy(f32[1,1,512,4608]{3,2,1,0:T(8,128)S(1)} %broadcast_bitcast_fusion) | data formatting | bytes 18874368
  80.4 102.3 %slice_reduce_fusion = f32[2358784]{0:T(1024)} fusion(f32[1,2359296]{1,0:T(1,128)} %bitcast.114), kind=kLoop, calls=%fused_computation.10 | loop fusion | bytes 18870272 | tf_op jit(solution)/shard_map/while/body/eval_jaxpr/slice | solution.py:36
  183.4 6.2 gather_fusion.2
  189.8 2.2 copy.41
  192.0 23.1 %slice_reduce_fusion.1 = f32[523776]{0:T(1024)} fusion(f32[1,524288]{1,0:T(1,128)S(1)} %bitcast.120), kind=kLoop, calls=%fused_computation.28 | loop fusion | bytes 4190208 | tf_op jit(solution)/shard_map/while/body/eval_jaxpr/slice | solution.py:36
  215.1 21.1 %all_gather.24 = bf16[1024,64]{0,1:T(8,128)(2,1)} all-gather(bf16[128,64]{0,1:T(8,128)(2,1)S(1)} %copy-done.11), channel_id=1, replica_groups=mesh['req'=8,'blk'=16] {'req'}, dimensions={0}, use_global_device_ids=true | all-gather | bytes 147456 | tf_op jit(solution)/shard_map/all_gather | solution.py:163
  236.2 13.1 %reshape.446 = f32[1,512,4607]{2,1,0:T(8,128)} reshape(f32[2358784]{0:T(1024)} %slice_reduce_fusion) | data formatting | bytes 18870272 | tf_op jit(solution)/shard_map/while/body/eval_jaxpr/reshape | solution.py:37
  249.3 4.4 reshape.448
  253.7 18.0 %all_gather.26 = bf16[64,1024]{1,0:T(8,128)(2,1)S(1)} all-gather(bf16[64,128]{1,0:T(8,128)(2,1)S(1)} %copy-done.12), channel_id=1, replica_groups=mesh['req'=8,'blk'=16] {'req'}, dimensions={1}, use_global_device_ids=true | all-gather | bytes 147456 | tf_op jit(solution)/shard_map/all_gather | solution.py:165
  272.3 20.5 %all_gather.25 = bf16[1024,2,64]{0,2,1:T(8,128)(2,1)} all-gather(bf16[128,2,64]{0,2,1:T(8,128)(2,1)S(1)} %copy-done.10), channel_id=1, replica_groups=mesh['req'=8,'blk'=16] {'req'}, dimensions={0}, use_global_device_ids=true | all-gather | bytes 294912 | tf_op jit(solution)/shard_map/all_gather | solution.py:164
  294.4 13.0 %copy.43 = bf16[1,256,2048]{1,0,2:T(2,128)(2,1)} copy(bf16[1,256,2048]{1,2,0:T(8,128)(2,1)S(1)} %bitcast.122) | data formatting | bytes 2097152 | tf_op jit(solution)/shard_map/all_to_all | solution.py:151
  307.9 11.6 %reduce.23 = bf16[2048,256]{1,0:T(8,128)(2,1)S(1)} reduce(bf16[2048,1,256]{2,1,0:T(2,128)(2,1)} %bitcast.119, bf16[]{:T(256)} %broadcast.285), dimensions={1}, to_apply=%bitcast.113.reduce_sub_computation | reduce | bytes 2097154
  319.5 1.1 reshape.495
  320.7 21.8 %all-to-all-start.1 = ((bf16[16,2,16384]{2,1,0:T(2,128)(2,1)}), bf16[16,2,16384]{2,1,0:T(2,128)(2,1)S(1)}, u32[]{:S(2)}, u32[]{:S(2)}) async-start(bf16[16,2,16384]{2,1,0:T(2,128)(2,1)} %reshape.495), calls=%async_computation.1 | async-start | bytes 2097152 | tf_op jit(solution)/shard_map/all_to_all | solution.py:150
  344.6 15.1 %all-to-all-done.1 = bf16[16,2,16384]{2,1,0:T(2,128)(2,1)S(1)} async-done(((bf16[16,2,16384]{2,1,0:T(2,128)(2,1)}), bf16[16,2,16384]{2,1,0:T(2,128)(2,1)S(1)}, u32[]{:S(2)}, u32[]{:S(2)}) %all-to-all-start.1) | async-done | bytes 1048608 | tf_op jit(solution)/shard_map/all_to_all | solution.py:150
  359.7 3.7 reshape.496
  363.4 1.8 copy.39
  365.2 1.6 copy.35
  366.7 2.3 squeeze.33
  369.1 1.9 slice_bitcast_fusion.2
  370.9 6.1 fusion.72
  377.1 1.7 fusion.3
  378.7 1.6 copy-done.2
  380.3 6.6 convolution_convert_fusion.2
  387.0 19.4 %all_gather.28 = bf16[1024,64]{0,1:T(8,128)(2,1)S(1)} all-gather(bf16[128,64]{0,1:T(8,128)(2,1)S(1)} %copy-done.13), channel_id=1, replica_groups=mesh['req'=8,'blk'=16] {'req'}, dimensions={0}, use_global_device_ids=true | all-gather | bytes 147456 | tf_op jit(solution)/shard_map/all_gather | solution.py:166
  406.4 21.1 %all_gather.29 = bf16[64,1024]{1,0:T(8,128)(2,1)S(1)} all-gather(bf16[64,128]{1,0:T(8,128)(2,1)S(1)} %copy-done.14), channel_id=1, replica_groups=mesh['req'=8,'blk'=16] {'req'}, dimensions={1}, use_global_device_ids=true | all-gather | bytes 147456 | tf_op jit(solution)/shard_map/all_gather | solution.py:168
  427.6 1.9 select_reduce_fusion
  430.1 21.1 %all_gather.27 = bf16[1024,2,64]{0,2,1:T(8,128)(2,1)S(1)} all-gather(bf16[128,2,64]{0,2,1:T(8,128)(2,1)} %param.32), channel_id=1, replica_groups=mesh['req'=8,'blk'=16] {'req'}, dimensions={0}, use_global_device_ids=true | all-gather | bytes 294912 | tf_op jit(solution)/shard_map/all_gather | solution.py:167
  451.2 1.7 convolution_convert_fusion.4
  452.9 73.4 %all-reduce.4.cloned.1.call-done = bf16[512,1024]{1,0:T(8,128)(2,1)} async-done(((bf16[512,1024]{1,0:T(8,128)(2,1)}), bf16[512,1024]{1,0:T(8,128)(2,1)}) %all-reduce.4.cloned.1.call-update) | async-done | bytes 1048592 | tf_op jit(solution)/shard_map/psum | solution.py:43
  526.4 1.7 multiply_reduce_fusion.1
  528.1 2.5 fusion.74
  530.6 1.4 fusion.32
  532.0 2.9 convolution_convert_fusion.1
  535.0 20.5 %all_gather.31 = bf16[176,1024]{1,0:T(8,128)(2,1)S(1)} all-gather(bf16[176,128]{1,0:T(8,128)(2,1)} %param.35), channel_id=1, replica_groups=mesh['req'=8,'blk'=16] {'req'}, dimensions={1}, use_global_device_ids=true | all-gather | bytes 405504 | tf_op jit(solution)/shard_map/all_gather | solution.py:170
  555.5 24.7 %all_gather.30 = bf16[1024,2,176]{0,2,1:T(8,128)(2,1)} all-gather(bf16[128,2,176]{0,2,1:T(8,128)(2,1)} %param.34), channel_id=1, replica_groups=mesh['req'=8,'blk'=16] {'req'}, dimensions={0}, use_global_device_ids=true | all-gather | bytes 811008 | tf_op jit(solution)/shard_map/all_gather | solution.py:169
  580.2 96.8 %all-reduce.6.cloned.1.call-done = bf16[512,1024]{1,0:T(8,128)(2,1)} async-done(((bf16[512,1024]{1,0:T(8,128)(2,1)}), bf16[512,1024]{1,0:T(8,128)(2,1)}) %all-reduce.6.cloned.1.call-update) | async-done | bytes 1048592 | tf_op jit(solution)/shard_map/psum | solution.py:43
  677.0 1.9 multiply_reduce_fusion
  679.8 1.5 convolution_convert_fusion
  681.3 1.3 copy.37
  682.6 140.1 %all-reduce.8.cloned.1.call-done = bf16[512,1024]{1,0:T(8,128)(2,1)} async-done(((bf16[512,1024]{1,0:T(8,128)(2,1)}), bf16[512,1024]{1,0:T(8,128)(2,1)}) %all-reduce.8.cloned.1.call-update) | async-done | bytes 1048592 | tf_op jit(solution)/shard_map/psum | solution.py:43
  822.8 3.7 add_convert_fusion
  (74 shorter events, 10.1 us)
Async XLA Ops:
  7.2 1.4 copy-start
  9.2 6.4 copy-start.20
  9.2 7.0 copy-start.17
  9.3 7.0 copy-start.18
  9.3 9.0 %copy-start.19 = (s32[4608]{0:T(1024)S(1)}, s32[4608]{0:T(1024)}, u32[]{:S(2)}) copy-start(s32[4608]{0:T(1024)} %param.25) | copy-start | bytes 55300
  10.4 283.3 %all-to-all-start = ((bf16[8,256,256]{2,1,0:T(8,128)(2,1)}), bf16[8,256,256]{2,1,0:T(8,128)(2,1)S(1)}, u32[]{:S(2)}, u32[]{:S(2)}) async-start(bf16[8,256,256]{2,1,0:T(8,128)(2,1)} %broadcast_select_fusion), calls=%async_computation | async-start | bytes 2097152 | tf_op jit(solution)/shard_map/all_to_all | solution.py:151
  192.0 23.1 %copy-start.11 = (bf16[128,64]{0,1:T(8,128)(2,1)S(1)}, bf16[128,64]{0,1:T(8,128)(2,1)}, u32[]{:S(2)}) copy-start(bf16[128,64]{0,1:T(8,128)(2,1)} %param.28) | copy-start | bytes 49156
  249.3 4.4 copy-start.12
  249.3 23.0 %copy-start.10 = (bf16[128,2,64]{0,2,1:T(8,128)(2,1)S(1)}, bf16[128,2,64]{0,2,1:T(8,128)(2,1)}, u32[]{:S(2)}) copy-start(bf16[128,2,64]{0,2,1:T(8,128)(2,1)} %param.29) | copy-start | bytes 98308
  249.3 43.5 %copy-start.3 = (bf16[512,1024]{1,0:T(8,128)(2,1)S(1)}, bf16[512,1024]{1,0:T(8,128)(2,1)}, u32[]{:S(2)}) copy-start(bf16[512,1024]{1,0:T(8,128)(2,1)} %param.18) | copy-start | bytes 3145732
  249.3 43.8 %copy-start.15 = (f32[3,1024]{1,0:T(4,128)S(1)}, f32[3,1024]{1,0:T(4,128)}, u32[]{:S(2)}) copy-start(f32[3,1024]{1,0:T(4,128)} %param.27) | copy-start | bytes 36868
  320.7 21.9 %copy-start.8 = (bf16[1024,2,64]{0,2,1:T(8,128)(2,1)S(1)}, bf16[1024,2,64]{0,2,1:T(8,128)(2,1)}, u32[]{:S(2)}) copy-start(bf16[1024,2,64]{0,2,1:T(8,128)(2,1)} %all_gather.25) | copy-start | bytes 786436
  320.7 21.9 %copy-start.9 = (bf16[1024,64]{0,1:T(8,128)(2,1)S(1)}, bf16[1024,64]{0,1:T(8,128)(2,1)}, u32[]{:S(2)}) copy-start(bf16[1024,64]{0,1:T(8,128)(2,1)} %all_gather.24) | copy-start | bytes 393220
  320.7 39.1 %all-to-all-start.1 = ((bf16[16,2,16384]{2,1,0:T(2,128)(2,1)}), bf16[16,2,16384]{2,1,0:T(2,128)(2,1)S(1)}, u32[]{:S(2)}, u32[]{:S(2)}) async-start(bf16[16,2,16384]{2,1,0:T(2,128)(2,1)} %reshape.495), calls=%async_computation.1 | async-start | bytes 2097152 | tf_op jit(solution)/shard_map/all_to_all | solution.py:150
  342.5 183.9 %all-reduce.4.cloned.1.call-start = ((), (), s32[]{:S(2)}) async-start(), calls=%async_computation.2 | async-start | bytes 2097152 | tf_op jit(solution)/shard_map/psum | solution.py:43
  342.5 1.6 copy-start.5
  377.1 3.2 copy-start.2
  380.3 6.7 copy-start.13
  380.3 26.1 %copy-start.14 = (bf16[64,128]{1,0:T(8,128)(2,1)S(1)}, bf16[64,128]{1,0:T(8,128)(2,1)}, u32[]{:S(2)}) copy-start(bf16[64,128]{1,0:T(8,128)(2,1)} %param.33) | copy-start | bytes 49156
  386.9 290.1 %all-reduce.6.cloned.1.call-start = ((), (), s32[]{:S(2)}) async-start(), calls=%async_computation.3 | async-start | bytes 2097152 | tf_op jit(solution)/shard_map/psum | solution.py:43
  526.4 1.7 copy-start.4
  535.0 144.0 %copy-start.16 = (f32[1,1024]{1,0:T(1,128)S(1)}, f32[1,1024]{1,0:T(1,128)}, u32[]{:S(2)}) copy-start(f32[1,1024]{1,0:T(1,128)} %get-tuple-element.20) | copy-start | bytes 12292
  535.0 287.8 %all-reduce.8.cloned.1.call-start = ((), (), s32[]{:S(2)}) async-start(), calls=%async_computation.4 | async-start | bytes 2097152 | tf_op jit(solution)/shard_map/psum | solution.py:43
  677.0 1.9 copy-start.6
  677.0 1.9 copy-start.7
  681.3 145.2 %copy-start.1 = (bf16[8,256,256]{2,1,0:T(8,128)(2,1)S(1)}, bf16[8,256,256]{2,1,0:T(8,128)(2,1)}, u32[]{:S(2)}) copy-start(bf16[8,256,256]{2,1,0:T(8,128)(2,1)} %param.20) | copy-start | bytes 3145732
Sparse Core Ops, SparseCore 0:
  387.1 139.2 all-reduce.3
  535.1 141.8 all-reduce.5
  681.4 141.2 all-reduce.7
where the time goes:
time: 845 us; the launch traced here: 833 us
  waiting for transfers between devices  326 us (39%)
  local copies, waits for them, and re-layouts  245 us (29%)
  blocking collectives  166 us (20%)
  other arithmetic  30.2 us (4%)
  starting transfers between devices  27.2 us (3%)
  matrix products  24.1 us (3%)
  between operations  15.2 us (2%)
    psum x3, waiting for transfers between devices, row_total(): return lax.psum(term.astype(jnp.bfloat16), 'blk').astype(jnp.float32)  310 us
    slice x2, local copies, waits for them, and re-layouts, shifted_bias(): tiled.reshape(heads_here, row_count * (line_len + 1))  125 us
    unnamed x50, local copies, waits for them, and re-layouts  49.1 us
    gather x2, local copies, waits for them, and re-layouts, shifted_bias(): line = bias_dist[:, jnp.clip(base + row_count - 1 - steps, 0, span_len - 1)]  30.2 us
    all_gather x1, blocking collectives, per_device(): lax.all_gather(ff_in, 'req', axis=0, tiled=True)  24.7 us
    all_to_all x1, starting transfers between devices, per_device(): lax.all_to_all(lax.all_to_all(ordered, 'req', split_axis=0, concat_axis=2...  21.8 us
    all_gather x1, blocking collectives, per_device(): lax.all_gather(cross_out, 'req', axis=1, tiled=True)  21.1 us
    all_gather x1, blocking collectives, per_device(): lax.all_gather(cross_kv, 'req', axis=0, tiled=True)  21.1 us
  transfers between devices with their start and end apart: 5, of which 4 were waited for; matrix products, arithmetic and copies ran while one was open for 27% of the time, Pallas kernels for 0%

commit v1 on v0

--- a/solution.py
+++ b/solution.py
@@ -2,6 +2,8 @@
 import jax.numpy as jnp
 from jax import lax
 from jax.sharding import PartitionSpec as P
+from jax.experimental import pallas as pl
+from jax.experimental.pallas import tpu as pltpu
 
 H = 16
 HD = 64
@@ -116,6 +118,89 @@
     residual = residual + row_total(left, weight)
     normed = rms_rows(residual, gain)
     return (residual, normed)
+
+
+TQ = 128
+
+
+def self_kernel(lens_ref, q_ref, c_ref, kn_ref, vn_ref, g_ref, f_ref, o_ref):
+    old_len = lens_ref[0]
+    fresh_len = lens_ref[1]
+    n_q = q_ref.shape[0]
+    n_ctx = c_ref.shape[0]
+    wide_old = n_ctx + TQ
+    wide_new = n_q + TQ
+    k_old = c_ref[:, :HD]
+    v_old = c_ref[:, HD:]
+    k_new = kn_ref[...]
+    v_new = vn_ref[...]
+    dims = (((1,), (1,)), ((), ()))
+    for t in range(n_q // TQ):
+        q = q_ref[t * TQ : (t + 1) * TQ, :]
+        start = n_q - TQ - t * TQ
+        s_old = lax.dot_general(q, k_old, dims, preferred_element_type=jnp.float32)
+        line = jnp.broadcast_to(g_ref[:, start : start + wide_old], (TQ, wide_old))
+        bias = pltpu.roll(line, wide_old - (TQ - 1), 1, stride=1, stride_axis=0)[:, :n_ctx]
+        col = lax.broadcasted_iota(jnp.int32, (TQ, n_ctx), 1)
+        s_old = jnp.where(col < old_len, s_old + bias, NEG_FILL)
+        s_new = lax.dot_general(q, k_new, dims, preferred_element_type=jnp.float32)
+        line = jnp.broadcast_to(f_ref[:, start : start + wide_new], (TQ, wide_new))
+        bias = pltpu.roll(line, wide_new - (TQ - 1), 1, stride=1, stride_axis=0)[:, :n_q]
+        row = lax.broadcasted_iota(jnp.int32, (TQ, n_q), 0) + t * TQ
+        col = lax.broadcasted_iota(jnp.int32, (TQ, n_q), 1)
+        s_new = jnp.where((col <= row) & (col < fresh_len), s_new + bias, NEG_FILL)
+        top = jnp.maximum(
+            jnp.max(s_old, axis=1, keepdims=True), jnp.max(s_new, axis=1, keepdims=True)
+        )
+        p_old = jnp.exp(s_old - top)
+        p_new = jnp.exp(s_new - top)
+        total = jnp.sum(p_old, axis=1, keepdims=True) + jnp.sum(p_new, axis=1, keepdims=True)
+        w_old = (p_old / total).astype(jnp.bfloat16)
+        w_new = (p_new / total).astype(jnp.bfloat16)
+        out = jnp.dot(w_old, v_old, preferred_element_type=jnp.float32) + jnp.dot(
+            w_new, v_new, preferred_element_type=jnp.float32
+        )
+        o_ref[t * TQ : (t + 1) * TQ, :] = out.astype(jnp.bfloat16)
+
+
+def bias_lines(line, old_len, n_q, n_ctx):
+    span = line.shape[0]
+    ext = jnp.concatenate([jnp.broadcast_to(line[:1], (n_ctx,)), line])
+    rev = ext[::-1]
+    g = lax.dynamic_slice_in_dim(rev, n_ctx - old_len, span)
+    f = rev[n_ctx : n_ctx + 2 * n_q]
+    return g[None, :], f[None, :]
+
+
+def self_attention(q, cache_blk, k_new, v_new, line, old_len, fresh_len):
+    n_q = q.shape[0]
+    n_ctx = cache_blk.shape[0]
+    g, f = bias_lines(line, old_len, n_q, n_ctx)
+    lens = jnp.stack([old_len, fresh_len]).astype(jnp.int32)
+    vmem = pl.BlockSpec(memory_space=pltpu.VMEM)
+    return pl.pallas_call(
+        self_kernel,
+        out_shape=jax.ShapeDtypeStruct((n_q, HD), jnp.bfloat16),
+        in_specs=[pl.BlockSpec(memory_space=pltpu.SMEM)] + [vmem] * 6,
+        out_specs=vmem,
+        compiler_params=pltpu.CompilerParams(vmem_limit_bytes=48 * 1024 * 1024),
+    )(lens, q, cache_blk, k_new, v_new, g, f)
+
+
+def pack_gather(pieces):
+    flat = jnp.concatenate([w.reshape(-1) for w, _ in pieces])
+    whole = lax.all_gather(flat, "req", axis=0, tiled=False)
+    n_req = whole.shape[0]
+    out, at = [], 0
+    for w, axis in pieces:
+        size = w.size
+        part = whole[:, at : at + size].reshape((n_req,) + w.shape)
+        at += size
+        part = jnp.moveaxis(part, 0, axis)
+        shape = list(w.shape)
+        shape[axis] *= n_req
+        out.append(part.reshape(shape))
+    return out
 
 
 def per_device(
@@ -159,28 +244,34 @@
     )
     own_bias = lax.dynamic_slice_in_dim(rel_bias, lax.axis_index("blk") * heads_dev, heads_dev, 1)
     bias_dist = jnp.dot(onehot, own_bias, precision=lax.Precision.HIGHEST).T
-    gathered = (
-        lax.all_gather(self_q, "req", axis=0, tiled=True),
-        lax.all_gather(self_kv, "req", axis=0, tiled=True),
-        lax.all_gather(self_out, "req", axis=1, tiled=True),
-        lax.all_gather(cross_q, "req", axis=0, tiled=True),
-        lax.all_gather(cross_kv, "req", axis=0, tiled=True),
-        lax.all_gather(cross_out, "req", axis=1, tiled=True),
-        lax.all_gather(ff_in, "req", axis=0, tiled=True),
-        lax.all_gather(ff_out, "req", axis=1, tiled=True),
+    gathered = pack_gather(
+        [
+            (self_q, 0),
+            (self_kv, 0),
+            (self_out, 1),
+            (cross_q, 0),
+            (cross_kv, 0),
+            (cross_out, 1),
+            (ff_in, 0),
+            (ff_out, 1),
+        ]
     )
     wq_self, wkv_self, wo_self, wq_cross, wkv_cross, wo_cross, w_in, w_out = gathered
     states_full = new_states.astype(jnp.float32)
     normed = rms_rows(states_full, norm_gain[0])
     residual = states_full
     self_cat = jnp.concatenate([wq_self, wkv_self.reshape(wkv_self.shape[0], -1)], axis=1)
-    projected = (
-        jnp.dot(normed, self_cat, preferred_element_type=jnp.float32)
-        .astype(jnp.bfloat16)
-        .reshape(req_dev, -1, 3, heads_dev, HD)
-    )
-    context = self_attend(
-        projected[:, :, 0], projected[:, :, 1:], cache_dec, slot_old, slot_new, bias_dist, heads_dev
+    projected = jnp.dot(normed, self_cat, preferred_element_type=jnp.float32).astype(
+        jnp.bfloat16
+    )
+    context = self_attention(
+        projected[:, :HD],
+        cache_dec[0],
+        projected[:, HD : 2 * HD],
+        projected[:, 2 * HD :],
+        bias_dist[0],
+        slot_old[0],
+        slot_new[0],
     )
     residual, normed = add_branch(residual, context.reshape(-1, width_dev), wo_self, norm_gain[1])
     queries = (

time: 845 us -> 574 us (0.68)
  local copies, waits for them, and re-layouts: 245 us -> 53.8 us
  blocking collectives: 166 us -> 0 us
  waiting for transfers between devices: 326 us -> 439 us
  starting transfers between devices: 27.2 us -> 14.4 us
  matrix products: 24.1 us -> 14.2 us
    all_gather x8 -> x0, blocking collectives: 166 us -> none  [the longest x1 24.7 us: per_device(): lax.all_gather(ff_in, 'req', axis=0, tiled=True)]
    slice x2 -> x9, local copies, waits for them, and re-layouts: 125 us -> 7.11 us  [the longest x5 5.78 us: pack_gather(): part = whole[:, at:at + size].reshape((n_req,) + w.shape)]
    psum x3, waiting for transfers between devices: 310 us -> 412 us  [row_total(): return lax.psum(term.astype(jnp.bfloat16), 'blk').astype(jnp.float32)]
    unnamed x50, local copies, waits for them, and re-layouts: 49.1 us -> 14.5 us
    gather x2 -> x0, local copies, waits for them, and re-layouts: 30.2 us -> none  [shifted_bias(): line = bias_dist[:, jnp.clip(base + row_count - 1 - steps, 0, span_len - 1)]]
    all_to_all x1, waiting for transfers between devices: 0.01 us -> 16.9 us  [per_device(): lax.all_to_all(ordered, 'req', split_axis=0, concat_axis=2, tiled=True)]
    reshape x2 -> x5, local copies, waits for them, and re-layouts: 17.5 us -> 0.6 us  [pack_gather(): flat = jnp.concatenate([w.reshape(-1) for w, _ in pieces])]
    all_to_all x1, starting transfers between devices: 21.8 us -> 8.65 us  [per_device(): lax.all_to_all(lax.all_to_all(ordered, 'req', split_axis=0, concat_axis=2...]
  transfers between devices with their start and end apart: 5 -> 6, of which waited for: 4 -> 5; matrix products, arithmetic and copies ran while one was open for 27% -> 10% of each run, Pallas kernels for 0% -> 0%
where the time goes in v1:
time: 574 us; the launch traced here: 571 us
  waiting for transfers between devices  439 us (76%)
  local copies, waits for them, and re-layouts  53.8 us (9%)
  other arithmetic  27.2 us (5%)
  between operations  15.4 us (3%)
  starting transfers between devices  14.4 us (3%)
  matrix products  14.2 us (2%)
  Pallas kernels  6.86 us (1%)
    psum x3, waiting for transfers between devices, row_total(): return lax.psum(term.astype(jnp.bfloat16), 'blk').astype(jnp.float32)  412 us
    all_to_all x1, waiting for transfers between devices, per_device(): lax.all_to_all(ordered, 'req', split_axis=0, concat_axis=2, tiled=True)  16.9 us
    unnamed x50, local copies, waits for them, and re-layouts  14.5 us
    all_to_all x2, local copies, waits for them, and re-layouts, per_device(): lax.all_to_all(ordered, 'req', split_axis=0, concat_axis=2, tiled=True)  13.4 us
    unnamed x1, other arithmetic  11.6 us
  transfers between devices with their start and end apart: 6, of which 5 were waited for; matrix products, arithmetic and copies ran while one was open for 10% of the time, Pallas kernels for 0%

profile of v1, /device:TPU:33, one launch (start us, length us, event | category | flops | bytes accessed | tf_op | source)
XLA Modules:
  0.0 570.8 jit_solution(13214549237436559292)
XLA Ops:
  7.2 0.9 copy.47
  8.2 0.8 copy.49
  9.2 0.9 copy.48
  10.2 0.9 copy.50
  11.1 1.0 copy.51
  12.4 0.7 bitcast_dynamic-update-slice_fusion.2
  13.1 0.7 bitcast_dynamic-update-slice_fusion.1
  13.9 0.8 bitcast_dynamic-update-slice_fusion
  16.7 1.1 broadcast_select_fusion
  17.8 5.2 all-to-all-start
  23.6 16.9 %all-to-all-done = bf16[8,256,256]{2,1,0:T(8,128)(2,1)S(1)} async-done(((bf16[8,256,256]{2,1,0:T(8,128)(2,1)}), bf16[8,256,256]{2,1,0:T(8,128)(2,1)S(1)}, u32[]{:S(2)}, u32[]{:S(2)}) %all-to-all-start) | async-done | bytes 1048608 | tf_op jit(solution)/shard_map/all_to_all | solution.py:236
  41.1 12.9 %copy.75 = bf16[1,256,2048]{1,0,2:T(2,128)(2,1)} copy(bf16[1,256,2048]{1,2,0:T(8,128)(2,1)S(1)} %bitcast.80) | data formatting | bytes 2097152 | tf_op jit(solution)/shard_map/all_to_all | solution.py:236
  54.5 11.6 %reduce.12 = bf16[2048,256]{1,0:T(8,128)(2,1)S(1)} reduce(bf16[2048,1,256]{2,1,0:T(2,128)(2,1)} %bitcast.79, bf16[]{:T(256)} %broadcast.87), dimensions={1}, to_apply=%bitcast.73.reduce_sub_computation | reduce | bytes 2097154
  66.2 1.1 reshape.175
  67.3 8.6 %all-to-all-start.1 = ((bf16[16,2,16384]{2,1,0:T(2,128)(2,1)}), bf16[16,2,16384]{2,1,0:T(2,128)(2,1)S(1)}, u32[]{:S(2)}, u32[]{:S(2)}) async-start(bf16[16,2,16384]{2,1,0:T(2,128)(2,1)} %reshape.175), calls=%async_computation.1 | async-start | bytes 2097152 | tf_op jit(solution)/shard_map/all_to_all | solution.py:235
  76.2 1.3 select_reduce_fusion.1
  78.8 1.0 convolution_reduce_fusion
  81.8 1.3 pad_add_fusion.lens_ref
  83.5 9.7 %all-to-all-done.1 = bf16[16,2,16384]{2,1,0:T(2,128)(2,1)S(1)} async-done(((bf16[16,2,16384]{2,1,0:T(2,128)(2,1)}), bf16[16,2,16384]{2,1,0:T(2,128)(2,1)S(1)}, u32[]{:S(2)}, u32[]{:S(2)}) %all-to-all-start.1) | async-done | bytes 1048608 | tf_op jit(solution)/shard_map/all_to_all | solution.py:235
  93.2 3.4 reshape.176
  96.6 2.7 copy.58
  99.3 1.6 copy.55
  101.0 4.2 reshape.170
  105.2 1.9 fusion.50
  107.1 1.8 fusion.51
  108.9 1.9 reshape_reshape.6
  110.8 1.8 reshape_reshape_reshape.9
  112.5 1.7 convolution_convert_fusion.3
  114.4 6.9 %shard_map.185 = bf16[512,64]{1,0:T(8,128)(2,1)S(1)} custom-call(s32[2]{0:T(128)S(1)} %pad_add_fusion.lens_ref, bf16[512,64]{1,0:T(8,128)(2,1)S(1)} %get-tuple-element.10.q_ref, bf16[4096,128]{1,0:T(8,128)(2,1)S(1)} %bitcast.74, bf16[512,64]{1,0:T(8,128)(2,1)S(1)} %get-tuple-element.9.kn_ref, bf16[512,64]{1,0:T(8,128)(2,1)S(1)} %get-tuple-element.8.vn_ref, ...), custom_call_target="tpu_custom_call" | custom-call | tf_op jit(solution)/shard_map/pallas_call | solution.py:181
  121.2 1.4 convolution_convert_fusion.2
  122.9 1.3 select_reduce_fusion
  124.2 1.1 iota_compare_fusion.2
  125.3 1.9 reshape_reshape.7
  127.2 0.8 reshape_reshape_reshape.10
  128.1 2.1 convolution_convert_fusion.4
  130.2 134.6 %all-reduce.5.cloned.1.call-done = bf16[512,1024]{1,0:T(8,128)(2,1)} async-done(((bf16[512,1024]{1,0:T(8,128)(2,1)}), bf16[512,1024]{1,0:T(8,128)(2,1)}) %all-reduce.5.cloned.1.call-update) | async-done | bytes 1048592 | tf_op jit(solution)/shard_map/psum | solution.py:45
  264.8 1.7 multiply_reduce_fusion.1
  266.6 2.7 fusion.54
  269.3 1.4 fusion.14
  270.7 3.0 convolution_convert_fusion.1
  273.7 2.0 slice.99
  275.8 3.2 reshape_reshape_reshape.11
  278.9 136.1 %all-reduce.7.cloned.1.call-done = bf16[512,1024]{1,0:T(8,128)(2,1)} async-done(((bf16[512,1024]{1,0:T(8,128)(2,1)}), bf16[512,1024]{1,0:T(8,128)(2,1)}) %all-reduce.7.cloned.1.call-update) | async-done | bytes 1048592 | tf_op jit(solution)/shard_map/psum | solution.py:45
  415.0 1.9 multiply_reduce_fusion
  417.0 0.9 fusion.4
  418.0 1.5 convolution_convert_fusion
  419.5 141.4 %all-reduce.9.cloned.1.call-done = bf16[512,1024]{1,0:T(8,128)(2,1)} async-done(((bf16[512,1024]{1,0:T(8,128)(2,1)}), bf16[512,1024]{1,0:T(8,128)(2,1)}) %all-reduce.9.cloned.1.call-update) | async-done | bytes 1048592 | tf_op jit(solution)/shard_map/psum | solution.py:45
  560.9 3.4 add_convert_fusion
  (75 shorter events, 7.5 us)
Async XLA Ops:
  7.2 8.9 %copy-start = (bf16[8,256,256]{2,1,0:T(8,128)(2,1)S(1)}, bf16[8,256,256]{2,1,0:T(8,128)(2,1)}, u32[]{:S(2)}) copy-start(bf16[8,256,256]{2,1,0:T(8,128)(2,1)} %param.20) | copy-start | bytes 3145732
  7.2 9.5 %copy-start.15 = (s32[8]{0:T(128)S(1)}, s32[8]{0:T(128)}, u32[]{:S(2)}) copy-start(s32[8]{0:T(128)} %param.21) | copy-start | bytes 100
  7.2 93.8 %all-gather.3.cloned.1.call-start = ((), (), s32[]{:S(2)}) async-start(), calls=%async_computation.5 | async-start | bytes 2396160 | tf_op jit(solution)/shard_map/all_gather | solution.py:192
  14.7 0.7 copy-start.8
  17.8 22.7 %all-to-all-start = ((bf16[8,256,256]{2,1,0:T(8,128)(2,1)}), bf16[8,256,256]{2,1,0:T(8,128)(2,1)S(1)}, u32[]{:S(2)}, u32[]{:S(2)}) async-start(bf16[8,256,256]{2,1,0:T(8,128)(2,1)} %broadcast_select_fusion), calls=%async_computation | async-start | bytes 2097152 | tf_op jit(solution)/shard_map/all_to_all | solution.py:236
  66.2 10.0 %copy-start.12 = (s32[8]{0:T(128)S(1)}, s32[8]{0:T(128)}, u32[]{:S(2)}) copy-start(s32[8]{0:T(128)} %param.22) | copy-start | bytes 100
  66.2 10.0 %copy-start.13 = (s32[8]{0:T(128)S(1)}, s32[8]{0:T(128)}, u32[]{:S(2)}) copy-start(s32[8]{0:T(128)} %param.23) | copy-start | bytes 100
  66.2 12.6 %copy-start.14 = (s32[4608]{0:T(1024)S(1)}, s32[4608]{0:T(1024)}, u32[]{:S(2)}) copy-start(s32[4608]{0:T(1024)} %param.25) | copy-start | bytes 55300
  66.2 16.9 %copy-start.2 = (bf16[512,1024]{1,0:T(8,128)(2,1)S(1)}, bf16[512,1024]{1,0:T(8,128)(2,1)}, u32[]{:S(2)}) copy-start(bf16[512,1024]{1,0:T(8,128)(2,1)} %param.18) | copy-start | bytes 3145732
  67.3 16.1 %copy-start.11 = (f32[3,1024]{1,0:T(4,128)S(1)}, f32[3,1024]{1,0:T(4,128)}, u32[]{:S(2)}) copy-start(f32[3,1024]{1,0:T(4,128)} %param.27) | copy-start | bytes 36868
  67.3 25.9 %all-to-all-start.1 = ((bf16[16,2,16384]{2,1,0:T(2,128)(2,1)}), bf16[16,2,16384]{2,1,0:T(2,128)(2,1)S(1)}, u32[]{:S(2)}, u32[]{:S(2)}) async-start(bf16[16,2,16384]{2,1,0:T(2,128)(2,1)} %reshape.175), calls=%async_computation.1 | async-start | bytes 2097152 | tf_op jit(solution)/shard_map/all_to_all | solution.py:235
  76.0 188.8 %all-reduce.5.cloned.1.call-start = ((), (), s32[]{:S(2)}) async-start(), calls=%async_computation.2 | async-start | bytes 2097152 | tf_op jit(solution)/shard_map/psum | solution.py:45
  101.0 13.4 %copy-start.1 = (bf16[1,16,256,128]{3,2,1,0:T(8,128)(2,1)}, bf16[1,16,256,128]{3,2,1,0:T(8,128)(2,1)S(1)}, u32[]{:S(2)}) copy-start(bf16[1,16,256,128]{3,2,1,0:T(8,128)(2,1)S(1)} %copy.55) | copy-start | bytes 3145732
  112.5 8.7 %copy-start.7 = (bf16[8,8192]{1,0:T(8,128)(2,1)S(1)}, bf16[8,8192]{1,0:T(8,128)(2,1)}, u32[]{:S(2)}) copy-start(bf16[8,8192]{1,0:T(8,128)(2,1)} %get-tuple-element.4) | copy-start | bytes 393220
  114.3 8.6 %copy-start.16 = (s32[8]{0:T(128)S(1)}, s32[8]{0:T(128)}, u32[]{:S(2)}) copy-start(s32[8]{0:T(128)} %param.24) | copy-start | bytes 100
  121.2 6.8 %copy-start.5 = (bf16[512,1024]{1,0:T(8,128)(2,1)S(1)}, bf16[512,1024]{1,0:T(8,128)(2,1)}, u32[]{:S(2)}) copy-start(bf16[512,1024]{1,0:T(8,128)(2,1)} %param.19) | copy-start | bytes 3145732
  122.7 292.4 %all-reduce.7.cloned.1.call-start = ((), (), s32[]{:S(2)}) async-start(), calls=%async_computation.3 | async-start | bytes 2097152 | tf_op jit(solution)/shard_map/psum | solution.py:45
  128.1 138.5 %copy-start.9 = (bf16[1024,64]{1,0:T(8,128)(2,1)S(1)}, bf16[1024,64]{1,0:T(8,128)(2,1)}, u32[]{:S(2)}) copy-start(bf16[1024,64]{1,0:T(8,128)(2,1)} %reshape_reshape.7) | copy-start | bytes 393220
  264.8 1.7 copy-start.3
  266.6 4.1 copy-start.10
  273.7 287.2 %all-reduce.9.cloned.1.call-start = ((), (), s32[]{:S(2)}) async-start(), calls=%async_computation.4 | async-start | bytes 2097152 | tf_op jit(solution)/shard_map/psum | solution.py:45
  415.0 1.9 copy-start.4
  415.0 1.9 copy-start.6
  417.0 1.0 slice-start
Sparse Core Ops, SparseCore 0:
  15.5 61.2 all-gather.2
  122.8 141.9 all-reduce.4
  273.8 141.1 all-reduce.6
  419.6 141.2 all-reduce.8

commit v2 on v1

--- a/solution.py
+++ b/solution.py
@@ -1,3 +1,5 @@
+import functools
+
 import jax
 import jax.numpy as jnp
 from jax import lax
@@ -201,6 +203,124 @@
         shape[axis] *= n_req
         out.append(part.reshape(shape))
     return out
+
+
+MESH_IDS = pl.DeviceIdType.MESH
+
+
+def greet_all(n_blk, me, req):
+    barrier = pltpu.get_barrier_semaphore()
+    for k in range(1, n_blk):
+        peer = lax.rem(me + k, n_blk)
+        pl.semaphore_signal(barrier, inc=1, device_id=(req, peer), device_id_type=MESH_IDS)
+    pl.semaphore_wait(barrier, n_blk - 1)
+
+
+def scatter_kernel(n_blk, part_ref, out_ref, recv, send_sem, recv_sem):
+    me = lax.axis_index("blk")
+    req = lax.axis_index("req")
+    rows = out_ref.shape[0]
+    greet_all(n_blk, me, req)
+    copies = []
+    for k in range(1, n_blk):
+        peer = lax.rem(me + k, n_blk)
+        copy = pltpu.make_async_remote_copy(
+            src_ref=part_ref.at[pl.ds(pl.multiple_of(peer * rows, rows), rows)],
+            dst_ref=recv.at[me],
+            send_sem=send_sem.at[peer],
+            recv_sem=recv_sem.at[me],
+            device_id=(req, peer),
+            device_id_type=MESH_IDS,
+        )
+        copy.start()
+        copies.append(copy)
+    total = part_ref[pl.ds(pl.multiple_of(me * rows, rows), rows), :].astype(jnp.float32)
+    for k in range(1, n_blk):
+        src = lax.rem(me + n_blk - k, n_blk)
+        incoming = pltpu.make_async_remote_copy(
+            src_ref=part_ref.at[pl.ds(0, rows)],
+            dst_ref=recv.at[src],
+            send_sem=send_sem.at[src],
+            recv_sem=recv_sem.at[src],
+            device_id=(req, src),
+            device_id_type=MESH_IDS,
+        )
+        incoming.wait_recv()
+        total = total + recv[src].astype(jnp.float32)
+    for copy in copies:
+        copy.wait_send()
+    out_ref[...] = total
+
+
+def gather_kernel(n_blk, piece_ref, out_ref, recv, send_sem, recv_sem):
+    me = lax.axis_index("blk")
+    req = lax.axis_index("req")
+    rows = piece_ref.shape[0]
+    greet_all(n_blk, me, req)
+    copies = []
+    for k in range(1, n_blk):
+        peer = lax.rem(me + k, n_blk)
+        copy = pltpu.make_async_remote_copy(
+            src_ref=piece_ref,
+            dst_ref=recv.at[me],
+            send_sem=send_sem.at[peer],
+            recv_sem=recv_sem.at[me],
+            device_id=(req, peer),
+            device_id_type=MESH_IDS,
+        )
+        copy.start()
+        copies.append(copy)
+    out_ref[pl.ds(pl.multiple_of(me * rows, rows), rows), :] = piece_ref[...]
+    for k in range(1, n_blk):
+        src = lax.rem(me + n_blk - k, n_blk)
+        incoming = pltpu.make_async_remote_copy(
+            src_ref=piece_ref,
+            dst_ref=recv.at[src],
+            send_sem=send_sem.at[src],
+            recv_sem=recv_sem.at[src],
+            device_id=(req, src),
+            device_id_type=MESH_IDS,
+        )
+        incoming.wait_recv()
+        out_ref[pl.ds(pl.multiple_of(src * rows, rows), rows), :] = recv[src]
+    for copy in copies:
+        copy.wait_send()
+
+
+def blk_scatter(part):
+    n_blk = lax.axis_size("blk")
+    rows = part.shape[0] // n_blk
+    vmem = pl.BlockSpec(memory_space=pltpu.VMEM)
+    return pl.pallas_call(
+        functools.partial(scatter_kernel, n_blk),
+        out_shape=jax.ShapeDtypeStruct((rows, part.shape[1]), jnp.float32),
+        in_specs=[vmem],
+        out_specs=vmem,
+        scratch_shapes=[
+            pltpu.VMEM((n_blk, rows, part.shape[1]), part.dtype),
+            pltpu.SemaphoreType.DMA((n_blk,)),
+            pltpu.SemaphoreType.DMA((n_blk,)),
+        ],
+        compiler_params=pltpu.CompilerParams(collective_id=1, has_side_effects=True),
+    )(part)
+
+
+def blk_gather(piece):
+    n_blk = lax.axis_size("blk")
+    rows = piece.shape[0]
+    vmem = pl.BlockSpec(memory_space=pltpu.VMEM)
+    return pl.pallas_call(
+        functools.partial(gather_kernel, n_blk),
+        out_shape=jax.ShapeDtypeStruct((rows * n_blk, piece.shape[1]), piece.dtype),
+        in_specs=[vmem],
+        out_specs=vmem,
+        scratch_shapes=[
+            pltpu.VMEM((n_blk, rows, piece.shape[1]), piece.dtype),
+            pltpu.SemaphoreType.DMA((n_blk,)),
+            pltpu.SemaphoreType.DMA((n_blk,)),
+        ],
+        compiler_params=pltpu.CompilerParams(collective_id=2, has_side_effects=True),
+    )(piece)
 
 
 def per_device(
@@ -257,9 +377,12 @@
         ]
     )
     wq_self, wkv_self, wo_self, wq_cross, wkv_cross, wo_cross, w_in, w_out = gathered
-    states_full = new_states.astype(jnp.float32)
-    normed = rms_rows(states_full, norm_gain[0])
-    residual = states_full
+    n_blk = lax.axis_size("blk")
+    rows_dev = new_states.shape[0] // n_blk
+    own_rows = lax.dynamic_slice_in_dim(
+        new_states, lax.axis_index("blk") * rows_dev, rows_dev, 0
+    ).astype(jnp.float32)
+    normed = rms_rows(new_states.astype(jnp.float32), norm_gain[0])
     self_cat = jnp.concatenate([wq_self, wkv_self.reshape(wkv_self.shape[0], -1)], axis=1)
     projected = jnp.dot(normed, self_cat, preferred_element_type=jnp.float32).astype(
         jnp.bfloat16
@@ -273,7 +396,9 @@
         slot_old[0],
         slot_new[0],
     )
-    residual, normed = add_branch(residual, context.reshape(-1, width_dev), wo_self, norm_gain[1])
+    part = jnp.dot(context, wo_self, preferred_element_type=jnp.float32).astype(jnp.bfloat16)
+    residual = own_rows + blk_scatter(part)
+    normed = blk_gather(rms_rows(residual, norm_gain[1]))
     queries = (
         jnp.dot(normed, wq_cross, preferred_element_type=jnp.float32)
         .astype(jnp.bfloat16)
@@ -286,13 +411,16 @@
         .reshape(req_dev, -1, 2, heads_dev, HD)
     )
     context = cross_attend(queries, key_value, slot_enc)
-    residual, normed = add_branch(residual, context.reshape(-1, width_dev), wo_cross, norm_gain[2])
+    part = jnp.dot(context.reshape(-1, width_dev), wo_cross, preferred_element_type=jnp.float32)
+    residual = residual + blk_scatter(part.astype(jnp.bfloat16))
+    normed = blk_gather(rms_rows(residual, norm_gain[2]))
     ff_dev = w_in.shape[2]
     gate_up = jnp.dot(normed, w_in.reshape(w_in.shape[0], -1), preferred_element_type=jnp.float32)
     hidden = (jax.nn.gelu(gate_up[:, :ff_dev], approximate=True) * gate_up[:, ff_dev:]).astype(
         jnp.bfloat16
     )
-    layer_out = (residual + row_total(hidden, w_out)).astype(jnp.bfloat16)
+    part = jnp.dot(hidden, w_out, preferred_element_type=jnp.float32).astype(jnp.bfloat16)
+    layer_out = blk_gather((residual + blk_scatter(part)).astype(jnp.bfloat16))
     return (layer_out, cache_dec)
 
 

time: 574 us -> 280 us (0.49)
  waiting for transfers between devices: 439 us -> 30.2 us
  Pallas kernels: 6.86 us -> 134 us
  local copies, waits for them, and re-layouts: 53.8 us -> 44 us
    psum x3 -> x0, waiting for transfers between devices: 412 us -> none  [row_total(): return lax.psum(term.astype(jnp.bfloat16), 'blk').astype(jnp.float32)]
    pallas_call x0 -> x6, Pallas kernels: none -> 127 us  [the longest x3 64.2 us: blk_gather(): pl.pallas_call(functools.partial(gather_kernel, n_blk), out_shape=jax.Sha...]
    all_to_all x2, local copies, waits for them, and re-layouts: 13.4 us -> 4.47 us  [per_device(): lax.all_to_all(ordered, 'req', split_axis=0, concat_axis=2, tiled=True)]
    unnamed x50 -> x45, local copies, waits for them, and re-layouts: 14.5 us -> 17.2 us
  transfers between devices with their start and end apart: 6 -> 3, of which waited for: 5 -> 2; matrix products, arithmetic and copies ran while one was open for 10% -> 14% of each run, Pallas kernels for 0% -> 0%
where the time goes in v2:
time: 280 us; the launch traced here: 275 us
  Pallas kernels  134 us (48%)
  local copies, waits for them, and re-layouts  44 us (16%)
  waiting for transfers between devices  30.2 us (11%)
  other arithmetic  25 us (9%)
  between operations  15.7 us (6%)
  starting transfers between devices  13.8 us (5%)
  matrix products  12.6 us (4%)
    pallas_call x3, Pallas kernels, blk_gather(): pl.pallas_call(functools.partial(gather_kernel, n_blk), out_shape=jax.Sha...  64.2 us
    pallas_call x3, Pallas kernels, blk_scatter(): pl.pallas_call(functools.partial(scatter_kernel, n_blk), out_shape=jax.Sh...  62.8 us
    unnamed x45, local copies, waits for them, and re-layouts  17.2 us
    all_to_all x1, waiting for transfers between devices, per_device(): lax.all_to_all(ordered, 'req', split_axis=0, concat_axis=2, tiled=True)  17.1 us
    all_to_all x1, waiting for transfers between devices, per_device(): lax.all_to_all(lax.all_to_all(ordered, 'req', split_axis=0, concat_axis=2...  13.1 us
    unnamed x1, other arithmetic  11.6 us
    all_to_all x1, starting transfers between devices, per_device(): lax.all_to_all(lax.all_to_all(ordered, 'req', split_axis=0, concat_axis=2...  8.61 us
    pallas_call x1, Pallas kernels, self_attention(): pl.pallas_call(self_kernel, out_shape=jax.ShapeDtypeStruct((n_q, HD), jnp...  6.86 us
  transfers between devices with their start and end apart: 3, of which 2 were waited for; matrix products, arithmetic and copies ran while one was open for 14% of the time, Pallas kernels for 0%

profile of v2, /device:TPU:33, one launch (start us, length us, event | category | flops | bytes accessed | tf_op | source)
XLA Modules:
  0.0 275.2 jit_solution(13675401297549857716)
XLA Ops:
  7.2 0.9 copy.47
  9.2 0.9 copy.48
  10.2 0.9 copy.50
  11.1 1.0 copy.51
  15.4 1.3 dynamic_slice.13
  16.7 2.0 compare_select_fusion
  19.3 1.1 broadcast_select_fusion
  20.5 5.2 %all-to-all-start = ((bf16[8,256,256]{2,1,0:T(8,128)(2,1)}), bf16[8,256,256]{2,1,0:T(8,128)(2,1)S(1)}, u32[]{:S(2)}, u32[]{:S(2)}) async-start(bf16[8,256,256]{2,1,0:T(8,128)(2,1)} %broadcast_select_fusion), calls=%async_computation | async-start | bytes 2097152 | tf_op jit(solution)/shard_map/all_to_all | solution.py:356
  25.7 1.0 convolution_reduce_fusion
  26.7 17.1 %all-to-all-done = bf16[8,256,256]{2,1,0:T(8,128)(2,1)S(1)} async-done(((bf16[8,256,256]{2,1,0:T(8,128)(2,1)}), bf16[8,256,256]{2,1,0:T(8,128)(2,1)S(1)}, u32[]{:S(2)}, u32[]{:S(2)}) %all-to-all-start) | async-done | bytes 1048608 | tf_op jit(solution)/shard_map/all_to_all | solution.py:356
  43.8 1.3 copy.53
  45.1 3.2 %copy.75 = bf16[1,256,2048]{1,0,2:T(2,128)(2,1)S(1)} copy(bf16[1,256,2048]{1,2,0:T(8,128)(2,1)} %bitcast.82) | data formatting | bytes 2097152 | tf_op jit(solution)/shard_map/all_to_all | solution.py:356
  48.7 11.6 %reduce.12 = bf16[2048,256]{1,0:T(8,128)(2,1)} reduce(bf16[2048,1,256]{2,1,0:T(2,128)(2,1)S(1)} %bitcast.81, bf16[]{:T(256)} %broadcast.85), dimensions={1}, to_apply=%bitcast.75.reduce_sub_computation | reduce | bytes 2097154
  60.3 2.2 reshape.175
  62.5 8.6 %all-to-all-start.1 = ((bf16[16,2,16384]{2,1,0:T(2,128)(2,1)}), bf16[16,2,16384]{2,1,0:T(2,128)(2,1)}, u32[]{:S(2)}, u32[]{:S(2)}) async-start(bf16[16,2,16384]{2,1,0:T(2,128)(2,1)} %reshape.175), calls=%async_computation.1 | async-start | bytes 2097152 | tf_op jit(solution)/shard_map/all_to_all | solution.py:355
  71.2 1.3 select_reduce_fusion.1
  75.9 1.2 iota_compare_fusion.2
  77.0 1.3 pad_add_fusion.lens_ref
  78.7 13.1 %all-to-all-done.1 = bf16[16,2,16384]{2,1,0:T(2,128)(2,1)} async-done(((bf16[16,2,16384]{2,1,0:T(2,128)(2,1)}), bf16[16,2,16384]{2,1,0:T(2,128)(2,1)}, u32[]{:S(2)}, u32[]{:S(2)}) %all-to-all-start.1) | async-done | bytes 1048608 | tf_op jit(solution)/shard_map/all_to_all | solution.py:355
  91.8 4.3 %reshape.176 = bf16[2048,1,256]{2,1,0:T(2,128)(2,1)S(1)} reshape(bf16[16,2,16384]{2,1,0:T(2,128)(2,1)} %all-to-all-done.1) | data formatting | bytes 2097152
  96.1 1.2 copy.58
  97.3 1.8 copy.55
  99.1 4.2 %reshape.170 = bf16[8,133120]{1,0:T(8,128)(2,1)} reshape(bf16[1064960]{0:T(1024)(128)(2,1)} %all-gather.3.cloned.1.call-done) | data formatting | bytes 4259840 | tf_op jit(solution)/shard_map/all_gather | solution.py:194
  103.3 1.9 fusion.43
  105.2 1.8 fusion.44
  107.0 1.2 reshape_reshape.7
  108.2 1.9 reshape_reshape.6
  110.1 1.8 reshape_reshape_reshape.10
  111.9 2.1 reshape_reshape_reshape.11
  114.1 1.9 convolution_convert_fusion.3
  116.1 6.9 %shard_map.185 = bf16[512,64]{1,0:T(8,128)(2,1)S(1)} custom-call(s32[2]{0:T(128)S(1)} %pad_add_fusion.lens_ref, bf16[512,64]{1,0:T(8,128)(2,1)S(1)} %get-tuple-element.12.q_ref, bf16[4096,128]{1,0:T(8,128)(2,1)S(1)} %bitcast.76, bf16[512,64]{1,0:T(8,128)(2,1)S(1)} %get-tuple-element.11.kn_ref, bf16[512,64]{1,0:T(8,128)(2,1)S(1)} %get-tuple-element.10.vn_ref, ...), custom_call_target="tpu_custom_call" | custom-call | tf_op jit(solution)/shard_map/pallas_call | solution.py:183
  123.0 1.4 convolution_convert_fusion.2.part_ref
  124.3 20.3 %shard_map.186 = f32[32,1024]{1,0:T(8,128)} custom-call(bf16[512,1024]{1,0:T(8,128)(2,1)} %convolution_convert_fusion.2.part_ref), custom_call_target="tpu_custom_call" | custom-call | tf_op jit(solution)/shard_map/pallas_call | solution.py:294
  144.6 1.0 multiply_reduce_fusion.1
  145.7 1.6 multiply_convert_fusion.1.piece_ref
  147.3 21.0 %shard_map.187 = bf16[512,1024]{1,0:T(8,128)(2,1)} custom-call(bf16[32,1024]{1,0:T(8,128)(2,1)} %multiply_convert_fusion.1.piece_ref), custom_call_target="tpu_custom_call" | custom-call | tf_op jit(solution)/shard_map/pallas_call | solution.py:312
  168.4 1.5 convolution_convert_fusion.4
  169.9 1.0 fusion.47
  171.1 2.6 convolution_convert_fusion.1.part_ref
  173.7 21.2 %shard_map.188 = f32[32,1024]{1,0:T(8,128)} custom-call(bf16[512,1024]{1,0:T(8,128)(2,1)} %convolution_convert_fusion.1.part_ref), custom_call_target="tpu_custom_call" | custom-call | tf_op jit(solution)/shard_map/pallas_call | solution.py:294
  194.9 1.1 multiply_reduce_fusion
  196.7 21.6 %shard_map.189 = bf16[512,1024]{1,0:T(8,128)(2,1)} custom-call(bf16[32,1024]{1,0:T(8,128)(2,1)} %multiply_convert_fusion.piece_ref), custom_call_target="tpu_custom_call" | custom-call | tf_op jit(solution)/shard_map/pallas_call | solution.py:312
  218.3 1.8 fusion.48
  220.1 1.5 convolution_convert_fusion.part_ref
  221.6 21.3 %shard_map.190 = f32[32,1024]{1,0:T(8,128)} custom-call(bf16[512,1024]{1,0:T(8,128)(2,1)} %convolution_convert_fusion.part_ref), custom_call_target="tpu_custom_call" | custom-call | tf_op jit(solution)/shard_map/pallas_call | solution.py:294
  243.0 1.5 add_convert_fusion.piece_ref
  244.5 21.5 %shard_map.191 = bf16[512,1024]{1,0:T(8,128)(2,1)} custom-call(bf16[32,1024]{1,0:T(8,128)(2,1)} %add_convert_fusion.piece_ref), custom_call_target="tpu_custom_call" | custom-call | tf_op jit(solution)/shard_map/pallas_call | solution.py:312
  266.1 2.3 copy.84
  (69 shorter events, 9.3 us)
Async XLA Ops:
  7.2 11.5 %copy-start = (bf16[8,256,256]{2,1,0:T(8,128)(2,1)S(1)}, bf16[8,256,256]{2,1,0:T(8,128)(2,1)}, u32[]{:S(2)}) copy-start(bf16[8,256,256]{2,1,0:T(8,128)(2,1)} %param.20) | copy-start | bytes 3145732
  7.2 12.1 %copy-start.10 = (s32[8]{0:T(128)S(1)}, s32[8]{0:T(128)}, u32[]{:S(2)}) copy-start(s32[8]{0:T(128)} %param.21) | copy-start | bytes 100
  7.2 91.9 %all-gather.3.cloned.1.call-start = ((), (), s32[]{:S(2)}) async-start(), calls=%async_computation.2 | async-start | bytes 2396160 | tf_op jit(solution)/shard_map/all_gather | solution.py:194
  14.7 0.7 copy-start.7
  19.3 6.3 %copy-start.13 = (s32[4608]{0:T(1024)S(1)}, s32[4608]{0:T(1024)}, u32[]{:S(2)}) copy-start(s32[4608]{0:T(1024)} %param.25) | copy-start | bytes 55300
  20.5 23.3 %all-to-all-start = ((bf16[8,256,256]{2,1,0:T(8,128)(2,1)}), bf16[8,256,256]{2,1,0:T(8,128)(2,1)S(1)}, u32[]{:S(2)}, u32[]{:S(2)}) async-start(bf16[8,256,256]{2,1,0:T(8,128)(2,1)} %broadcast_select_fusion), calls=%async_computation | async-start | bytes 2097152 | tf_op jit(solution)/shard_map/all_to_all | solution.py:356
  60.3 10.8 %copy-start.11 = (s32[8]{0:T(128)S(1)}, s32[8]{0:T(128)}, u32[]{:S(2)}) copy-start(s32[8]{0:T(128)} %param.22) | copy-start | bytes 100
  60.3 10.8 %copy-start.12 = (s32[8]{0:T(128)S(1)}, s32[8]{0:T(128)}, u32[]{:S(2)}) copy-start(s32[8]{0:T(128)} %param.23) | copy-start | bytes 100
  60.3 18.1 %copy-start.5 = (bf16[512,1024]{1,0:T(8,128)(2,1)S(1)}, bf16[512,1024]{1,0:T(8,128)(2,1)}, u32[]{:S(2)}) copy-start(bf16[512,1024]{1,0:T(8,128)(2,1)} %param.18) | copy-start | bytes 3145732
  62.5 16.1 %copy-start.8 = (f32[3,1024]{1,0:T(4,128)S(1)}, f32[3,1024]{1,0:T(4,128)}, u32[]{:S(2)}) copy-start(f32[3,1024]{1,0:T(4,128)} %param.27) | copy-start | bytes 36868
  62.5 29.3 %all-to-all-start.1 = ((bf16[16,2,16384]{2,1,0:T(2,128)(2,1)}), bf16[16,2,16384]{2,1,0:T(2,128)(2,1)}, u32[]{:S(2)}, u32[]{:S(2)}) async-start(bf16[16,2,16384]{2,1,0:T(2,128)(2,1)} %reshape.175), calls=%async_computation.1 | async-start | bytes 2097152 | tf_op jit(solution)/shard_map/all_to_all | solution.py:355
  99.1 17.0 %copy-start.1 = (bf16[1,16,256,128]{3,2,1,0:T(8,128)(2,1)}, bf16[1,16,256,128]{3,2,1,0:T(8,128)(2,1)S(1)}, u32[]{:S(2)}) copy-start(bf16[1,16,256,128]{3,2,1,0:T(8,128)(2,1)S(1)} %copy.55) | copy-start | bytes 3145732
  105.2 6.7 %slice-start.1 = ((bf16[8,133120]{1,0:T(8,128)(2,1)}), bf16[8,45056]{1,0:T(8,128)(2,1)S(1)}, s32[]{:S(2)}) async-start(bf16[8,133120]{1,0:T(8,128)(2,1)} %reshape.170), calls=%async_computation.4 | async-start | bytes 1441792 | tf_op jit(solution)/shard_map/slice | solution.py:199
  122.9 45.4 %copy-start.6 = (bf16[512,1024]{1,0:T(8,128)(2,1)S(1)}, bf16[512,1024]{1,0:T(8,128)(2,1)}, u32[]{:S(2)}) copy-start(bf16[512,1024]{1,0:T(8,128)(2,1)} %param.19) | copy-start | bytes 3145732
  124.3 45.6 %copy-start.9 = (pred[512]{0:T(512)(128)(4,1)S(1)}, pred[512]{0:T(512)(128)(4,1)}, u32[]{:S(2)}) copy-start(pred[512]{0:T(512)(128)(4,1)} %iota_compare_fusion.2) | copy-start | bytes 1540
  168.4 1.6 copy-start.2
  171.1 23.8 %copy-start.4 = (f32[32,1024]{1,0:T(8,128)S(1)}, f32[32,1024]{1,0:T(8,128)}, u32[]{:S(2)}) copy-start(f32[32,1024]{1,0:T(8,128)} %shard_map.186) | copy-start | bytes 393220
  173.7 44.6 %copy-start.3 = (bf16[1024,352]{1,0:T(8,128)(2,1)S(1)}, bf16[1024,352]{1,0:T(8,128)(2,1)}, u32[]{:S(2)}) copy-start(bf16[1024,352]{1,0:T(8,128)(2,1)} %reshape_reshape_reshape.11) | copy-start | bytes 2162692
  194.9 25.2 %slice-start = ((bf16[8,133120]{1,0:T(8,128)(2,1)}), bf16[8,22528]{1,0:T(8,128)(2,1)S(1)}, s32[]{:S(2)}) async-start(bf16[8,133120]{1,0:T(8,128)(2,1)} %reshape.170), calls=%async_computation.3 | async-start | bytes 720896 | tf_op jit(solution)/shard_map/slice | solution.py:199
Sparse Core Ops, SparseCore 0:
  15.5 74.2 all-gather.2

commit v3 on v2

--- a/solution.py
+++ b/solution.py
@@ -321,6 +321,129 @@
         ],
         compiler_params=pltpu.CompilerParams(collective_id=2, has_side_effects=True),
     )(piece)
+
+
+def prologue_kernel(n_req, n_blk, ordered_ref, packed_ref, cache_ref, wts_ref, w_send, w_recv, c_send, c_recv, local_sem):
+    r = lax.axis_index("req")
+    b = lax.axis_index("blk")
+    n_slot, span, width = ordered_ref.shape
+    piece = width // 2
+    copies = []
+    for k in range(1, n_req):
+        peer = lax.rem(r + k, n_req)
+        copy = pltpu.make_async_remote_copy(
+            src_ref=packed_ref,
+            dst_ref=wts_ref.at[r],
+            send_sem=w_send.at[peer],
+            recv_sem=w_recv.at[r],
+            device_id=(peer, b),
+            device_id_type=MESH_IDS,
+        )
+        copy.start()
+        copies.append(copy)
+    rows = pl.ds(pl.multiple_of(b * span, span), span)
+    for s in range(n_slot):
+        for hh in range(2):
+            head = 2 * r + hh
+            is_self = jnp.logical_and(r == s, head == b)
+            src = ordered_ref.at[s, :, pl.ds(hh * piece, piece)]
+            copy = pltpu.make_async_remote_copy(
+                src_ref=src,
+                dst_ref=cache_ref.at[rows],
+                send_sem=c_send.at[s * 2 + hh],
+                recv_sem=c_recv.at[b],
+                device_id=(s, head),
+                device_id_type=MESH_IDS,
+            )
+
+            @pl.when(jnp.logical_not(is_self))
+            def _():
+                copy.start()
+
+            @pl.when(is_self)
+            def _():
+                local = pltpu.make_async_copy(src, cache_ref.at[rows], local_sem.at[0])
+                local.start()
+                local.wait()
+
+            copies.append((copy, is_self))
+    wts_ref[r] = packed_ref[...]
+    for k in range(1, n_req):
+        src_req = lax.rem(r + n_req - k, n_req)
+        incoming = pltpu.make_async_remote_copy(
+            src_ref=packed_ref,
+            dst_ref=wts_ref.at[src_req],
+            send_sem=w_send.at[src_req],
+            recv_sem=w_recv.at[src_req],
+            device_id=(src_req, b),
+            device_id_type=MESH_IDS,
+        )
+        incoming.wait_recv()
+    owner = b // 2
+    for j in range(n_blk):
+        incoming = pltpu.make_async_remote_copy(
+            src_ref=ordered_ref.at[0, :, pl.ds(0, piece)],
+            dst_ref=cache_ref.at[pl.ds(j * span, span)],
+            send_sem=c_send.at[0],
+            recv_sem=c_recv.at[j],
+            device_id=(owner, j),
+            device_id_type=MESH_IDS,
+        )
+
+        @pl.when(jnp.logical_not(jnp.logical_and(owner == r, j == b)))
+        def _():
+            incoming.wait_recv()
+
+    for item in copies:
+        if isinstance(item, tuple):
+            copy, is_self = item
+
+            @pl.when(jnp.logical_not(is_self))
+            def _():
+                copy.wait_send()
+
+        else:
+            item.wait_send()
+
+
+def prologue(ordered, packed):
+    n_req = lax.axis_size("req")
+    n_blk = lax.axis_size("blk")
+    n_slot, span, width = ordered.shape
+    any_spec = pl.BlockSpec(memory_space=pl.ANY)
+    vmem = pl.BlockSpec(memory_space=pltpu.VMEM)
+    return pl.pallas_call(
+        functools.partial(prologue_kernel, n_req, n_blk),
+        out_shape=(
+            jax.ShapeDtypeStruct((span * n_blk, width // 2), ordered.dtype),
+            jax.ShapeDtypeStruct((n_req,) + packed.shape, packed.dtype),
+        ),
+        in_specs=[any_spec, vmem],
+        out_specs=(any_spec, vmem),
+        scratch_shapes=[
+            pltpu.SemaphoreType.DMA((n_req,)),
+            pltpu.SemaphoreType.DMA((n_req,)),
+            pltpu.SemaphoreType.DMA((2 * n_slot,)),
+            pltpu.SemaphoreType.DMA((n_blk,)),
+            pltpu.SemaphoreType.DMA((1,)),
+        ],
+        compiler_params=pltpu.CompilerParams(has_side_effects=True),
+    )(ordered, packed)
+
+
+def unpack(whole, pieces):
+    n_req = whole.shape[0]
+    whole = whole.reshape(n_req, -1)
+    out, at = [], 0
+    for w, axis in pieces:
+        size = w.size
+        part = whole[:, at : at + size].reshape((n_req,) + w.shape)
+        at += size
+        part = jnp.moveaxis(part, 0, axis)
+        shape = list(w.shape)
+        shape[axis] *= n_req
+        out.append(part.reshape(shape))
+    return out
 
 
 def per_device(
@@ -352,30 +475,25 @@
     slot_old = pick_lengths(cache_lengths, own_slots)
     slot_enc = pick_lengths(enc_lengths, own_slots)
     ordered = jnp.take(cache_in, slot_order, axis=0)
-    cache_dec = lax.all_to_all(
-        lax.all_to_all(ordered, "req", split_axis=0, concat_axis=2, tiled=True),
-        "blk",
-        split_axis=2,
-        concat_axis=1,
-        tiled=True,
-    )
     onehot = (bucket_of[:, None] == jnp.arange(rel_bias.shape[0], dtype=jnp.int32)[None, :]).astype(
         jnp.float32
     )
     own_bias = lax.dynamic_slice_in_dim(rel_bias, lax.axis_index("blk") * heads_dev, heads_dev, 1)
     bias_dist = jnp.dot(onehot, own_bias, precision=lax.Precision.HIGHEST).T
-    gathered = pack_gather(
-        [
-            (self_q, 0),
-            (self_kv, 0),
-            (self_out, 1),
-            (cross_q, 0),
-            (cross_kv, 0),
-            (cross_out, 1),
-            (ff_in, 0),
-            (ff_out, 1),
-        ]
-    )
+    pieces = [
+        (self_q, 0),
+        (self_kv, 0),
+        (self_out, 1),
+        (cross_q, 0),
+        (cross_kv, 0),
+        (cross_out, 1),
+        (ff_in, 0),
+        (ff_out, 1),
+    ]
+    flat = jnp.concatenate([w.reshape(-1) for w, _ in pieces])
+    cache_blk, whole = prologue(ordered, flat.reshape(-1, 128))
+    cache_dec = cache_blk[None]
+    gathered = unpack(whole, pieces)
     wq_self, wkv_self, wo_self, wq_cross, wkv_cross, wo_cross, w_in, w_out = gathered
     n_blk = lax.axis_size("blk")
     rows_dev = new_states.shape[0] // n_blk

time: 280 us -> 274 us (0.979)
  Pallas kernels: 134 us -> 209 us
  waiting for transfers between devices: 30.2 us -> 0 us
  local copies, waits for them, and re-layouts: 44 us -> 28.3 us
  starting transfers between devices: 13.8 us -> 0 us
  between operations: 15.7 us -> 2.45 us
  other arithmetic: 25 us -> 15.6 us
    pallas_call x0 -> x1, Pallas kernels: none -> 56.9 us  [prologue(): pl.pallas_call(functools.partial(prologue_kernel, n_req, n_blk), out_shap...]
    all_to_all x2 -> x0, waiting for transfers between devices: 30.2 us -> none  [the longest x1 17.1 us: per_device(): lax.all_to_all(ordered, 'req', split_axis=0, concat_axis=2, tiled=True)]
    pallas_call x3, Pallas kernels: 62.8 us -> 79.9 us  [blk_scatter(): pl.pallas_call(functools.partial(scatter_kernel, n_blk), out_shape=jax.Sh...]
    all_to_all x2 -> x0, starting transfers between devices: 13.8 us -> none  [the longest x1 8.61 us: per_device(): lax.all_to_all(lax.all_to_all(ordered, 'req', split_axis=0, concat_axis=2...]
    unnamed x1 -> x0, other arithmetic: 11.6 us -> none
    all_to_all x3 -> x0, local copies, waits for them, and re-layouts: 6.26 us -> none  [the longest x2 4.47 us: per_device(): lax.all_to_all(ordered, 'req', split_axis=0, concat_axis=2, tiled=True)]
    unnamed x45 -> x43, local copies, waits for them, and re-layouts: 17.2 us -> 11.6 us
    all_gather x1 -> x0, local copies, waits for them, and re-layouts: 4.2 us -> none  [pack_gather(): whole = lax.all_gather(flat, 'req', axis=0, tiled=False)]
  transfers between devices with their start and end apart: 3 -> 0, of which waited for: 2 -> 0; matrix products, arithmetic and copies ran while one was open for 14% -> 0% of each run, Pallas kernels for 0% -> 0%
where the time goes in v3:
time: 274 us; the launch traced here: 270 us
  Pallas kernels  209 us (76%)
  local copies, waits for them, and re-layouts  28.3 us (10%)
  other arithmetic  15.6 us (6%)
  matrix products  14.5 us (5%)
    pallas_call x3, Pallas kernels, blk_scatter(): pl.pallas_call(functools.partial(scatter_kernel, n_blk), out_shape=jax.Sh...  79.9 us
    pallas_call x3, Pallas kernels, blk_gather(): pl.pallas_call(functools.partial(gather_kernel, n_blk), out_shape=jax.Sha...  65 us
    pallas_call x1, Pallas kernels, prologue(): pl.pallas_call(functools.partial(prologue_kernel, n_req, n_blk), out_shap...  56.9 us
    unnamed x43, local copies, waits for them, and re-layouts  11.6 us
    pallas_call x1, Pallas kernels, self_attention(): pl.pallas_call(self_kernel, out_shape=jax.ShapeDtypeStruct((n_q, HD), jnp...  6.85 us

profile of v3, /device:TPU:33, one launch (start us, length us, event | category | flops | bytes accessed | tf_op | source)
XLA Modules:
  0.0 269.6 jit_solution(4835046352006533077)
XLA Ops:
  0.7 1.3 dynamic_slice.13
  2.0 0.7 compare_and_fusion
  2.7 2.0 select_reduce_fusion.1
  6.1 1.4 pad_add_fusion.lens_ref
  7.5 2.0 compare_select_fusion
  9.5 0.6 iota_compare_fusion.2
  10.1 1.5 fusion
  11.7 0.8 fusion.46
  12.5 1.0 convolution_reduce_fusion
  14.1 0.6 pad_slice_fusion
  14.8 0.6 concatenate.11
  15.6 0.8 copy.27
  16.6 0.8 copy.29
  17.5 0.9 copy.28
  18.5 0.9 copy.30
  20.6 1.1 broadcast_select_fusion.ordered_ref
  21.8 56.9 %shard_map.185 = (bf16[4096,128]{1,0:T(8,128)(2,1)}, bf16[8,1040,128]{2,1,0:T(8,128)(2,1)}) custom-call(bf16[8,256,256]{2,1,0:T(8,128)(2,1)} %broadcast_select_fusion.ordered_ref, bf16[1040,128]{1,0:T(8,128)(2,1)} %bitcast.78), custom_call_target="tpu_custom_call" | custom-call | tf_op jit(solution)/shard_map/pallas_call | solution.py:415
  78.6 4.8 %copy.51 = bf16[1,8,1040,128]{3,1,2,0:T(8,128)(2,1)S(1)} copy(bf16[1,8,1040,128]{3,2,1,0:T(8,128)(2,1)} %bitcast.75) | data formatting | bytes 4259840
  83.4 0.8 slice.102
  84.2 0.8 fusion.43
  85.0 1.2 reshape_reshape.7
  86.1 1.9 reshape_reshape.6
  88.0 0.8 fusion.44
  88.8 0.9 slice.99
  89.8 1.9 reshape_reshape_reshape.10
  91.7 2.4 convolution_convert_fusion.4
  94.1 2.1 reshape_reshape_reshape.11
  96.2 0.8 reshape_reshape_reshape.9
  97.0 1.7 convolution_convert_fusion.3
  98.9 6.8 %shard_map.186 = bf16[512,64]{1,0:T(8,128)(2,1)S(1)} custom-call(s32[2]{0:T(128)S(1)} %pad_add_fusion.lens_ref, bf16[512,64]{1,0:T(8,128)(2,1)S(1)} %get-tuple-element.16.q_ref, bf16[4096,128]{1,0:T(8,128)(2,1)S(1)} %copy-done.1, bf16[512,64]{1,0:T(8,128)(2,1)S(1)} %get-tuple-element.15.kn_ref, bf16[512,64]{1,0:T(8,128)(2,1)S(1)} %get-tuple-element.14.vn_ref, ...), custom_call_target="tpu_custom_call" | custom-call | tf_op jit(solution)/shard_map/pallas_call | solution.py:183
  105.8 1.4 convolution_convert_fusion.2.part_ref
  107.1 37.5 %shard_map.187 = f32[32,1024]{1,0:T(8,128)} custom-call(bf16[512,1024]{1,0:T(8,128)(2,1)} %convolution_convert_fusion.2.part_ref), custom_call_target="tpu_custom_call" | custom-call | tf_op jit(solution)/shard_map/pallas_call | solution.py:294
  144.6 1.0 multiply_reduce_fusion.1
  145.6 1.6 multiply_convert_fusion.1.piece_ref
  147.3 21.8 %shard_map.188 = bf16[512,1024]{1,0:T(8,128)(2,1)} custom-call(bf16[32,1024]{1,0:T(8,128)(2,1)} %multiply_convert_fusion.1.piece_ref), custom_call_target="tpu_custom_call" | custom-call | tf_op jit(solution)/shard_map/pallas_call | solution.py:312
  169.1 2.0 fusion.47
  171.3 2.7 convolution_convert_fusion.1.part_ref
  173.9 21.2 %shard_map.189 = f32[32,1024]{1,0:T(8,128)} custom-call(bf16[512,1024]{1,0:T(8,128)(2,1)} %convolution_convert_fusion.1.part_ref), custom_call_target="tpu_custom_call" | custom-call | tf_op jit(solution)/shard_map/pallas_call | solution.py:294
  195.1 1.0 multiply_reduce_fusion
  196.2 0.7 multiply_convert_fusion.piece_ref
  196.9 21.6 %shard_map.190 = bf16[512,1024]{1,0:T(8,128)(2,1)} custom-call(bf16[32,1024]{1,0:T(8,128)(2,1)} %multiply_convert_fusion.piece_ref), custom_call_target="tpu_custom_call" | custom-call | tf_op jit(solution)/shard_map/pallas_call | solution.py:312
  218.5 1.8 fusion.48
  220.4 1.5 convolution_convert_fusion.part_ref
  221.9 21.3 %shard_map.191 = f32[32,1024]{1,0:T(8,128)} custom-call(bf16[512,1024]{1,0:T(8,128)(2,1)} %convolution_convert_fusion.part_ref), custom_call_target="tpu_custom_call" | custom-call | tf_op jit(solution)/shard_map/pallas_call | solution.py:294
  243.2 1.6 add_convert_fusion.piece_ref
  244.7 21.6 %shard_map.192 = bf16[512,1024]{1,0:T(8,128)(2,1)} custom-call(bf16[32,1024]{1,0:T(8,128)(2,1)} %add_convert_fusion.piece_ref), custom_call_target="tpu_custom_call" | custom-call | tf_op jit(solution)/shard_map/pallas_call | solution.py:312
  266.3 2.3 copy.61
  268.6 1.0 copy.62
  (54 shorter events, 2.6 us)
Async XLA Ops:
  0.6 19.4 %copy-start = (bf16[8,256,256]{2,1,0:T(8,128)(2,1)S(1)}, bf16[8,256,256]{2,1,0:T(8,128)(2,1)}, u32[]{:S(2)}) copy-start(bf16[8,256,256]{2,1,0:T(8,128)(2,1)} %param.20) | copy-start | bytes 3145732
  0.6 19.3 %copy-start.11 = (bf16[176,128]{1,0:T(8,128)(2,1)S(1)}, bf16[176,128]{1,0:T(8,128)(2,1)}, u32[]{:S(2)}) copy-start(bf16[176,128]{1,0:T(8,128)(2,1)} %param.35) | copy-start | bytes 135172
  0.7 18.8 %copy-start.10 = (bf16[128,2,176]{0,2,1:T(8,128)(2,1)S(1)}, bf16[128,2,176]{0,2,1:T(8,128)(2,1)}, u32[]{:S(2)}) copy-start(bf16[128,2,176]{0,2,1:T(8,128)(2,1)} %param.34) | copy-start | bytes 270340
  0.7 19.3 %copy-start.13 = (bf16[64,128]{1,0:T(8,128)(2,1)S(1)}, bf16[64,128]{1,0:T(8,128)(2,1)}, u32[]{:S(2)}) copy-start(bf16[64,128]{1,0:T(8,128)(2,1)} %param.33) | copy-start | bytes 49156
  0.7 19.2 %copy-start.12 = (bf16[64,128]{1,0:T(8,128)(2,1)S(1)}, bf16[64,128]{1,0:T(8,128)(2,1)}, u32[]{:S(2)}) copy-start(bf16[64,128]{1,0:T(8,128)(2,1)} %param.30) | copy-start | bytes 49156
  20.0 1.8 copy-start.9
  89.7 4.4 %copy-start.3 = (bf16[8,45056]{1,0:T(8,128)(2,1)S(1)}, bf16[8,45056]{1,0:T(8,128)(2,1)}, u32[]{:S(2)}) copy-start(bf16[8,45056]{1,0:T(8,128)(2,1)} %slice.99) | copy-start | bytes 2162692
  89.8 6.4 %copy-start.6 = (bf16[8,16384]{1,0:T(8,128)(2,1)S(1)}, bf16[8,16384]{1,0:T(8,128)(2,1)}, u32[]{:S(2)}) copy-start(bf16[8,16384]{1,0:T(8,128)(2,1)} %get-tuple-element.13) | copy-start | bytes 786436
  89.8 7.3 %copy-start.5 = (bf16[512,1024]{1,0:T(8,128)(2,1)S(1)}, bf16[512,1024]{1,0:T(8,128)(2,1)}, u32[]{:S(2)}) copy-start(bf16[512,1024]{1,0:T(8,128)(2,1)} %param.18) | copy-start | bytes 3145732
  97.0 1.9 copy-start.1
  97.0 8.7 %copy-start.7 = (bf16[8,8192]{1,0:T(8,128)(2,1)S(1)}, bf16[8,8192]{1,0:T(8,128)(2,1)}, u32[]{:S(2)}) copy-start(bf16[8,8192]{1,0:T(8,128)(2,1)} %get-tuple-element.10) | copy-start | bytes 393220
  171.3 23.8 %copy-start.4 = (f32[32,1024]{1,0:T(8,128)S(1)}, f32[32,1024]{1,0:T(8,128)}, u32[]{:S(2)}) copy-start(f32[32,1024]{1,0:T(8,128)} %shard_map.187) | copy-start | bytes 393220
  173.9 44.6 %copy-start.2 = (bf16[1024,352]{1,0:T(8,128)(2,1)S(1)}, bf16[1024,352]{1,0:T(8,128)(2,1)}, u32[]{:S(2)}) copy-start(bf16[1024,352]{1,0:T(8,128)(2,1)} %reshape_reshape_reshape.11) | copy-start | bytes 2162692
  196.2 24.2 %copy-start.8 = (bf16[8,22528]{1,0:T(8,128)(2,1)S(1)}, bf16[8,22528]{1,0:T(8,128)(2,1)}, u32[]{:S(2)}) copy-start(bf16[8,22528]{1,0:T(8,128)(2,1)} %slice.102) | copy-start | bytes 1081348

commit v4 on v3

--- a/solution.py
+++ b/solution.py
@@ -480,20 +480,12 @@
     )
     own_bias = lax.dynamic_slice_in_dim(rel_bias, lax.axis_index("blk") * heads_dev, heads_dev, 1)
     bias_dist = jnp.dot(onehot, own_bias, precision=lax.Precision.HIGHEST).T
-    pieces = [
-        (self_q, 0),
-        (self_kv, 0),
-        (self_out, 1),
-        (cross_q, 0),
-        (cross_kv, 0),
-        (cross_out, 1),
-        (ff_in, 0),
-        (ff_out, 1),
-    ]
-    flat = jnp.concatenate([w.reshape(-1) for w, _ in pieces])
+    early = [(self_q, 0), (self_kv, 0), (self_out, 1)]
+    late = [(cross_q, 0), (cross_kv, 0), (cross_out, 1), (ff_in, 0), (ff_out, 1)]
+    flat = jnp.concatenate([w.reshape(-1) for w, _ in early])
     cache_blk, whole = prologue(ordered, flat.reshape(-1, 128))
     cache_dec = cache_blk[None]
-    gathered = unpack(whole, pieces)
+    gathered = unpack(whole, early) + pack_gather(late)
     wq_self, wkv_self, wo_self, wq_cross, wkv_cross, wo_cross, w_in, w_out = gathered
     n_blk = lax.axis_size("blk")
     rows_dev = new_states.shape[0] // n_blk

time: 274 us -> 259 us (0.945)
  Pallas kernels: 209 us -> 183 us
  between operations: 2.45 us -> 15.5 us
    pallas_call x1, Pallas kernels: 56.9 us -> 39.7 us  [prologue(): pl.pallas_call(functools.partial(prologue_kernel, n_req, n_blk), out_shap...]
    pallas_call x3, Pallas kernels: 79.9 us -> 71.4 us  [blk_scatter(): pl.pallas_call(functools.partial(scatter_kernel, n_blk), out_shape=jax.Sh...]
    all_gather x0 -> x1, local copies, waits for them, and re-layouts: none -> 3.26 us  [pack_gather(): whole = lax.all_gather(flat, 'req', axis=0, tiled=False)]
    slice x4 -> x2, local copies, waits for them, and re-layouts: 3.27 us -> 0.04 us  [unpack(): part = whole[:, at:at + size].reshape((n_req,) + w.shape)]
    unnamed x43 -> x36, local copies, waits for them, and re-layouts: 11.6 us -> 10.7 us
  transfers between devices with their start and end apart: 0 -> 1, of which waited for: 0 -> 0; matrix products, arithmetic and copies ran while one was open for 0% -> 9% of each run, Pallas kernels for 0% -> 38%
where the time goes in v4:
time: 259 us; the launch traced here: 254 us
  Pallas kernels  183 us (71%)
  local copies, waits for them, and re-layouts  26.3 us (10%)
  between operations  15.5 us (6%)
  other arithmetic  15.2 us (6%)
  matrix products  13.9 us (5%)
    pallas_call x3, Pallas kernels, blk_scatter(): pl.pallas_call(functools.partial(scatter_kernel, n_blk), out_shape=jax.Sh...  71.4 us
    pallas_call x3, Pallas kernels, blk_gather(): pl.pallas_call(functools.partial(gather_kernel, n_blk), out_shape=jax.Sha...  64.7 us
    pallas_call x1, Pallas kernels, prologue(): pl.pallas_call(functools.partial(prologue_kernel, n_req, n_blk), out_shap...  39.7 us
    unnamed x36, local copies, waits for them, and re-layouts  10.7 us
    pallas_call x1, Pallas kernels, self_attention(): pl.pallas_call(self_kernel, out_shape=jax.ShapeDtypeStruct((n_q, HD), jnp...  6.86 us
  transfers between devices with their start and end apart: 1, of which 0 were waited for; matrix products, arithmetic and copies ran while one was open for 9% of the time, Pallas kernels for 38%

profile of v4, /device:TPU:33, one launch (start us, length us, event | category | flops | bytes accessed | tf_op | source)
XLA Modules:
  0.0 253.7 jit_solution(8012191416013887834)
XLA Ops:
  7.2 0.9 copy.36
  8.2 0.9 copy.37
  9.2 1.0 copy.38
  10.5 0.7 bitcast_dynamic-update-slice_fusion.1
  11.2 0.8 bitcast_dynamic-update-slice_fusion
  12.0 0.7 copy-done.6
  12.7 0.7 compare_and_fusion
  13.4 1.2 dynamic_slice.13
  14.6 1.9 compare_select_fusion
  16.5 0.8 copy.33
  17.5 0.9 copy.34
  19.1 1.1 broadcast_select_fusion.ordered_ref
  20.2 0.6 maximum_bitcast_fusion.packed_ref
  20.9 39.7 %shard_map.185 = (bf16[4096,128]{1,0:T(8,128)(2,1)}, bf16[8,256,128]{2,1,0:T(8,128)(2,1)}) custom-call(bf16[8,256,256]{2,1,0:T(8,128)(2,1)} %broadcast_select_fusion.ordered_ref, bf16[256,128]{1,0:T(8,128)(2,1)} %maximum_bitcast_fusion.packed_ref), custom_call_target="tpu_custom_call" | custom-call | tf_op jit(solution)/shard_map/pallas_call | solution.py:415
  60.6 1.5 copy.57
  62.2 1.2 select_reduce_fusion.1
  64.5 1.0 convolution_reduce_fusion
  66.1 0.6 concatenate.14
  66.7 0.7 pad_slice_fusion
  67.7 0.8 reshape_reshape_reshape.9
  68.5 1.0 reshape_reshape.6
  69.4 1.3 pad_add_fusion.lens_ref
  71.0 1.7 convolution_convert_fusion.3
  72.9 6.9 %shard_map.186 = bf16[512,64]{1,0:T(8,128)(2,1)S(1)} custom-call(s32[2]{0:T(128)S(1)} %pad_add_fusion.lens_ref, bf16[512,64]{1,0:T(8,128)(2,1)S(1)} %get-tuple-element.14.q_ref, bf16[4096,128]{1,0:T(8,128)(2,1)S(1)} %copy-done.1, bf16[512,64]{1,0:T(8,128)(2,1)S(1)} %get-tuple-element.13.kn_ref, bf16[512,64]{1,0:T(8,128)(2,1)S(1)} %get-tuple-element.12.vn_ref, ...), custom_call_target="tpu_custom_call" | custom-call | tf_op jit(solution)/shard_map/pallas_call | solution.py:183
  79.8 1.4 convolution_convert_fusion.2.part_ref
  81.1 28.9 %shard_map.187 = f32[32,1024]{1,0:T(8,128)} custom-call(bf16[512,1024]{1,0:T(8,128)(2,1)} %convolution_convert_fusion.2.part_ref), custom_call_target="tpu_custom_call" | custom-call | tf_op jit(solution)/shard_map/pallas_call | solution.py:294
  110.0 1.0 multiply_reduce_fusion.1
  111.1 1.6 multiply_convert_fusion.1.piece_ref
  112.7 21.5 %shard_map.188 = bf16[512,1024]{1,0:T(8,128)(2,1)} custom-call(bf16[32,1024]{1,0:T(8,128)(2,1)} %multiply_convert_fusion.1.piece_ref), custom_call_target="tpu_custom_call" | custom-call | tf_op jit(solution)/shard_map/pallas_call | solution.py:312
  134.9 3.3 %reshape.177 = bf16[8,100352]{1,0:T(8,128)(2,1)} reshape(bf16[802816]{0:T(1024)(128)(2,1)} %all-gather.3.cloned.1.call-done) | data formatting | bytes 3211264 | tf_op jit(solution)/shard_map/all_gather | solution.py:194
  138.1 1.7 fusion.43
  139.8 0.8 reshape_reshape_reshape.10
  141.0 2.3 reshape_reshape_reshape.11
  143.3 1.9 convolution_convert_fusion.4
  145.2 1.7 fusion.47
  146.9 1.4 fusion.7
  148.3 3.0 %convolution_convert_fusion.1.part_ref = bf16[512,1024]{1,0:T(8,128)(2,1)} fusion(f32[512,512]{0,1:T(8,128)} %get-tuple-element.19, f32[512]{0:T(512)S(1)} %fusion.7, f32[512]{0:T(512)S(1)} %get-tuple-element.18, bf16[8,8,8,128]{3,2,1,0:T(8,128)(2,1)} %bitcast.78, bf16[1,512,2,1,64]{1,4,2,3,0:T(8,128)(2,1)S(1)} %bitcast.77), kind=kOutput, calls=%fused_computation.7 | convolution fusion | flops 102006784 | bytes 2297856 | tf_op jit(solution)/shard_map/dot_general | solution.py:524
  151.2 21.2 %shard_map.189 = f32[32,1024]{1,0:T(8,128)} custom-call(bf16[512,1024]{1,0:T(8,128)(2,1)} %convolution_convert_fusion.1.part_ref), custom_call_target="tpu_custom_call" | custom-call | tf_op jit(solution)/shard_map/pallas_call | solution.py:294
  172.4 1.0 multiply_reduce_fusion
  173.5 0.7 multiply_convert_fusion.piece_ref
  174.2 21.6 %shard_map.190 = bf16[512,1024]{1,0:T(8,128)(2,1)} custom-call(bf16[32,1024]{1,0:T(8,128)(2,1)} %multiply_convert_fusion.piece_ref), custom_call_target="tpu_custom_call" | custom-call | tf_op jit(solution)/shard_map/pallas_call | solution.py:312
  195.8 1.8 fusion.48
  197.7 1.5 convolution_convert_fusion.part_ref
  199.2 21.3 %shard_map.191 = f32[32,1024]{1,0:T(8,128)} custom-call(bf16[512,1024]{1,0:T(8,128)(2,1)} %convolution_convert_fusion.part_ref), custom_call_target="tpu_custom_call" | custom-call | tf_op jit(solution)/shard_map/pallas_call | solution.py:294
  220.5 1.5 add_convert_fusion.piece_ref
  222.0 21.6 %shard_map.192 = bf16[512,1024]{1,0:T(8,128)(2,1)} custom-call(bf16[32,1024]{1,0:T(8,128)(2,1)} %add_convert_fusion.piece_ref), custom_call_target="tpu_custom_call" | custom-call | tf_op jit(solution)/shard_map/pallas_call | solution.py:312
  243.6 2.3 copy.64
  245.9 1.0 copy.65
  (57 shorter events, 3.6 us)
Async XLA Ops:
  7.2 11.3 %copy-start = (bf16[8,256,256]{2,1,0:T(8,128)(2,1)S(1)}, bf16[8,256,256]{2,1,0:T(8,128)(2,1)}, u32[]{:S(2)}) copy-start(bf16[8,256,256]{2,1,0:T(8,128)(2,1)} %param.20) | copy-start | bytes 3145732
  7.2 127.7 %all-gather.3.cloned.1.call-start = ((), (), s32[]{:S(2)}) async-start(), calls=%async_computation | async-start | bytes 1806336 | tf_op jit(solution)/shard_map/all_gather | solution.py:194
  12.0 0.7 copy-start.6
  18.5 1.8 copy-start.7
  20.9 41.3 %copy-start.9 = (s32[8]{0:T(128)S(1)}, s32[8]{0:T(128)}, u32[]{:S(2)}) copy-start(s32[8]{0:T(128)} %param.22) | copy-start | bytes 100
  20.9 41.3 %copy-start.10 = (s32[8]{0:T(128)S(1)}, s32[8]{0:T(128)}, u32[]{:S(2)}) copy-start(s32[8]{0:T(128)} %param.23) | copy-start | bytes 100
  20.9 43.7 %copy-start.11 = (s32[4608]{0:T(1024)S(1)}, s32[4608]{0:T(1024)}, u32[]{:S(2)}) copy-start(s32[4608]{0:T(1024)} %param.25) | copy-start | bytes 55300
  60.6 10.1 %copy-start.5 = (bf16[512,1024]{1,0:T(8,128)(2,1)S(1)}, bf16[512,1024]{1,0:T(8,128)(2,1)}, u32[]{:S(2)}) copy-start(bf16[512,1024]{1,0:T(8,128)(2,1)} %param.18) | copy-start | bytes 3145732
  62.2 8.8 %copy-start.8 = (f32[3,1024]{1,0:T(4,128)S(1)}, f32[3,1024]{1,0:T(4,128)}, u32[]{:S(2)}) copy-start(f32[3,1024]{1,0:T(4,128)} %param.27) | copy-start | bytes 36868
  71.0 1.9 copy-start.1
  138.1 1.7 slice-start
  139.8 1.2 slice-start.2
  143.3 1.9 copy-start.2
  148.3 24.1 %copy-start.4 = (f32[32,1024]{1,0:T(8,128)S(1)}, f32[32,1024]{1,0:T(8,128)}, u32[]{:S(2)}) copy-start(f32[32,1024]{1,0:T(8,128)} %shard_map.187) | copy-start | bytes 393220
  151.2 44.6 %copy-start.3 = (bf16[1024,352]{1,0:T(8,128)(2,1)S(1)}, bf16[1024,352]{1,0:T(8,128)(2,1)}, u32[]{:S(2)}) copy-start(bf16[1024,352]{1,0:T(8,128)(2,1)} %reshape_reshape_reshape.11) | copy-start | bytes 2162692
  174.2 23.5 %slice-start.1 = ((bf16[8,100352]{1,0:T(8,128)(2,1)}), bf16[8,22528]{1,0:T(8,128)(2,1)S(1)}, s32[]{:S(2)}) async-start(bf16[8,100352]{1,0:T(8,128)(2,1)} %reshape.177), calls=%async_computation.2 | async-start | bytes 720896 | tf_op jit(solution)/shard_map/slice | solution.py:199
Sparse Core Ops, SparseCore 0:
  12.8 62.1 all-gather.2

commit v5 on v4

--- a/solution.py
+++ b/solution.py
@@ -216,6 +216,10 @@
     pl.semaphore_wait(barrier, n_blk - 1)
 
 
+def chunk_of(b, n_blk):
+    return lax.rem(b, 2) * (n_blk // 2) + b // 2
+
+
 def scatter_kernel(n_blk, part_ref, out_ref, recv, send_sem, recv_sem):
     me = lax.axis_index("blk")
     req = lax.axis_index("req")
@@ -225,7 +229,7 @@
     for k in range(1, n_blk):
         peer = lax.rem(me + k, n_blk)
         copy = pltpu.make_async_remote_copy(
-            src_ref=part_ref.at[pl.ds(pl.multiple_of(peer * rows, rows), rows)],
+            src_ref=part_ref.at[pl.ds(pl.multiple_of(chunk_of(peer, n_blk) * rows, rows), rows)],
             dst_ref=recv.at[me],
             send_sem=send_sem.at[peer],
             recv_sem=recv_sem.at[me],
@@ -234,7 +238,8 @@
         )
         copy.start()
         copies.append(copy)
-    total = part_ref[pl.ds(pl.multiple_of(me * rows, rows), rows), :].astype(jnp.float32)
+    own = pl.ds(pl.multiple_of(chunk_of(me, n_blk) * rows, rows), rows)
+    total = part_ref[own, :].astype(jnp.float32)
     for k in range(1, n_blk):
         src = lax.rem(me + n_blk - k, n_blk)
         incoming = pltpu.make_async_remote_copy(
@@ -252,38 +257,80 @@
     out_ref[...] = total
 
 
-def gather_kernel(n_blk, piece_ref, out_ref, recv, send_sem, recv_sem):
-    me = lax.axis_index("blk")
+def gather_kernel(n_blk, piece_ref, out_ref, send_sem, recv_sem):
+    b = lax.axis_index("blk")
     req = lax.axis_index("req")
+    n_grp = n_blk // 2
+    g = b // 2
+    c = lax.rem(b, 2)
+    partner = g * 2 + 1 - c
     rows = piece_ref.shape[0]
-    greet_all(n_blk, me, req)
-    copies = []
-    for k in range(1, n_blk):
-        peer = lax.rem(me + k, n_blk)
+    half = n_grp * rows
+    barrier = pltpu.get_barrier_semaphore()
+    for k in range(1, n_grp):
+        peer = lax.rem(g + k, n_grp) * 2 + c
+        pl.semaphore_signal(barrier, inc=1, device_id=(req, peer), device_id_type=MESH_IDS)
+    pl.semaphore_signal(barrier, inc=1, device_id=(req, partner), device_id_type=MESH_IDS)
+    pl.semaphore_wait(barrier, n_grp)
+    mine = pl.ds(pl.multiple_of(c * half + g * rows, rows), rows)
+    sends = []
+    for k in range(1, n_grp):
+        peer = lax.rem(g + k, n_grp) * 2 + c
         copy = pltpu.make_async_remote_copy(
             src_ref=piece_ref,
-            dst_ref=recv.at[me],
-            send_sem=send_sem.at[peer],
-            recv_sem=recv_sem.at[me],
+            dst_ref=out_ref.at[mine],
+            send_sem=send_sem.at[k],
+            recv_sem=recv_sem.at[g],
             device_id=(req, peer),
             device_id_type=MESH_IDS,
         )
         copy.start()
-        copies.append(copy)
-    out_ref[pl.ds(pl.multiple_of(me * rows, rows), rows), :] = piece_ref[...]
-    for k in range(1, n_blk):
-        src = lax.rem(me + n_blk - k, n_blk)
+        sends.append(copy)
+    copy = pltpu.make_async_remote_copy(
+        src_ref=piece_ref,
+        dst_ref=out_ref.at[mine],
+        send_sem=send_sem.at[0],
+        recv_sem=recv_sem.at[n_grp + g],
+        device_id=(req, partner),
+        device_id_type=MESH_IDS,
+    )
+    copy.start()
+    sends.append(copy)
+    out_ref[mine, :] = piece_ref[...]
+    for k in range(1, n_grp):
+        grp = lax.rem(g + n_grp - k, n_grp)
+        there = pl.ds(pl.multiple_of(c * half + grp * rows, rows), rows)
         incoming = pltpu.make_async_remote_copy(
             src_ref=piece_ref,
-            dst_ref=recv.at[src],
-            send_sem=send_sem.at[src],
-            recv_sem=recv_sem.at[src],
-            device_id=(req, src),
+            dst_ref=out_ref.at[there],
+            send_sem=send_sem.at[0],
+            recv_sem=recv_sem.at[grp],
+            device_id=(req, grp * 2 + c),
             device_id_type=MESH_IDS,
         )
         incoming.wait_recv()
-        out_ref[pl.ds(pl.multiple_of(src * rows, rows), rows), :] = recv[src]
-    for copy in copies:
+        forward = pltpu.make_async_remote_copy(
+            src_ref=out_ref.at[there],
+            dst_ref=out_ref.at[there],
+            send_sem=send_sem.at[n_grp + k],
+            recv_sem=recv_sem.at[n_grp + grp],
+            device_id=(req, partner),
+            device_id_type=MESH_IDS,
+        )
+        forward.start()
+        sends.append(forward)
+    for grp in range(n_grp):
+        there = pl.ds(pl.multiple_of((1 - c) * half + grp * rows, rows), rows)
+        incoming = pltpu.make_async_remote_copy(
+            src_ref=piece_ref,
+            dst_ref=out_ref.at[there],
+            send_sem=send_sem.at[0],
+            recv_sem=recv_sem.at[n_grp + grp],
+            device_id=(req, partner),
+            device_id_type=MESH_IDS,
+        )
+        incoming.wait_recv()
+    for copy in sends:
         copy.wait_send()
 
 
@@ -315,7 +362,6 @@
         in_specs=[vmem],
         out_specs=vmem,
         scratch_shapes=[
-            pltpu.VMEM((n_blk, rows, piece.shape[1]), piece.dtype),
             pltpu.SemaphoreType.DMA((n_blk,)),
             pltpu.SemaphoreType.DMA((n_blk,)),
         ],
@@ -490,7 +536,7 @@
     n_blk = lax.axis_size("blk")
     rows_dev = new_states.shape[0] // n_blk
     own_rows = lax.dynamic_slice_in_dim(
-        new_states, lax.axis_index("blk") * rows_dev, rows_dev, 0
+        new_states, chunk_of(lax.axis_index("blk"), n_blk) * rows_dev, rows_dev, 0
     ).astype(jnp.float32)
     normed = rms_rows(new_states.astype(jnp.float32), norm_gain[0])
     self_cat = jnp.concatenate([wq_self, wkv_self.reshape(wkv_self.shape[0], -1)], axis=1)

time: 259 us -> 242 us (0.934)
  Pallas kernels: 183 us -> 168 us
    pallas_call x3, Pallas kernels: 64.7 us -> 51.8 us  [blk_gather(): pl.pallas_call(functools.partial(gather_kernel, n_blk), out_shape=jax.Sha...]
  transfers between devices with their start and end apart: 1 -> 1, of which waited for: 0 -> 0; matrix products, arithmetic and copies ran while one was open for 9% -> 10% of each run, Pallas kernels for 38% -> 39%
where the time goes in v5:
time: 242 us; the launch traced here: 239 us
  Pallas kernels  168 us (69%)
  local copies, waits for them, and re-layouts  26.3 us (11%)
  between operations  15.6 us (6%)
  other arithmetic  15.2 us (6%)
  matrix products  13.9 us (6%)
    pallas_call x3, Pallas kernels, blk_scatter(): pl.pallas_call(functools.partial(scatter_kernel, n_blk), out_shape=jax.Sh...  69.3 us
    pallas_call x3, Pallas kernels, blk_gather(): pl.pallas_call(functools.partial(gather_kernel, n_blk), out_shape=jax.Sha...  51.8 us
    pallas_call x1, Pallas kernels, prologue(): pl.pallas_call(functools.partial(prologue_kernel, n_req, n_blk), out_shap...  39.7 us
    unnamed x36, local copies, waits for them, and re-layouts  10.7 us
    pallas_call x1, Pallas kernels, self_attention(): pl.pallas_call(self_kernel, out_shape=jax.ShapeDtypeStruct((n_q, HD), jnp...  6.87 us
  transfers between devices with their start and end apart: 1, of which 0 were waited for; matrix products, arithmetic and copies ran while one was open for 10% of the time, Pallas kernels for 39%

profile of v5, /device:TPU:33, one launch (start us, length us, event | category | flops | bytes accessed | tf_op | source)
XLA Modules:
  0.0 238.8 jit_solution(1242480434303046409)
XLA Ops:
  7.2 0.9 copy.36
  8.2 0.9 copy.37
  9.2 1.0 copy.38
  10.5 0.7 bitcast_dynamic-update-slice_fusion.1
  11.2 0.8 bitcast_dynamic-update-slice_fusion
  12.0 0.7 copy-done.6
  12.7 0.7 compare_and_fusion
  13.4 1.2 dynamic_slice.13
  14.6 1.9 compare_select_fusion
  16.5 0.8 copy.33
  17.5 0.9 copy.34
  19.1 1.1 broadcast_select_fusion.ordered_ref
  20.2 0.6 maximum_bitcast_fusion.packed_ref
  20.9 39.7 %shard_map.185 = (bf16[4096,128]{1,0:T(8,128)(2,1)}, bf16[8,256,128]{2,1,0:T(8,128)(2,1)}) custom-call(bf16[8,256,256]{2,1,0:T(8,128)(2,1)} %broadcast_select_fusion.ordered_ref, bf16[256,128]{1,0:T(8,128)(2,1)} %maximum_bitcast_fusion.packed_ref), custom_call_target="tpu_custom_call" | custom-call | tf_op jit(solution)/shard_map/pallas_call | solution.py:461
  60.6 1.5 copy.57
  62.2 1.2 select_reduce_fusion.1
  64.6 1.0 convolution_reduce_fusion
  66.1 0.6 concatenate.14
  66.7 0.7 pad_slice_fusion
  67.7 0.8 reshape_reshape_reshape.9
  68.5 1.0 reshape_reshape.6
  69.5 1.3 pad_add_fusion.lens_ref
  71.1 1.7 convolution_convert_fusion.3
  72.9 6.9 %shard_map.186 = bf16[512,64]{1,0:T(8,128)(2,1)S(1)} custom-call(s32[2]{0:T(128)S(1)} %pad_add_fusion.lens_ref, bf16[512,64]{1,0:T(8,128)(2,1)S(1)} %get-tuple-element.14.q_ref, bf16[4096,128]{1,0:T(8,128)(2,1)S(1)} %copy-done.1, bf16[512,64]{1,0:T(8,128)(2,1)S(1)} %get-tuple-element.13.kn_ref, bf16[512,64]{1,0:T(8,128)(2,1)S(1)} %get-tuple-element.12.vn_ref, ...), custom_call_target="tpu_custom_call" | custom-call | tf_op jit(solution)/shard_map/pallas_call | solution.py:183
  79.8 1.4 convolution_convert_fusion.2.part_ref
  81.2 28.9 %shard_map.187 = f32[32,1024]{1,0:T(8,128)} custom-call(bf16[512,1024]{1,0:T(8,128)(2,1)} %convolution_convert_fusion.2.part_ref), custom_call_target="tpu_custom_call" | custom-call | tf_op jit(solution)/shard_map/pallas_call | solution.py:341
  110.0 1.0 multiply_reduce_fusion.1
  111.1 1.6 multiply_convert_fusion.1.piece_ref
  112.7 17.2 %shard_map.188 = bf16[512,1024]{1,0:T(8,128)(2,1)} custom-call(bf16[32,1024]{1,0:T(8,128)(2,1)} %multiply_convert_fusion.1.piece_ref), custom_call_target="tpu_custom_call" | custom-call | tf_op jit(solution)/shard_map/pallas_call | solution.py:359
  130.6 3.3 %reshape.177 = bf16[8,100352]{1,0:T(8,128)(2,1)} reshape(bf16[802816]{0:T(1024)(128)(2,1)} %all-gather.3.cloned.1.call-done) | data formatting | bytes 3211264 | tf_op jit(solution)/shard_map/all_gather | solution.py:194
  133.8 1.7 fusion.43
  135.5 0.8 reshape_reshape_reshape.10
  136.7 2.3 reshape_reshape_reshape.11
  139.0 1.9 convolution_convert_fusion.4
  140.9 1.7 fusion.47
  142.6 1.4 fusion.7
  144.0 2.9 %convolution_convert_fusion.1.part_ref = bf16[512,1024]{1,0:T(8,128)(2,1)} fusion(f32[512,512]{0,1:T(8,128)} %get-tuple-element.19, f32[512]{0:T(512)S(1)} %fusion.7, f32[512]{0:T(512)S(1)} %get-tuple-element.18, bf16[8,8,8,128]{3,2,1,0:T(8,128)(2,1)} %bitcast.78, bf16[1,512,2,1,64]{1,4,2,3,0:T(8,128)(2,1)S(1)} %bitcast.77), kind=kOutput, calls=%fused_computation.7 | convolution fusion | flops 102006784 | bytes 2297856 | tf_op jit(solution)/shard_map/dot_general | solution.py:570
  146.9 20.3 %shard_map.189 = f32[32,1024]{1,0:T(8,128)} custom-call(bf16[512,1024]{1,0:T(8,128)(2,1)} %convolution_convert_fusion.1.part_ref), custom_call_target="tpu_custom_call" | custom-call | tf_op jit(solution)/shard_map/pallas_call | solution.py:341
  167.2 1.0 multiply_reduce_fusion
  168.3 0.7 multiply_convert_fusion.piece_ref
  169.0 17.3 %shard_map.190 = bf16[512,1024]{1,0:T(8,128)(2,1)} custom-call(bf16[32,1024]{1,0:T(8,128)(2,1)} %multiply_convert_fusion.piece_ref), custom_call_target="tpu_custom_call" | custom-call | tf_op jit(solution)/shard_map/pallas_call | solution.py:359
  186.4 1.8 fusion.48
  188.2 1.5 convolution_convert_fusion.part_ref
  189.7 20.2 %shard_map.191 = f32[32,1024]{1,0:T(8,128)} custom-call(bf16[512,1024]{1,0:T(8,128)(2,1)} %convolution_convert_fusion.part_ref), custom_call_target="tpu_custom_call" | custom-call | tf_op jit(solution)/shard_map/pallas_call | solution.py:341
  209.9 1.5 add_convert_fusion.piece_ref
  211.4 17.3 %shard_map.192 = bf16[512,1024]{1,0:T(8,128)(2,1)} custom-call(bf16[32,1024]{1,0:T(8,128)(2,1)} %add_convert_fusion.piece_ref), custom_call_target="tpu_custom_call" | custom-call | tf_op jit(solution)/shard_map/pallas_call | solution.py:359
  228.7 2.3 copy.64
  231.0 1.0 copy.65
  (57 shorter events, 3.6 us)
Async XLA Ops:
  7.2 11.3 %copy-start = (bf16[8,256,256]{2,1,0:T(8,128)(2,1)S(1)}, bf16[8,256,256]{2,1,0:T(8,128)(2,1)}, u32[]{:S(2)}) copy-start(bf16[8,256,256]{2,1,0:T(8,128)(2,1)} %param.20) | copy-start | bytes 3145732
  7.2 123.4 %all-gather.3.cloned.1.call-start = ((), (), s32[]{:S(2)}) async-start(), calls=%async_computation | async-start | bytes 1806336 | tf_op jit(solution)/shard_map/all_gather | solution.py:194
  12.0 0.7 copy-start.6
  18.5 1.8 copy-start.7
  20.9 41.3 %copy-start.9 = (s32[8]{0:T(128)S(1)}, s32[8]{0:T(128)}, u32[]{:S(2)}) copy-start(s32[8]{0:T(128)} %param.22) | copy-start | bytes 100
  20.9 41.4 %copy-start.10 = (s32[8]{0:T(128)S(1)}, s32[8]{0:T(128)}, u32[]{:S(2)}) copy-start(s32[8]{0:T(128)} %param.23) | copy-start | bytes 100
  20.9 43.7 %copy-start.11 = (s32[4608]{0:T(1024)S(1)}, s32[4608]{0:T(1024)}, u32[]{:S(2)}) copy-start(s32[4608]{0:T(1024)} %param.25) | copy-start | bytes 55300
  60.6 10.1 %copy-start.5 = (bf16[512,1024]{1,0:T(8,128)(2,1)S(1)}, bf16[512,1024]{1,0:T(8,128)(2,1)}, u32[]{:S(2)}) copy-start(bf16[512,1024]{1,0:T(8,128)(2,1)} %param.18) | copy-start | bytes 3145732
  62.2 8.9 %copy-start.8 = (f32[3,1024]{1,0:T(4,128)S(1)}, f32[3,1024]{1,0:T(4,128)}, u32[]{:S(2)}) copy-start(f32[3,1024]{1,0:T(4,128)} %param.27) | copy-start | bytes 36868
  71.0 1.9 copy-start.1
  133.8 1.7 slice-start
  135.5 1.2 slice-start.2
  139.0 1.9 copy-start.2
  144.0 23.2 %copy-start.4 = (f32[32,1024]{1,0:T(8,128)S(1)}, f32[32,1024]{1,0:T(8,128)}, u32[]{:S(2)}) copy-start(f32[32,1024]{1,0:T(8,128)} %shard_map.187) | copy-start | bytes 393220
  146.9 39.4 %copy-start.3 = (bf16[1024,352]{1,0:T(8,128)(2,1)S(1)}, bf16[1024,352]{1,0:T(8,128)(2,1)}, u32[]{:S(2)}) copy-start(bf16[1024,352]{1,0:T(8,128)(2,1)} %reshape_reshape_reshape.11) | copy-start | bytes 2162692
  169.0 19.2 %slice-start.1 = ((bf16[8,100352]{1,0:T(8,128)(2,1)}), bf16[8,22528]{1,0:T(8,128)(2,1)S(1)}, s32[]{:S(2)}) async-start(bf16[8,100352]{1,0:T(8,128)(2,1)} %reshape.177), calls=%async_computation.2 | async-start | bytes 720896 | tf_op jit(solution)/shard_map/slice | solution.py:199
Sparse Core Ops, SparseCore 0:
  12.8 62.1 all-gather.2

commit v6 on v5

--- a/solution.py
+++ b/solution.py
@@ -123,6 +123,136 @@
 
 
 TQ = 128
+
+
+def stage_kernel(n_blk, final, part_ref, resid_ref, gain_ref, res_out, full_ref, recv, rs_send, rs_recv, ag_send, ag_recv):
+    me = lax.axis_index("blk")
+    req = lax.axis_index("req")
+    rows = resid_ref.shape[0]
+    n_grp = n_blk // 2
+    g = me // 2
+    c = lax.rem(me, 2)
+    partner = g * 2 + 1 - c
+    half = n_grp * rows
+    greet_all(n_blk, me, req)
+    sends = []
+    for k in range(1, n_blk):
+        peer = lax.rem(me + k, n_blk)
+        copy = pltpu.make_async_remote_copy(
+            src_ref=part_ref.at[pl.ds(pl.multiple_of(chunk_of(peer, n_blk) * rows, rows), rows)],
+            dst_ref=recv.at[me],
+            send_sem=rs_send.at[peer],
+            recv_sem=rs_recv.at[me],
+            device_id=(req, peer),
+            device_id_type=MESH_IDS,
+        )
+        copy.start()
+        sends.append(copy)
+    mine = pl.ds(pl.multiple_of(c * half + g * rows, rows), rows)
+    total = part_ref[mine, :].astype(jnp.float32)
+    for k in range(1, n_blk):
+        src = lax.rem(me + n_blk - k, n_blk)
+        incoming = pltpu.make_async_remote_copy(
+            src_ref=part_ref.at[pl.ds(0, rows)],
+            dst_ref=recv.at[src],
+            send_sem=rs_send.at[src],
+            recv_sem=rs_recv.at[src],
+            device_id=(req, src),
+            device_id_type=MESH_IDS,
+        )
+        incoming.wait_recv()
+        total = total + recv[src].astype(jnp.float32)
+    resid = resid_ref[...] + total
+    res_out[...] = resid
+    if final:
+        full_ref[mine, :] = resid.astype(full_ref.dtype)
+    else:
+        mean_square = jnp.mean(resid * resid, axis=-1, keepdims=True)
+        full_ref[mine, :] = (resid * lax.rsqrt(mean_square + EPSILON) * gain_ref[...]).astype(
+            full_ref.dtype
+        )
+    for k in range(1, n_grp):
+        peer = lax.rem(g + k, n_grp) * 2 + c
+        copy = pltpu.make_async_remote_copy(
+            src_ref=full_ref.at[mine],
+            dst_ref=full_ref.at[mine],
+            send_sem=ag_send.at[k],
+            recv_sem=ag_recv.at[g],
+            device_id=(req, peer),
+            device_id_type=MESH_IDS,
+        )
+        copy.start()
+        sends.append(copy)
+    copy = pltpu.make_async_remote_copy(
+        src_ref=full_ref.at[mine],
+        dst_ref=full_ref.at[mine],
+        send_sem=ag_send.at[0],
+        recv_sem=ag_recv.at[n_grp + g],
+        device_id=(req, partner),
+        device_id_type=MESH_IDS,
+    )
+    copy.start()
+    sends.append(copy)
+    for k in range(1, n_grp):
+        grp = lax.rem(g + n_grp - k, n_grp)
+        there = pl.ds(pl.multiple_of(c * half + grp * rows, rows), rows)
+        incoming = pltpu.make_async_remote_copy(
+            src_ref=full_ref.at[there],
+            dst_ref=full_ref.at[there],
+            send_sem=ag_send.at[0],
+            recv_sem=ag_recv.at[grp],
+            device_id=(req, grp * 2 + c),
+            device_id_type=MESH_IDS,
+        )
+        incoming.wait_recv()
+        forward = pltpu.make_async_remote_copy(
+            src_ref=full_ref.at[there],
+            dst_ref=full_ref.at[there],
+            send_sem=ag_send.at[n_grp + k],
+            recv_sem=ag_recv.at[n_grp + grp],
+            device_id=(req, partner),
+            device_id_type=MESH_IDS,
+        )
+        forward.start()
+        sends.append(forward)
+    for grp in range(n_grp):
+        there = pl.ds(pl.multiple_of((1 - c) * half + grp * rows, rows), rows)
+        incoming = pltpu.make_async_remote_copy(
+            src_ref=full_ref.at[there],
+            dst_ref=full_ref.at[there],
+            send_sem=ag_send.at[0],
+            recv_sem=ag_recv.at[n_grp + grp],
+            device_id=(req, partner),
+            device_id_type=MESH_IDS,
+        )
+        incoming.wait_recv()
+    for copy in sends:
+        copy.wait_send()
+
+
+def blk_stage(part, resid, gain, final):
+    n_blk = lax.axis_size("blk")
+    rows, width = resid.shape
+    vmem = pl.BlockSpec(memory_space=pltpu.VMEM)
+    return pl.pallas_call(
+        functools.partial(stage_kernel, n_blk, final),
+        out_shape=(
+            jax.ShapeDtypeStruct((rows, width), jnp.float32),
+            jax.ShapeDtypeStruct((rows * n_blk, width), jnp.bfloat16),
+        ),
+        in_specs=[vmem] * 3,
+        out_specs=(vmem, vmem),
+        scratch_shapes=[
+            pltpu.VMEM((n_blk, rows, width), part.dtype),
+            pltpu.SemaphoreType.DMA((n_blk,)),
+            pltpu.SemaphoreType.DMA((n_blk,)),
+            pltpu.SemaphoreType.DMA((n_blk,)),
+            pltpu.SemaphoreType.DMA((n_blk,)),
+        ],
+        compiler_params=pltpu.CompilerParams(
+            collective_id=4 if final else 3, has_side_effects=True
+        ),
+    )(part, resid, gain[None, :])
 
 
 def self_kernel(lens_ref, q_ref, c_ref, kn_ref, vn_ref, g_ref, f_ref, o_ref):
@@ -553,8 +683,7 @@
         slot_new[0],
     )
     part = jnp.dot(context, wo_self, preferred_element_type=jnp.float32).astype(jnp.bfloat16)
-    residual = own_rows + blk_scatter(part)
-    normed = blk_gather(rms_rows(residual, norm_gain[1]))
+    residual, normed = blk_stage(part, own_rows, norm_gain[1], False)
     queries = (
         jnp.dot(normed, wq_cross, preferred_element_type=jnp.float32)
         .astype(jnp.bfloat16)
@@ -568,15 +697,14 @@
     )
     context = cross_attend(queries, key_value, slot_enc)
     part = jnp.dot(context.reshape(-1, width_dev), wo_cross, preferred_element_type=jnp.float32)
-    residual = residual + blk_scatter(part.astype(jnp.bfloat16))
-    normed = blk_gather(rms_rows(residual, norm_gain[2]))
+    residual, normed = blk_stage(part.astype(jnp.bfloat16), residual, norm_gain[2], False)
     ff_dev = w_in.shape[2]
     gate_up = jnp.dot(normed, w_in.reshape(w_in.shape[0], -1), preferred_element_type=jnp.float32)
     hidden = (jax.nn.gelu(gate_up[:, :ff_dev], approximate=True) * gate_up[:, ff_dev:]).astype(
         jnp.bfloat16
     )
     part = jnp.dot(hidden, w_out, preferred_element_type=jnp.float32).astype(jnp.bfloat16)
-    layer_out = blk_gather((residual + blk_scatter(part)).astype(jnp.bfloat16))
+    _, layer_out = blk_stage(part, residual, norm_gain[2], True)
     return (layer_out, cache_dec)
 
 

time: 242 us -> 220 us (0.909)
  the two profiles are of different devices: /device:TPU:33 before, /device:TPU:37 now
where the time goes in v6:
time: 220 us; the launch traced here: 219 us
  Pallas kernels  157 us (71%)
  local copies, waits for them, and re-layouts  24.6 us (11%)
  between operations  15.8 us (7%)
  matrix products  14.1 us (6%)
  other arithmetic  7.51 us (3%)
    pallas_call x3, Pallas kernels, blk_stage(): pl.pallas_call(functools.partial(stage_kernel, n_blk, final), out_shape=(...  103 us
    pallas_call x1, Pallas kernels, prologue(): pl.pallas_call(functools.partial(prologue_kernel, n_req, n_blk), out_shap...  46.6 us
    unnamed x38, local copies, waits for them, and re-layouts  9.21 us
    pallas_call x1, Pallas kernels, self_attention(): pl.pallas_call(self_kernel, out_shape=jax.ShapeDtypeStruct((n_q, HD), jnp...  6.87 us
  transfers between devices with their start and end apart: 1, of which 0 were waited for; matrix products, arithmetic and copies ran while one was open for 9% of the time, Pallas kernels for 42%

profile of v6, /device:TPU:37, one launch (start us, length us, event | category | flops | bytes accessed | tf_op | source)
XLA Modules:
  0.0 218.7 jit_solution(16734248991687918679)
XLA Ops:
  7.3 0.9 copy.33
  8.3 0.9 copy.34
  9.3 1.0 copy.35
  10.3 0.2 reshape.135
  10.5 0.7 bitcast_dynamic-update-slice_fusion.1
  11.3 0.8 bitcast_dynamic-update-slice_fusion
  12.1 0.7 copy-done.4
  12.8 1.0 convolution_reduce_fusion
  13.8 0.5 slice.95
  14.3 0.6 pad_slice_fusion
  15.0 0.7 concatenate.15
  15.7 0.6 dynamic_slice.12
  16.3 1.3 compare_select_fusion
  17.6 1.4 select_reduce_fusion.1
  20.6 0.1 copy.36
  20.8 0.1 copy.37
  21.1 0.6 gather_fusion
  21.7 1.1 broadcast_select_fusion.ordered_ref
  22.9 0.6 maximum_bitcast_fusion.packed_ref
  23.5 46.6 %shard_map.185 = (bf16[4096,128]{1,0:T(8,128)(2,1)}, bf16[8,256,128]{2,1,0:T(8,128)(2,1)}) custom-call(bf16[8,256,256]{2,1,0:T(8,128)(2,1)} %broadcast_select_fusion.ordered_ref, bf16[256,128]{1,0:T(8,128)(2,1)} %maximum_bitcast_fusion.packed_ref), custom_call_target="tpu_custom_call" | custom-call | tf_op jit(solution)/shard_map/pallas_call | solution.py:591
  70.1 1.5 copy.57
  71.7 0.8 reshape_reshape_reshape.10
  72.5 1.0 reshape_reshape.6
  73.5 1.3 pad_add_fusion.lens_ref
  74.8 0.3 fusion
  75.1 0.6 fusion.44
  75.7 1.7 convolution_convert_fusion.3
  77.6 6.9 %shard_map.186 = bf16[512,64]{1,0:T(8,128)(2,1)S(1)} custom-call(s32[2]{0:T(128)S(1)} %pad_add_fusion.lens_ref, bf16[512,64]{1,0:T(8,128)(2,1)S(1)} %get-tuple-element.22.q_ref, bf16[4096,128]{1,0:T(8,128)(2,1)S(1)} %copy-done.1, bf16[512,64]{1,0:T(8,128)(2,1)S(1)} %get-tuple-element.21.kn_ref, bf16[512,64]{1,0:T(8,128)(2,1)S(1)} %get-tuple-element.20.vn_ref, ...), custom_call_target="tpu_custom_call" | custom-call | tf_op jit(solution)/shard_map/pallas_call | solution.py:313
  84.4 0.7 dynamic-slice_convert_fusion.resid_ref
  85.1 1.4 convolution_convert_fusion.2.part_ref
  86.5 38.7 %shard_map.187 = (f32[32,1024]{1,0:T(8,128)}, bf16[512,1024]{1,0:T(8,128)(2,1)}) custom-call(bf16[512,1024]{1,0:T(8,128)(2,1)} %convolution_convert_fusion.2.part_ref, f32[32,1024]{1,0:T(8,128)} %dynamic-slice_convert_fusion.resid_ref, f32[1,1024]{1,0:T(1,128)} %get-tuple-element.25.gain_ref), custom_call_target="tpu_custom_call" | custom-call | tf_op jit(solution)/shard_map/pallas_call | solution.py:237
  125.2 0.6 iota_compare_fusion.2
  125.9 3.3 %reshape.161 = bf16[8,100352]{1,0:T(8,128)(2,1)} reshape(bf16[802816]{0:T(1024)(128)(2,1)} %all-gather.3.cloned.1.call-done) | data formatting | bytes 3211264 | tf_op jit(solution)/shard_map/all_gather | solution.py:324
  129.1 1.7 fusion.41
  130.8 0.8 reshape_reshape_reshape.9
  131.6 0.2 reshape_reshape.7
  131.9 0.1 slice-done.2
  132.0 2.1 reshape_reshape_reshape.11
  134.1 1.9 convolution_convert_fusion.4
  136.0 2.0 fusion.45
  137.9 0.2 fusion.7
  138.1 2.6 %convolution_convert_fusion.1.part_ref = bf16[512,1024]{1,0:T(8,128)(2,1)} fusion(f32[512,512]{0,1:T(8,128)S(1)} %get-tuple-element.27, f32[512]{0:T(512)S(1)} %fusion.7, f32[512]{0:T(512)S(1)} %get-tuple-element.26, bf16[8,8,8,128]{3,2,1,0:T(8,128)(2,1)} %bitcast.76, bf16[1,512,2,1,64]{1,4,2,3,0:T(8,128)(2,1)S(1)} %bitcast.75), kind=kOutput, calls=%fused_computation.7 | convolution fusion | flops 102006784 | bytes 2297856 | tf_op jit(solution)/shard_map/dot_general | solution.py:699
  140.7 32.8 %shard_map.188 = (f32[32,1024]{1,0:T(8,128)}, bf16[512,1024]{1,0:T(8,128)(2,1)}) custom-call(bf16[512,1024]{1,0:T(8,128)(2,1)} %convolution_convert_fusion.1.part_ref, f32[32,1024]{1,0:T(8,128)} %get-tuple-element.12.resid_ref, f32[1,1024]{1,0:T(1,128)} %get-tuple-element.23.gain_ref), custom_call_target="tpu_custom_call" | custom-call | tf_op jit(solution)/shard_map/pallas_call | solution.py:237
  173.5 2.0 fusion.46
  175.5 1.5 convolution_convert_fusion.part_ref
  177.0 31.5 %shard_map.189 = (f32[32,1024]{1,0:T(8,128)}, bf16[512,1024]{1,0:T(8,128)(2,1)}) custom-call(bf16[512,1024]{1,0:T(8,128)(2,1)} %convolution_convert_fusion.part_ref, f32[32,1024]{1,0:T(8,128)} %get-tuple-element.14.resid_ref, f32[1,1024]{1,0:T(1,128)} %get-tuple-element.23.gain_ref), custom_call_target="tpu_custom_call" | custom-call | tf_op jit(solution)/shard_map/pallas_call | solution.py:237
  208.6 2.3 %copy.64 = bf16[512,1024]{1,0:T(8,128)(2,1)} copy(bf16[512,1024]{1,0:T(8,128)(2,1)} %get-tuple-element.34) | data formatting | bytes 2097152
  210.8 1.0 copy.65
  (50 shorter events, 1.0 us)
Async XLA Ops:
  7.2 13.9 %copy-start = (bf16[8,256,256]{2,1,0:T(8,128)(2,1)S(1)}, bf16[8,256,256]{2,1,0:T(8,128)(2,1)}, u32[]{:S(2)}) copy-start(bf16[8,256,256]{2,1,0:T(8,128)(2,1)} %param.20) | copy-start | bytes 3145732
  7.2 8.5 %copy-start.9 = (s32[8]{0:T(128)S(1)}, s32[8]{0:T(128)}, u32[]{:S(2)}) copy-start(s32[8]{0:T(128)} %param.21) | copy-start | bytes 100
  7.2 9.1 %copy-start.10 = (s32[8]{0:T(128)S(1)}, s32[8]{0:T(128)}, u32[]{:S(2)}) copy-start(s32[8]{0:T(128)} %param.22) | copy-start | bytes 100
  7.2 10.4 %copy-start.12 = (s32[8]{0:T(128)S(1)}, s32[8]{0:T(128)}, u32[]{:S(2)}) copy-start(s32[8]{0:T(128)} %param.24) | copy-start | bytes 100
  7.2 10.4 %copy-start.11 = (s32[8]{0:T(128)S(1)}, s32[8]{0:T(128)}, u32[]{:S(2)}) copy-start(s32[8]{0:T(128)} %param.23) | copy-start | bytes 100
  7.2 13.4 %copy-start.6 = (bf16[128,64]{0,1:T(8,128)(2,1)S(1)}, bf16[128,64]{0,1:T(8,128)(2,1)}, u32[]{:S(2)}) copy-start(bf16[128,64]{0,1:T(8,128)(2,1)} %param.28) | copy-start | bytes 49156
  7.2 13.6 %copy-start.5 = (bf16[128,2,64]{0,2,1:T(8,128)(2,1)S(1)}, bf16[128,2,64]{0,2,1:T(8,128)(2,1)}, u32[]{:S(2)}) copy-start(bf16[128,2,64]{0,2,1:T(8,128)(2,1)} %param.29) | copy-start | bytes 98308
  7.2 118.6 %all-gather.3.cloned.1.call-start = ((), (), s32[]{:S(2)}) async-start(), calls=%async_computation | async-start | bytes 1806336 | tf_op jit(solution)/shard_map/all_gather | solution.py:324
  12.1 0.7 copy-start.4
  21.1 1.8 copy-start.7
  70.1 4.7 %copy-start.2 = (bf16[512,1024]{1,0:T(8,128)(2,1)S(1)}, bf16[512,1024]{1,0:T(8,128)(2,1)}, u32[]{:S(2)}) copy-start(bf16[512,1024]{1,0:T(8,128)(2,1)} %param.18) | copy-start | bytes 3145732
  71.6 3.5 %copy-start.8 = (f32[3,1024]{1,0:T(4,128)S(1)}, f32[3,1024]{1,0:T(4,128)}, u32[]{:S(2)}) copy-start(f32[3,1024]{1,0:T(4,128)} %param.27) | copy-start | bytes 36868
  75.7 1.9 copy-start.1
  129.1 1.7 slice-start
  130.8 1.2 slice-start.2
  131.6 2.4 %copy-start.3 = (bf16[1024,128]{1,0:T(8,128)(2,1)S(1)}, bf16[1024,128]{1,0:T(8,128)(2,1)}, u32[]{:S(2)}) copy-start(bf16[1024,128]{1,0:T(8,128)(2,1)} %reshape_reshape_reshape.9) | copy-start | bytes 786436
  140.7 34.8 %slice-start.1 = ((bf16[8,100352]{1,0:T(8,128)(2,1)}), bf16[8,22528]{1,0:T(8,128)(2,1)S(1)}, s32[]{:S(2)}) async-start(bf16[8,100352]{1,0:T(8,128)(2,1)} %reshape.161), calls=%async_computation.2 | async-start | bytes 720896 | tf_op jit(solution)/shard_map/slice | solution.py:329
Sparse Core Ops, SparseCore 0:
  12.9 68.0 all-gather.2

commit v7 on v6

--- a/solution.py
+++ b/solution.py
@@ -125,7 +125,13 @@
 TQ = 128
 
 
-def stage_kernel(n_blk, final, part_ref, resid_ref, gain_ref, res_out, full_ref, recv, rs_send, rs_recv, ag_send, ag_recv):
+def stage_kernel(n_blk, final, extra, *refs):
+    if extra:
+        (part_ref, resid_ref, gain_ref, packed_ref, res_out, full_ref, wts_ref,
+         recv, rs_send, rs_recv, ag_send, ag_recv, w_send, w_recv) = refs
+    else:
+        (part_ref, resid_ref, gain_ref, res_out, full_ref,
+         recv, rs_send, rs_recv, ag_send, ag_recv) = refs
     me = lax.axis_index("blk")
     req = lax.axis_index("req")
     rows = resid_ref.shape[0]
@@ -134,8 +140,29 @@
     c = lax.rem(me, 2)
     partner = g * 2 + 1 - c
     half = n_grp * rows
-    greet_all(n_blk, me, req)
+    barrier = pltpu.get_barrier_semaphore()
+    for k in range(1, n_blk):
+        peer = lax.rem(me + k, n_blk)
+        pl.semaphore_signal(barrier, inc=1, device_id=(req, peer), device_id_type=MESH_IDS)
+    n_req = wts_ref.shape[0] if extra else 1
+    for k in range(1, n_req):
+        peer = lax.rem(req + k, n_req)
+        pl.semaphore_signal(barrier, inc=1, device_id=(peer, me), device_id_type=MESH_IDS)
+    pl.semaphore_wait(barrier, n_blk - 1 + n_req - 1)
     sends = []
+    w_sends = []
+    for k in range(1, n_req):
+        peer = lax.rem(req + k, n_req)
+        copy = pltpu.make_async_remote_copy(
+            src_ref=packed_ref,
+            dst_ref=wts_ref.at[req],
+            send_sem=w_send.at[peer],
+            recv_sem=w_recv.at[req],
+            device_id=(peer, me),
+            device_id_type=MESH_IDS,
+        )
+        copy.start()
+        w_sends.append(copy)
     for k in range(1, n_blk):
         peer = lax.rem(me + k, n_blk)
         copy = pltpu.make_async_remote_copy(
@@ -226,33 +253,55 @@
             device_id_type=MESH_IDS,
         )
         incoming.wait_recv()
-    for copy in sends:
+    if extra:
+        wts_ref[req] = packed_ref[...]
+        for k in range(1, n_req):
+            src = lax.rem(req + n_req - k, n_req)
+            incoming = pltpu.make_async_remote_copy(
+                src_ref=packed_ref,
+                dst_ref=wts_ref.at[src],
+                send_sem=w_send.at[src],
+                recv_sem=w_recv.at[src],
+                device_id=(src, me),
+                device_id_type=MESH_IDS,
+            )
+            incoming.wait_recv()
+    for copy in sends + w_sends:
         copy.wait_send()
 
 
-def blk_stage(part, resid, gain, final):
+def blk_stage(part, resid, gain, final, packed=None):
     n_blk = lax.axis_size("blk")
     rows, width = resid.shape
     vmem = pl.BlockSpec(memory_space=pltpu.VMEM)
+    extra = packed is not None
+    outs = [
+        jax.ShapeDtypeStruct((rows, width), jnp.float32),
+        jax.ShapeDtypeStruct((rows * n_blk, width), jnp.bfloat16),
+    ]
+    scratch = [
+        pltpu.VMEM((n_blk, rows, width), part.dtype),
+        pltpu.SemaphoreType.DMA((n_blk,)),
+        pltpu.SemaphoreType.DMA((n_blk,)),
+        pltpu.SemaphoreType.DMA((n_blk,)),
+        pltpu.SemaphoreType.DMA((n_blk,)),
+    ]
+    args = [part, resid, gain[None, :]]
+    if extra:
+        n_req = lax.axis_size("req")
+        outs.append(jax.ShapeDtypeStruct((n_req,) + packed.shape, packed.dtype))
+        scratch += [pltpu.SemaphoreType.DMA((n_req,)), pltpu.SemaphoreType.DMA((n_req,))]
+        args.append(packed)
     return pl.pallas_call(
-        functools.partial(stage_kernel, n_blk, final),
-        out_shape=(
-            jax.ShapeDtypeStruct((rows, width), jnp.float32),
-            jax.ShapeDtypeStruct((rows * n_blk, width), jnp.bfloat16),
+        functools.partial(stage_kernel, n_blk, final, extra),
+        out_shape=tuple(outs),
+        in_specs=[vmem] * len(args),
+        out_specs=tuple([vmem] * len(outs)),
+        scratch_shapes=scratch,
+        compiler_params=pltpu.CompilerParams(
+            collective_id=5 if extra else (4 if final else 3), has_side_effects=True
         ),
-        in_specs=[vmem] * 3,
-        out_specs=(vmem, vmem),
-        scratch_shapes=[
-            pltpu.VMEM((n_blk, rows, width), part.dtype),
-            pltpu.SemaphoreType.DMA((n_blk,)),
-            pltpu.SemaphoreType.DMA((n_blk,)),
-            pltpu.SemaphoreType.DMA((n_blk,)),
-            pltpu.SemaphoreType.DMA((n_blk,)),
-        ],
-        compiler_params=pltpu.CompilerParams(
-            collective_id=4 if final else 3, has_side_effects=True
-        ),
-    )(part, resid, gain[None, :])
+    )(*args)
 
 
 def self_kernel(lens_ref, q_ref, c_ref, kn_ref, vn_ref, g_ref, f_ref, o_ref):
@@ -661,8 +710,9 @@
     flat = jnp.concatenate([w.reshape(-1) for w, _ in early])
     cache_blk, whole = prologue(ordered, flat.reshape(-1, 128))
     cache_dec = cache_blk[None]
-    gathered = unpack(whole, early) + pack_gather(late)
-    wq_self, wkv_self, wo_self, wq_cross, wkv_cross, wo_cross, w_in, w_out = gathered
+    late_flat = jnp.concatenate([w.reshape(-1) for w, _ in late]).reshape(-1, 128)
+    gathered = unpack(whole, early)
+    wq_self, wkv_self, wo_self = gathered
     n_blk = lax.axis_size("blk")
     rows_dev = new_states.shape[0] // n_blk
     own_rows = lax.dynamic_slice_in_dim(
@@ -683,7 +733,8 @@
         slot_new[0],
     )
     part = jnp.dot(context, wo_self, preferred_element_type=jnp.float32).astype(jnp.bfloat16)
-    residual, normed = blk_stage(part, own_rows, norm_gain[1], False)
+    residual, normed, late_whole = blk_stage(part, own_rows, norm_gain[1], False, late_flat)
+    wq_cross, wkv_cross, wo_cross, w_in, w_out = unpack(late_whole, late)
     queries = (
         jnp.dot(normed, wq_cross, preferred_element_type=jnp.float32)
         .astype(jnp.bfloat16)

time: 220 us -> 219 us (level)
  the two profiles are of different devices: /device:TPU:37 before, /device:TPU:33 now
where the time goes in v7:
time: 219 us; the launch traced here: 216 us
  Pallas kernels  165 us (75%)
  local copies, waits for them, and re-layouts  24.5 us (11%)
  matrix products  13.4 us (6%)
  other arithmetic  10.7 us (5%)
  between operations  2.35 us (1%)
    pallas_call x3, Pallas kernels, blk_stage(): pl.pallas_call(functools.partial(stage_kernel, n_blk, final, extra), out_...  126 us
    pallas_call x1, Pallas kernels, prologue(): pl.pallas_call(functools.partial(prologue_kernel, n_req, n_blk), out_shap...  31.6 us
    unnamed x41, local copies, waits for them, and re-layouts  8.39 us
    pallas_call x1, Pallas kernels, self_attention(): pl.pallas_call(self_kernel, out_shape=jax.ShapeDtypeStruct((n_q, HD), jnp...  6.85 us
    slice x6, local copies, waits for them, and re-layouts, unpack(): part = whole[:, at:at + size].reshape((n_req,) + w.shape)  4.72 us

profile of v7, /device:TPU:33, one launch (start us, length us, event | category | flops | bytes accessed | tf_op | source)
XLA Modules:
  0.0 215.6 jit_solution(14820962045660141796)
XLA Ops:
  0.8 1.4 dynamic_slice.12
  2.1 0.7 compare_and_fusion
  2.8 2.0 select_reduce_fusion.1
  6.0 1.3 pad_add_fusion.lens_ref
  7.4 2.0 compare_select_fusion
  9.3 0.6 iota_compare_fusion.2
  10.0 1.5 fusion
  11.5 1.4 fusion.44
  12.9 1.0 convolution_reduce_fusion
  14.0 0.5 slice.93
  14.5 0.6 pad_slice_fusion
  15.2 0.6 concatenate.14
  16.1 0.1 copy.27
  16.3 0.1 copy.30
  16.5 0.1 copy.28
  16.8 0.6 maximum_bitcast_fusion.packed_ref
  17.4 0.1 copy.31
  17.7 0.7 dynamic-slice_convert_fusion.refs_1_
  18.3 0.1 copy.32
  18.5 0.2 reshape.149
  18.8 0.6 gather_fusion
  19.4 1.1 broadcast_select_fusion.ordered_ref
  20.6 31.6 %shard_map.185 = (bf16[4096,128]{1,0:T(8,128)(2,1)}, bf16[8,256,128]{2,1,0:T(8,128)(2,1)}) custom-call(bf16[8,256,256]{2,1,0:T(8,128)(2,1)} %broadcast_select_fusion.ordered_ref, bf16[256,128]{1,0:T(8,128)(2,1)} %maximum_bitcast_fusion.packed_ref), custom_call_target="tpu_custom_call" | custom-call | tf_op jit(solution)/shard_map/pallas_call | solution.py:640
  52.1 1.4 copy.54
  53.6 0.8 reshape_reshape_reshape.9
  54.4 1.0 reshape_reshape.6
  55.4 1.7 convolution_convert_fusion.3
  57.2 6.8 %shard_map.186 = bf16[512,64]{1,0:T(8,128)(2,1)S(1)} custom-call(s32[2]{0:T(128)S(1)} %pad_add_fusion.lens_ref, bf16[512,64]{1,0:T(8,128)(2,1)S(1)} %get-tuple-element.24.q_ref, bf16[4096,128]{1,0:T(8,128)(2,1)S(1)} %copy-done.1, bf16[512,64]{1,0:T(8,128)(2,1)S(1)} %get-tuple-element.23.kn_ref, bf16[512,64]{1,0:T(8,128)(2,1)S(1)} %get-tuple-element.22.vn_ref, ...), custom_call_target="tpu_custom_call" | custom-call | tf_op jit(solution)/shard_map/pallas_call | solution.py:362
  64.1 1.4 convolution_convert_fusion.2.refs_0_
  65.4 61.0 %shard_map.187 = (f32[32,1024]{1,0:T(8,128)}, bf16[512,1024]{1,0:T(8,128)(2,1)}, bf16[8,784,128]{2,1,0:T(8,128)(2,1)}) custom-call(bf16[512,1024]{1,0:T(8,128)(2,1)} %convolution_convert_fusion.2.refs_0_, f32[32,1024]{1,0:T(8,128)} %dynamic-slice_convert_fusion.refs_1_, f32[1,1024]{1,0:T(1,128)} %get-tuple-element.27.refs_2_, bf16[784,128]{1,0:T(8,128)(2,1)} %bitcast.86), custom_call_target="tpu_custom_call" | custom-call | tf_op jit(solution)/shard_map/pallas_call | solution.py:295
  126.5 1.9 copy.53
  128.4 1.2 copy-done.2
  129.6 0.8 reshape_reshape_reshape.10
  130.4 1.4 convolution_convert_fusion.4
  131.8 1.6 fusion.41
  133.5 0.2 reshape_reshape.7
  133.7 2.0 fusion.45
  135.7 0.2 fusion.7
  135.9 2.6 %convolution_convert_fusion.1.refs_0_ = bf16[512,1024]{1,0:T(8,128)(2,1)} fusion(f32[512,512]{0,1:T(8,128)S(1)} %get-tuple-element.29, f32[512]{0:T(512)S(1)} %fusion.7, f32[512]{0:T(512)S(1)} %get-tuple-element.28, bf16[8,8,8,128]{3,2,1,0:T(8,128)(2,1)} %bitcast.87, bf16[1,512,2,1,64]{1,4,2,3,0:T(8,128)(2,1)S(1)} %bitcast.85), kind=kOutput, calls=%fused_computation.8 | convolution fusion | flops 102006784 | bytes 2297856 | tf_op jit(solution)/shard_map/dot_general | solution.py:750
  138.5 33.5 %shard_map.188 = (f32[32,1024]{1,0:T(8,128)}, bf16[512,1024]{1,0:T(8,128)(2,1)}) custom-call(bf16[512,1024]{1,0:T(8,128)(2,1)} %convolution_convert_fusion.1.refs_0_, f32[32,1024]{1,0:T(8,128)} %get-tuple-element.14.refs_1_, f32[1,1024]{1,0:T(1,128)} %get-tuple-element.25.refs_2_), custom_call_target="tpu_custom_call" | custom-call | tf_op jit(solution)/shard_map/pallas_call | solution.py:295
  172.0 1.0 slice.103
  173.0 2.0 slice.100
  175.0 2.3 %reshape_reshape_reshape.11 = bf16[1024,352]{1,0:T(8,128)(2,1)S(1)} reshape(bf16[8,45056]{1,0:T(8,128)(2,1)} %slice.100) | data formatting | bytes 1441792 | tf_op jit(solution)/shard_map/reshape;reshape;reshape | solution.py:753
  177.3 1.8 fusion.46
  179.1 1.5 convolution_convert_fusion.refs_0_
  180.6 31.7 %shard_map.189 = (f32[32,1024]{1,0:T(8,128)}, bf16[512,1024]{1,0:T(8,128)(2,1)}) custom-call(bf16[512,1024]{1,0:T(8,128)(2,1)} %convolution_convert_fusion.refs_0_, f32[32,1024]{1,0:T(8,128)} %get-tuple-element.16.refs_1_, f32[1,1024]{1,0:T(1,128)} %get-tuple-element.25.refs_2_), custom_call_target="tpu_custom_call" | custom-call | tf_op jit(solution)/shard_map/pallas_call | solution.py:295
  212.4 2.3 %copy.61 = bf16[512,1024]{1,0:T(8,128)(2,1)} copy(bf16[512,1024]{1,0:T(8,128)(2,1)} %get-tuple-element.36) | data formatting | bytes 2097152
  214.6 1.0 copy.62
  (46 shorter events, 0.9 us)
Async XLA Ops:
  0.6 18.2 %copy-start = (bf16[8,256,256]{2,1,0:T(8,128)(2,1)S(1)}, bf16[8,256,256]{2,1,0:T(8,128)(2,1)}, u32[]{:S(2)}) copy-start(bf16[8,256,256]{2,1,0:T(8,128)(2,1)} %param.20) | copy-start | bytes 3145732
  0.6 17.0 %copy-start.3 = (bf16[512,1024]{1,0:T(8,128)(2,1)S(1)}, bf16[512,1024]{1,0:T(8,128)(2,1)}, u32[]{:S(2)}) copy-start(bf16[512,1024]{1,0:T(8,128)(2,1)} %param.18) | copy-start | bytes 3145732
  0.7 17.7 %copy-start.6 = (bf16[128,2,176]{0,2,1:T(8,128)(2,1)S(1)}, bf16[128,2,176]{0,2,1:T(8,128)(2,1)}, u32[]{:S(2)}) copy-start(bf16[128,2,176]{0,2,1:T(8,128)(2,1)} %param.34) | copy-start | bytes 270340
  0.7 18.1 %copy-start.12 = (bf16[64,128]{1,0:T(8,128)(2,1)S(1)}, bf16[64,128]{1,0:T(8,128)(2,1)}, u32[]{:S(2)}) copy-start(bf16[64,128]{1,0:T(8,128)(2,1)} %param.33) | copy-start | bytes 49156
  0.7 16.7 %copy-start.9 = (bf16[128,2,64]{0,2,1:T(8,128)(2,1)S(1)}, bf16[128,2,64]{0,2,1:T(8,128)(2,1)}, u32[]{:S(2)}) copy-start(bf16[128,2,64]{0,2,1:T(8,128)(2,1)} %param.32) | copy-start | bytes 98308
  0.7 15.6 %copy-start.11 = (bf16[128,64]{0,1:T(8,128)(2,1)S(1)}, bf16[128,64]{0,1:T(8,128)(2,1)}, u32[]{:S(2)}) copy-start(bf16[128,64]{0,1:T(8,128)(2,1)} %param.31) | copy-start | bytes 49156
  0.7 16.1 %copy-start.13 = (bf16[64,128]{1,0:T(8,128)(2,1)S(1)}, bf16[64,128]{1,0:T(8,128)(2,1)}, u32[]{:S(2)}) copy-start(bf16[64,128]{1,0:T(8,128)(2,1)} %param.30) | copy-start | bytes 49156
  0.7 15.8 %copy-start.8 = (bf16[128,2,64]{0,2,1:T(8,128)(2,1)S(1)}, bf16[128,2,64]{0,2,1:T(8,128)(2,1)}, u32[]{:S(2)}) copy-start(bf16[128,2,64]{0,2,1:T(8,128)(2,1)} %param.29) | copy-start | bytes 98308
  0.7 15.4 %copy-start.10 = (bf16[128,64]{0,1:T(8,128)(2,1)S(1)}, bf16[128,64]{0,1:T(8,128)(2,1)}, u32[]{:S(2)}) copy-start(bf16[128,64]{0,1:T(8,128)(2,1)} %param.28) | copy-start | bytes 49156
  5.4 13.4 %copy-start.7 = (bf16[176,128]{1,0:T(8,128)(2,1)S(1)}, bf16[176,128]{1,0:T(8,128)(2,1)}, u32[]{:S(2)}) copy-start(bf16[176,128]{1,0:T(8,128)(2,1)} %param.35) | copy-start | bytes 135172
  18.8 1.8 copy-start.5
  55.4 1.8 copy-start.1
  126.5 4.0 %copy-start.4 = (bf16[512,1024]{1,0:T(8,128)(2,1)S(1)}, bf16[512,1024]{1,0:T(8,128)(2,1)}, u32[]{:S(2)}) copy-start(bf16[512,1024]{1,0:T(8,128)(2,1)} %param.19) | copy-start | bytes 3145732
  128.4 1.2 copy-start.2

commit v8 on v7

--- a/solution.py
+++ b/solution.py
@@ -128,10 +128,10 @@
 def stage_kernel(n_blk, final, extra, *refs):
     if extra:
         (part_ref, resid_ref, gain_ref, packed_ref, res_out, full_ref, wts_ref,
-         recv, rs_send, rs_recv, ag_send, ag_recv, w_send, w_recv) = refs
+         recv_a, send_b, recv_b, sems, b_send, b_recv, ag_send, ag_recv, w_send, w_recv) = refs
     else:
         (part_ref, resid_ref, gain_ref, res_out, full_ref,
-         recv, rs_send, rs_recv, ag_send, ag_recv) = refs
+         recv_a, send_b, recv_b, sems, b_send, b_recv, ag_send, ag_recv) = refs
     me = lax.axis_index("blk")
     req = lax.axis_index("req")
     rows = resid_ref.shape[0]
@@ -140,17 +140,27 @@
     c = lax.rem(me, 2)
     partner = g * 2 + 1 - c
     half = n_grp * rows
+    n_req = wts_ref.shape[0] if extra else 1
     barrier = pltpu.get_barrier_semaphore()
-    for k in range(1, n_blk):
-        peer = lax.rem(me + k, n_blk)
+    for k in range(1, n_grp):
+        peer = lax.rem(g + k, n_grp) * 2 + c
         pl.semaphore_signal(barrier, inc=1, device_id=(req, peer), device_id_type=MESH_IDS)
-    n_req = wts_ref.shape[0] if extra else 1
+    pl.semaphore_signal(barrier, inc=1, device_id=(req, partner), device_id_type=MESH_IDS)
     for k in range(1, n_req):
         peer = lax.rem(req + k, n_req)
         pl.semaphore_signal(barrier, inc=1, device_id=(peer, me), device_id_type=MESH_IDS)
-    pl.semaphore_wait(barrier, n_blk - 1 + n_req - 1)
+    pl.semaphore_wait(barrier, n_grp + n_req - 1)
     sends = []
-    w_sends = []
+    exchange = pltpu.make_async_remote_copy(
+        src_ref=part_ref.at[pl.ds(pl.multiple_of((1 - c) * half, half), half)],
+        dst_ref=recv_a,
+        send_sem=sems.at[0],
+        recv_sem=sems.at[1],
+        device_id=(req, partner),
+        device_id_type=MESH_IDS,
+    )
+    exchange.start()
+    sends.append(exchange)
     for k in range(1, n_req):
         peer = lax.rem(req + k, n_req)
         copy = pltpu.make_async_remote_copy(
@@ -162,33 +172,38 @@
             device_id_type=MESH_IDS,
         )
         copy.start()
-        w_sends.append(copy)
-    for k in range(1, n_blk):
-        peer = lax.rem(me + k, n_blk)
+        sends.append(copy)
+    exchange.wait_recv()
+    pair = part_ref[pl.ds(pl.multiple_of(c * half, half), half), :].astype(jnp.float32) + recv_a[
+        ...
+    ].astype(jnp.float32)
+    send_b[...] = pair.astype(send_b.dtype)
+    for k in range(1, n_grp):
+        grp = lax.rem(g + k, n_grp)
         copy = pltpu.make_async_remote_copy(
-            src_ref=part_ref.at[pl.ds(pl.multiple_of(chunk_of(peer, n_blk) * rows, rows), rows)],
-            dst_ref=recv.at[me],
-            send_sem=rs_send.at[peer],
-            recv_sem=rs_recv.at[me],
-            device_id=(req, peer),
+            src_ref=send_b.at[pl.ds(pl.multiple_of(grp * rows, rows), rows)],
+            dst_ref=recv_b.at[g],
+            send_sem=b_send.at[grp],
+            recv_sem=b_recv.at[g],
+            device_id=(req, grp * 2 + c),
             device_id_type=MESH_IDS,
         )
         copy.start()
         sends.append(copy)
+    total = send_b[pl.ds(pl.multiple_of(g * rows, rows), rows), :].astype(jnp.float32)
+    for k in range(1, n_grp):
+        grp = lax.rem(g + n_grp - k, n_grp)
+        incoming = pltpu.make_async_remote_copy(
+            src_ref=send_b.at[pl.ds(0, rows)],
+            dst_ref=recv_b.at[grp],
+            send_sem=b_send.at[grp],
+            recv_sem=b_recv.at[grp],
+            device_id=(req, grp * 2 + c),
+            device_id_type=MESH_IDS,
+        )
+        incoming.wait_recv()
+        total = total + recv_b[grp].astype(jnp.float32)
     mine = pl.ds(pl.multiple_of(c * half + g * rows, rows), rows)
-    total = part_ref[mine, :].astype(jnp.float32)
-    for k in range(1, n_blk):
-        src = lax.rem(me + n_blk - k, n_blk)
-        incoming = pltpu.make_async_remote_copy(
-            src_ref=part_ref.at[pl.ds(0, rows)],
-            dst_ref=recv.at[src],
-            send_sem=rs_send.at[src],
-            recv_sem=rs_recv.at[src],
-            device_id=(req, src),
-            device_id_type=MESH_IDS,
-        )
-        incoming.wait_recv()
-        total = total + recv[src].astype(jnp.float32)
     resid = resid_ref[...] + total
     res_out[...] = resid
     if final:
@@ -266,7 +281,7 @@
                 device_id_type=MESH_IDS,
             )
             incoming.wait_recv()
-    for copy in sends + w_sends:
+    for copy in sends:
         copy.wait_send()
 
 
@@ -279,10 +294,14 @@
         jax.ShapeDtypeStruct((rows, width), jnp.float32),
         jax.ShapeDtypeStruct((rows * n_blk, width), jnp.bfloat16),
     ]
+    n_grp = n_blk // 2
     scratch = [
-        pltpu.VMEM((n_blk, rows, width), part.dtype),
-        pltpu.SemaphoreType.DMA((n_blk,)),
-        pltpu.SemaphoreType.DMA((n_blk,)),
+        pltpu.VMEM((n_grp * rows, width), part.dtype),
+        pltpu.VMEM((n_grp * rows, width), part.dtype),
+        pltpu.VMEM((n_grp, rows, width), part.dtype),
+        pltpu.SemaphoreType.DMA((2,)),
+        pltpu.SemaphoreType.DMA((n_grp,)),
+        pltpu.SemaphoreType.DMA((n_grp,)),
         pltpu.SemaphoreType.DMA((n_blk,)),
         pltpu.SemaphoreType.DMA((n_blk,)),
     ]

time: 219 us -> 204 us (0.932); the launches traced: 216 us -> 203 us
  Pallas kernels: 165 us -> 152 us
    pallas_call x3, Pallas kernels: 126 us -> 114 us  [blk_stage(): pl.pallas_call(functools.partial(stage_kernel, n_blk, final, extra), out_...]
where the time goes in v8:
time: 204 us; the launch traced here: 203 us
  Pallas kernels  152 us (75%)
  local copies, waits for them, and re-layouts  24.5 us (12%)
  matrix products  13.4 us (7%)
  other arithmetic  10.7 us (5%)
  between operations  2.35 us (1%)
    pallas_call x3, Pallas kernels, blk_stage(): pl.pallas_call(functools.partial(stage_kernel, n_blk, final, extra), out_...  114 us
    pallas_call x1, Pallas kernels, prologue(): pl.pallas_call(functools.partial(prologue_kernel, n_req, n_blk), out_shap...  31.6 us
    unnamed x41, local copies, waits for them, and re-layouts  8.39 us
    pallas_call x1, Pallas kernels, self_attention(): pl.pallas_call(self_kernel, out_shape=jax.ShapeDtypeStruct((n_q, HD), jnp...  6.85 us
    slice x6, local copies, waits for them, and re-layouts, unpack(): part = whole[:, at:at + size].reshape((n_req,) + w.shape)  4.72 us

profile of v8, /device:TPU:33, one launch (start us, length us, event | category | flops | bytes accessed | tf_op | source)
XLA Modules:
  0.0 203.0 jit_solution(14577944736282514473)
XLA Ops:
  0.8 1.4 dynamic_slice.12
  2.1 0.7 compare_and_fusion
  2.8 2.0 select_reduce_fusion.1
  6.0 1.3 pad_add_fusion.lens_ref
  7.4 2.0 compare_select_fusion
  9.3 0.6 iota_compare_fusion.2
  10.0 1.5 fusion
  11.5 1.4 fusion.44
  12.9 1.0 convolution_reduce_fusion
  14.0 0.5 slice.93
  14.5 0.6 pad_slice_fusion
  15.2 0.6 concatenate.14
  16.1 0.1 copy.27
  16.3 0.1 copy.30
  16.5 0.1 copy.28
  16.8 0.6 maximum_bitcast_fusion.packed_ref
  17.4 0.1 copy.31
  17.7 0.7 dynamic-slice_convert_fusion.refs_1_
  18.3 0.1 copy.32
  18.5 0.2 reshape.149
  18.8 0.6 gather_fusion
  19.4 1.1 broadcast_select_fusion.ordered_ref
  20.6 31.6 %shard_map.185 = (bf16[4096,128]{1,0:T(8,128)(2,1)}, bf16[8,256,128]{2,1,0:T(8,128)(2,1)}) custom-call(bf16[8,256,256]{2,1,0:T(8,128)(2,1)} %broadcast_select_fusion.ordered_ref, bf16[256,128]{1,0:T(8,128)(2,1)} %maximum_bitcast_fusion.packed_ref), custom_call_target="tpu_custom_call" | custom-call | tf_op jit(solution)/shard_map/pallas_call | solution.py:659
  52.1 1.4 copy.54
  53.6 0.8 reshape_reshape_reshape.9
  54.4 1.0 reshape_reshape.6
  55.4 1.7 convolution_convert_fusion.3
  57.2 6.8 %shard_map.186 = bf16[512,64]{1,0:T(8,128)(2,1)S(1)} custom-call(s32[2]{0:T(128)S(1)} %pad_add_fusion.lens_ref, bf16[512,64]{1,0:T(8,128)(2,1)S(1)} %get-tuple-element.24.q_ref, bf16[4096,128]{1,0:T(8,128)(2,1)S(1)} %copy-done.1, bf16[512,64]{1,0:T(8,128)(2,1)S(1)} %get-tuple-element.23.kn_ref, bf16[512,64]{1,0:T(8,128)(2,1)S(1)} %get-tuple-element.22.vn_ref, ...), custom_call_target="tpu_custom_call" | custom-call | tf_op jit(solution)/shard_map/pallas_call | solution.py:381
  64.1 1.4 convolution_convert_fusion.2.refs_0_
  65.4 55.8 %shard_map.187 = (f32[32,1024]{1,0:T(8,128)}, bf16[512,1024]{1,0:T(8,128)(2,1)}, bf16[8,784,128]{2,1,0:T(8,128)(2,1)}) custom-call(bf16[512,1024]{1,0:T(8,128)(2,1)} %convolution_convert_fusion.2.refs_0_, f32[32,1024]{1,0:T(8,128)} %dynamic-slice_convert_fusion.refs_1_, f32[1,1024]{1,0:T(1,128)} %get-tuple-element.27.refs_2_, bf16[784,128]{1,0:T(8,128)(2,1)} %bitcast.86), custom_call_target="tpu_custom_call" | custom-call | tf_op jit(solution)/shard_map/pallas_call | solution.py:314
  121.3 1.9 copy.53
  123.2 1.2 copy-done.2
  124.4 0.8 reshape_reshape_reshape.10
  125.2 1.4 convolution_convert_fusion.4
  126.7 1.6 fusion.41
  128.3 0.2 reshape_reshape.7
  128.5 2.0 fusion.45
  130.5 0.2 fusion.7
  130.7 2.6 %convolution_convert_fusion.1.refs_0_ = bf16[512,1024]{1,0:T(8,128)(2,1)} fusion(f32[512,512]{0,1:T(8,128)S(1)} %get-tuple-element.29, f32[512]{0:T(512)S(1)} %fusion.7, f32[512]{0:T(512)S(1)} %get-tuple-element.28, bf16[8,8,8,128]{3,2,1,0:T(8,128)(2,1)} %bitcast.87, bf16[1,512,2,1,64]{1,4,2,3,0:T(8,128)(2,1)S(1)} %bitcast.85), kind=kOutput, calls=%fused_computation.8 | convolution fusion | flops 102006784 | bytes 2297856 | tf_op jit(solution)/shard_map/dot_general | solution.py:769
  133.3 31.5 %shard_map.188 = (f32[32,1024]{1,0:T(8,128)}, bf16[512,1024]{1,0:T(8,128)(2,1)}) custom-call(bf16[512,1024]{1,0:T(8,128)(2,1)} %convolution_convert_fusion.1.refs_0_, f32[32,1024]{1,0:T(8,128)} %get-tuple-element.14.refs_1_, f32[1,1024]{1,0:T(1,128)} %get-tuple-element.25.refs_2_), custom_call_target="tpu_custom_call" | custom-call | tf_op jit(solution)/shard_map/pallas_call | solution.py:314
  164.8 1.0 slice.103
  165.8 2.0 slice.100
  167.8 2.3 %reshape_reshape_reshape.11 = bf16[1024,352]{1,0:T(8,128)(2,1)S(1)} reshape(bf16[8,45056]{1,0:T(8,128)(2,1)} %slice.100) | data formatting | bytes 1441792 | tf_op jit(solution)/shard_map/reshape;reshape;reshape | solution.py:772
  170.1 1.8 fusion.46
  171.9 1.5 convolution_convert_fusion.refs_0_
  173.4 26.4 %shard_map.189 = (f32[32,1024]{1,0:T(8,128)}, bf16[512,1024]{1,0:T(8,128)(2,1)}) custom-call(bf16[512,1024]{1,0:T(8,128)(2,1)} %convolution_convert_fusion.refs_0_, f32[32,1024]{1,0:T(8,128)} %get-tuple-element.16.refs_1_, f32[1,1024]{1,0:T(1,128)} %get-tuple-element.25.refs_2_), custom_call_target="tpu_custom_call" | custom-call | tf_op jit(solution)/shard_map/pallas_call | solution.py:314
  199.8 2.3 %copy.61 = bf16[512,1024]{1,0:T(8,128)(2,1)} copy(bf16[512,1024]{1,0:T(8,128)(2,1)} %get-tuple-element.36) | data formatting | bytes 2097152
  202.1 1.0 copy.62
  (46 shorter events, 0.9 us)
Async XLA Ops:
  0.6 18.2 %copy-start = (bf16[8,256,256]{2,1,0:T(8,128)(2,1)S(1)}, bf16[8,256,256]{2,1,0:T(8,128)(2,1)}, u32[]{:S(2)}) copy-start(bf16[8,256,256]{2,1,0:T(8,128)(2,1)} %param.20) | copy-start | bytes 3145732
  0.6 17.0 %copy-start.3 = (bf16[512,1024]{1,0:T(8,128)(2,1)S(1)}, bf16[512,1024]{1,0:T(8,128)(2,1)}, u32[]{:S(2)}) copy-start(bf16[512,1024]{1,0:T(8,128)(2,1)} %param.18) | copy-start | bytes 3145732
  0.7 17.7 %copy-start.6 = (bf16[128,2,176]{0,2,1:T(8,128)(2,1)S(1)}, bf16[128,2,176]{0,2,1:T(8,128)(2,1)}, u32[]{:S(2)}) copy-start(bf16[128,2,176]{0,2,1:T(8,128)(2,1)} %param.34) | copy-start | bytes 270340
  0.7 18.1 %copy-start.12 = (bf16[64,128]{1,0:T(8,128)(2,1)S(1)}, bf16[64,128]{1,0:T(8,128)(2,1)}, u32[]{:S(2)}) copy-start(bf16[64,128]{1,0:T(8,128)(2,1)} %param.33) | copy-start | bytes 49156
  0.7 16.7 %copy-start.9 = (bf16[128,2,64]{0,2,1:T(8,128)(2,1)S(1)}, bf16[128,2,64]{0,2,1:T(8,128)(2,1)}, u32[]{:S(2)}) copy-start(bf16[128,2,64]{0,2,1:T(8,128)(2,1)} %param.32) | copy-start | bytes 98308
  0.7 15.6 %copy-start.11 = (bf16[128,64]{0,1:T(8,128)(2,1)S(1)}, bf16[128,64]{0,1:T(8,128)(2,1)}, u32[]{:S(2)}) copy-start(bf16[128,64]{0,1:T(8,128)(2,1)} %param.31) | copy-start | bytes 49156
  0.7 16.1 %copy-start.13 = (bf16[64,128]{1,0:T(8,128)(2,1)S(1)}, bf16[64,128]{1,0:T(8,128)(2,1)}, u32[]{:S(2)}) copy-start(bf16[64,128]{1,0:T(8,128)(2,1)} %param.30) | copy-start | bytes 49156
  0.7 15.8 %copy-start.8 = (bf16[128,2,64]{0,2,1:T(8,128)(2,1)S(1)}, bf16[128,2,64]{0,2,1:T(8,128)(2,1)}, u32[]{:S(2)}) copy-start(bf16[128,2,64]{0,2,1:T(8,128)(2,1)} %param.29) | copy-start | bytes 98308
  0.7 15.4 %copy-start.10 = (bf16[128,64]{0,1:T(8,128)(2,1)S(1)}, bf16[128,64]{0,1:T(8,128)(2,1)}, u32[]{:S(2)}) copy-start(bf16[128,64]{0,1:T(8,128)(2,1)} %param.28) | copy-start | bytes 49156
  5.4 13.4 %copy-start.7 = (bf16[176,128]{1,0:T(8,128)(2,1)S(1)}, bf16[176,128]{1,0:T(8,128)(2,1)}, u32[]{:S(2)}) copy-start(bf16[176,128]{1,0:T(8,128)(2,1)} %param.35) | copy-start | bytes 135172
  18.8 1.8 copy-start.5
  55.4 1.8 copy-start.1
  121.3 4.0 %copy-start.4 = (bf16[512,1024]{1,0:T(8,128)(2,1)S(1)}, bf16[512,1024]{1,0:T(8,128)(2,1)}, u32[]{:S(2)}) copy-start(bf16[512,1024]{1,0:T(8,128)(2,1)} %param.19) | copy-start | bytes 3145732
  123.2 1.2 copy-start.2

commit v9 on v8

--- a/solution.py
+++ b/solution.py
@@ -729,8 +729,8 @@
     flat = jnp.concatenate([w.reshape(-1) for w, _ in early])
     cache_blk, whole = prologue(ordered, flat.reshape(-1, 128))
     cache_dec = cache_blk[None]
-    late_flat = jnp.concatenate([w.reshape(-1) for w, _ in late]).reshape(-1, 128)
     gathered = unpack(whole, early)
+    late_gathered = pack_gather(late)
     wq_self, wkv_self, wo_self = gathered
     n_blk = lax.axis_size("blk")
     rows_dev = new_states.shape[0] // n_blk
@@ -752,8 +752,8 @@
         slot_new[0],
     )
     part = jnp.dot(context, wo_self, preferred_element_type=jnp.float32).astype(jnp.bfloat16)
-    residual, normed, late_whole = blk_stage(part, own_rows, norm_gain[1], False, late_flat)
-    wq_cross, wkv_cross, wo_cross, w_in, w_out = unpack(late_whole, late)
+    residual, normed = blk_stage(part, own_rows, norm_gain[1], False)
+    wq_cross, wkv_cross, wo_cross, w_in, w_out = late_gathered
     queries = (
         jnp.dot(normed, wq_cross, preferred_element_type=jnp.float32)
         .astype(jnp.bfloat16)

time: 204 us -> 202 us (level)
  Pallas kernels: 152 us -> 137 us
  between operations: 2.35 us -> 15.8 us
  other arithmetic: 10.7 us -> 7.51 us
    pallas_call x3, Pallas kernels: 114 us -> 91.1 us  [blk_stage(): pl.pallas_call(functools.partial(stage_kernel, n_blk, final, extra), out_...]
    pallas_call x1, Pallas kernels: 31.6 us -> 39.5 us  [prologue(): pl.pallas_call(functools.partial(prologue_kernel, n_req, n_blk), out_shap...]
    slice x6 -> x2, local copies, waits for them, and re-layouts: 4.72 us -> 0.04 us  [unpack(): part = whole[:, at:at + size].reshape((n_req,) + w.shape)]
    all_gather x0 -> x1, local copies, waits for them, and re-layouts: none -> 3.25 us  [pack_gather(): whole = lax.all_gather(flat, 'req', axis=0, tiled=False)]
    unnamed x41 -> x38, local copies, waits for them, and re-layouts: 8.39 us -> 9.21 us
  transfers between devices with their start and end apart: 0 -> 1, of which waited for: 0 -> 0; matrix products, arithmetic and copies ran while one was open for 0% -> 10% of each run, Pallas kernels for 0% -> 41%
where the time goes in v9:
time: 202 us; the launch traced here: 200 us
  Pallas kernels  137 us (68%)
  local copies, waits for them, and re-layouts  24.6 us (12%)
  between operations  15.8 us (8%)
  matrix products  14.1 us (7%)
  other arithmetic  7.51 us (4%)
    pallas_call x3, Pallas kernels, blk_stage(): pl.pallas_call(functools.partial(stage_kernel, n_blk, final, extra), out_...  91.1 us
    pallas_call x1, Pallas kernels, prologue(): pl.pallas_call(functools.partial(prologue_kernel, n_req, n_blk), out_shap...  39.5 us
    unnamed x38, local copies, waits for them, and re-layouts  9.21 us
    pallas_call x1, Pallas kernels, self_attention(): pl.pallas_call(self_kernel, out_shape=jax.ShapeDtypeStruct((n_q, HD), jnp...  6.87 us
  transfers between devices with their start and end apart: 1, of which 0 were waited for; matrix products, arithmetic and copies ran while one was open for 10% of the time, Pallas kernels for 41%

profile of v9, /device:TPU:33, one launch (start us, length us, event | category | flops | bytes accessed | tf_op | source)
XLA Modules:
  0.0 199.6 jit_solution(8759942568576781531)
XLA Ops:
  7.3 0.9 copy.33
  8.3 0.9 copy.34
  9.3 1.0 copy.35
  10.3 0.2 reshape.135
  10.5 0.7 bitcast_dynamic-update-slice_fusion.1
  11.3 0.8 bitcast_dynamic-update-slice_fusion
  12.1 0.7 copy-done.4
  12.8 1.0 convolution_reduce_fusion
  13.8 0.5 slice.95
  14.3 0.6 pad_slice_fusion
  15.0 0.7 concatenate.15
  15.7 0.6 dynamic_slice.12
  16.3 1.3 compare_select_fusion
  17.6 1.4 select_reduce_fusion.1
  20.6 0.1 copy.36
  20.8 0.1 copy.37
  21.1 0.6 gather_fusion
  21.7 1.1 broadcast_select_fusion.ordered_ref
  22.9 0.6 maximum_bitcast_fusion.packed_ref
  23.5 39.5 %shard_map.185 = (bf16[4096,128]{1,0:T(8,128)(2,1)}, bf16[8,256,128]{2,1,0:T(8,128)(2,1)}) custom-call(bf16[8,256,256]{2,1,0:T(8,128)(2,1)} %broadcast_select_fusion.ordered_ref, bf16[256,128]{1,0:T(8,128)(2,1)} %maximum_bitcast_fusion.packed_ref), custom_call_target="tpu_custom_call" | custom-call | tf_op jit(solution)/shard_map/pallas_call | solution.py:659
  63.0 1.5 copy.57
  64.5 0.8 reshape_reshape_reshape.10
  65.4 1.0 reshape_reshape.6
  66.3 1.3 pad_add_fusion.lens_ref
  67.6 0.3 fusion
  67.9 0.6 fusion.44
  68.5 1.7 convolution_convert_fusion.3
  70.4 6.9 %shard_map.186 = bf16[512,64]{1,0:T(8,128)(2,1)S(1)} custom-call(s32[2]{0:T(128)S(1)} %pad_add_fusion.lens_ref, bf16[512,64]{1,0:T(8,128)(2,1)S(1)} %get-tuple-element.22.q_ref, bf16[4096,128]{1,0:T(8,128)(2,1)S(1)} %copy-done.1, bf16[512,64]{1,0:T(8,128)(2,1)S(1)} %get-tuple-element.21.kn_ref, bf16[512,64]{1,0:T(8,128)(2,1)S(1)} %get-tuple-element.20.vn_ref, ...), custom_call_target="tpu_custom_call" | custom-call | tf_op jit(solution)/shard_map/pallas_call | solution.py:381
  77.3 0.7 dynamic-slice_convert_fusion.refs_1_
  78.0 1.4 convolution_convert_fusion.2.refs_0_
  79.3 36.2 %shard_map.187 = (f32[32,1024]{1,0:T(8,128)}, bf16[512,1024]{1,0:T(8,128)(2,1)}) custom-call(bf16[512,1024]{1,0:T(8,128)(2,1)} %convolution_convert_fusion.2.refs_0_, f32[32,1024]{1,0:T(8,128)} %dynamic-slice_convert_fusion.refs_1_, f32[1,1024]{1,0:T(1,128)} %get-tuple-element.25.refs_2_), custom_call_target="tpu_custom_call" | custom-call | tf_op jit(solution)/shard_map/pallas_call | solution.py:314
  115.6 0.6 iota_compare_fusion.2
  116.2 3.3 %reshape.161 = bf16[8,100352]{1,0:T(8,128)(2,1)} reshape(bf16[802816]{0:T(1024)(128)(2,1)} %all-gather.3.cloned.1.call-done) | data formatting | bytes 3211264 | tf_op jit(solution)/shard_map/all_gather | solution.py:392
  119.5 1.7 fusion.41
  121.2 0.8 reshape_reshape_reshape.9
  122.0 0.2 reshape_reshape.7
  122.2 0.1 slice-done.2
  122.4 2.1 %reshape_reshape_reshape.11 = bf16[1024,352]{1,0:T(8,128)(2,1)} reshape(bf16[8,45056]{1,0:T(8,128)(2,1)S(1)} %slice-done.2) | data formatting | bytes 1441792 | tf_op jit(solution)/shard_map/reshape;reshape;reshape | solution.py:772
  124.4 1.9 convolution_convert_fusion.4
  126.3 2.0 fusion.45
  128.3 0.2 fusion.7
  128.5 2.6 %convolution_convert_fusion.1.refs_0_ = bf16[512,1024]{1,0:T(8,128)(2,1)} fusion(f32[512,512]{0,1:T(8,128)S(1)} %get-tuple-element.27, f32[512]{0:T(512)S(1)} %fusion.7, f32[512]{0:T(512)S(1)} %get-tuple-element.26, bf16[8,8,8,128]{3,2,1,0:T(8,128)(2,1)} %bitcast.76, bf16[1,512,2,1,64]{1,4,2,3,0:T(8,128)(2,1)S(1)} %bitcast.75), kind=kOutput, calls=%fused_computation.7 | convolution fusion | flops 102006784 | bytes 2297856 | tf_op jit(solution)/shard_map/dot_general | solution.py:769
  131.1 28.4 %shard_map.188 = (f32[32,1024]{1,0:T(8,128)}, bf16[512,1024]{1,0:T(8,128)(2,1)}) custom-call(bf16[512,1024]{1,0:T(8,128)(2,1)} %convolution_convert_fusion.1.refs_0_, f32[32,1024]{1,0:T(8,128)} %get-tuple-element.12.refs_1_, f32[1,1024]{1,0:T(1,128)} %get-tuple-element.23.refs_2_), custom_call_target="tpu_custom_call" | custom-call | tf_op jit(solution)/shard_map/pallas_call | solution.py:314
  159.5 2.0 %fusion.46 = f32[512,352]{0,1:T(8,128)S(1)} fusion(bf16[512,1024]{1,0:T(8,128)(2,1)} %get-tuple-element.13, bf16[1024,352]{1,0:T(8,128)(2,1)} %reshape_reshape_reshape.11), kind=kOutput, calls=%fused_computation.81 | convolution fusion | flops 369098752 | bytes 2490368 | tf_op jit(solution)/shard_map/dot_general | solution.py:772
  161.5 1.5 convolution_convert_fusion.refs_0_
  163.0 26.4 %shard_map.189 = (f32[32,1024]{1,0:T(8,128)}, bf16[512,1024]{1,0:T(8,128)(2,1)}) custom-call(bf16[512,1024]{1,0:T(8,128)(2,1)} %convolution_convert_fusion.refs_0_, f32[32,1024]{1,0:T(8,128)} %get-tuple-element.14.refs_1_, f32[1,1024]{1,0:T(1,128)} %get-tuple-element.23.refs_2_), custom_call_target="tpu_custom_call" | custom-call | tf_op jit(solution)/shard_map/pallas_call | solution.py:314
  189.5 2.3 %copy.64 = bf16[512,1024]{1,0:T(8,128)(2,1)} copy(bf16[512,1024]{1,0:T(8,128)(2,1)} %get-tuple-element.34) | data formatting | bytes 2097152
  191.7 1.0 copy.65
  (50 shorter events, 1.0 us)
Async XLA Ops:
  7.2 13.9 %copy-start = (bf16[8,256,256]{2,1,0:T(8,128)(2,1)S(1)}, bf16[8,256,256]{2,1,0:T(8,128)(2,1)}, u32[]{:S(2)}) copy-start(bf16[8,256,256]{2,1,0:T(8,128)(2,1)} %param.20) | copy-start | bytes 3145732
  7.2 8.5 %copy-start.9 = (s32[8]{0:T(128)S(1)}, s32[8]{0:T(128)}, u32[]{:S(2)}) copy-start(s32[8]{0:T(128)} %param.21) | copy-start | bytes 100
  7.2 9.1 %copy-start.10 = (s32[8]{0:T(128)S(1)}, s32[8]{0:T(128)}, u32[]{:S(2)}) copy-start(s32[8]{0:T(128)} %param.22) | copy-start | bytes 100
  7.2 10.4 %copy-start.12 = (s32[8]{0:T(128)S(1)}, s32[8]{0:T(128)}, u32[]{:S(2)}) copy-start(s32[8]{0:T(128)} %param.24) | copy-start | bytes 100
  7.2 10.4 %copy-start.11 = (s32[8]{0:T(128)S(1)}, s32[8]{0:T(128)}, u32[]{:S(2)}) copy-start(s32[8]{0:T(128)} %param.23) | copy-start | bytes 100
  7.2 13.4 %copy-start.6 = (bf16[128,64]{0,1:T(8,128)(2,1)S(1)}, bf16[128,64]{0,1:T(8,128)(2,1)}, u32[]{:S(2)}) copy-start(bf16[128,64]{0,1:T(8,128)(2,1)} %param.28) | copy-start | bytes 49156
  7.2 13.6 %copy-start.5 = (bf16[128,2,64]{0,2,1:T(8,128)(2,1)S(1)}, bf16[128,2,64]{0,2,1:T(8,128)(2,1)}, u32[]{:S(2)}) copy-start(bf16[128,2,64]{0,2,1:T(8,128)(2,1)} %param.29) | copy-start | bytes 98308
  7.2 109.0 %all-gather.3.cloned.1.call-start = ((), (), s32[]{:S(2)}) async-start(), calls=%async_computation | async-start | bytes 1806336 | tf_op jit(solution)/shard_map/all_gather | solution.py:392
  12.1 0.7 copy-start.4
  21.1 1.8 copy-start.7
  63.0 4.7 %copy-start.2 = (bf16[512,1024]{1,0:T(8,128)(2,1)S(1)}, bf16[512,1024]{1,0:T(8,128)(2,1)}, u32[]{:S(2)}) copy-start(bf16[512,1024]{1,0:T(8,128)(2,1)} %param.18) | copy-start | bytes 3145732
  64.5 3.5 %copy-start.8 = (f32[3,1024]{1,0:T(4,128)S(1)}, f32[3,1024]{1,0:T(4,128)}, u32[]{:S(2)}) copy-start(f32[3,1024]{1,0:T(4,128)} %param.27) | copy-start | bytes 36868
  68.5 1.9 copy-start.1
  119.5 1.7 slice-start
  121.2 1.2 slice-start.2
  122.0 2.4 %copy-start.3 = (bf16[1024,128]{1,0:T(8,128)(2,1)S(1)}, bf16[1024,128]{1,0:T(8,128)(2,1)}, u32[]{:S(2)}) copy-start(bf16[1024,128]{1,0:T(8,128)(2,1)} %reshape_reshape_reshape.9) | copy-start | bytes 786436
  131.1 30.4 %slice-start.1 = ((bf16[8,100352]{1,0:T(8,128)(2,1)}), bf16[8,22528]{1,0:T(8,128)(2,1)S(1)}, s32[]{:S(2)}) async-start(bf16[8,100352]{1,0:T(8,128)(2,1)} %reshape.161), calls=%async_computation.2 | async-start | bytes 720896 | tf_op jit(solution)/shard_map/slice | solution.py:397
Sparse Core Ops, SparseCore 0:
  12.9 64.4 all-gather.2

commit v10 on v9

--- a/solution.py
+++ b/solution.py
@@ -586,7 +586,8 @@
         copy.start()
         copies.append(copy)
     rows = pl.ds(pl.multiple_of(b * span, span), span)
-    for s in range(n_slot):
+    for k in range(n_slot):
+        s = lax.rem(b + k, n_slot)
         for hh in range(2):
             head = 2 * r + hh
             is_self = jnp.logical_and(r == s, head == b)
@@ -594,7 +595,7 @@
             copy = pltpu.make_async_remote_copy(
                 src_ref=src,
                 dst_ref=cache_ref.at[rows],
-                send_sem=c_send.at[s * 2 + hh],
+                send_sem=c_send.at[k * 2 + hh],
                 recv_sem=c_recv.at[b],
                 device_id=(s, head),
                 device_id_type=MESH_IDS,

time: 202 us -> 201 us (level)
  transfers between devices with their start and end apart: 1 -> 1, of which waited for: 0 -> 0; matrix products, arithmetic and copies ran while one was open for 10% -> 10% of each run, Pallas kernels for 41% -> 42%
where the time goes in v10:
time: 201 us
  Pallas kernels  138 us (69%)
  local copies, waits for them, and re-layouts  24.6 us (12%)
  between operations  15.8 us (8%)
  matrix products  14.1 us (7%)
  other arithmetic  7.51 us (4%)
    pallas_call x3, Pallas kernels, blk_stage(): pl.pallas_call(functools.partial(stage_kernel, n_blk, final, extra), out_...  92.1 us
    pallas_call x1, Pallas kernels, prologue(): pl.pallas_call(functools.partial(prologue_kernel, n_req, n_blk), out_shap...  39.5 us
    unnamed x38, local copies, waits for them, and re-layouts  9.21 us
    pallas_call x1, Pallas kernels, self_attention(): pl.pallas_call(self_kernel, out_shape=jax.ShapeDtypeStruct((n_q, HD), jnp...  6.87 us
  transfers between devices with their start and end apart: 1, of which 0 were waited for; matrix products, arithmetic and copies ran while one was open for 10% of the time, Pallas kernels for 42%

profile of v10, /device:TPU:33, one launch (start us, length us, event | category | flops | bytes accessed | tf_op | source)
XLA Modules:
  0.0 200.6 jit_solution(9630971451047213737)
XLA Ops:
  7.3 0.9 copy.33
  8.3 0.9 copy.34
  9.3 1.0 copy.35
  10.3 0.2 reshape.135
  10.5 0.7 bitcast_dynamic-update-slice_fusion.1
  11.3 0.8 bitcast_dynamic-update-slice_fusion
  12.1 0.7 copy-done.4
  12.8 1.0 convolution_reduce_fusion
  13.8 0.5 slice.95
  14.3 0.6 pad_slice_fusion
  15.0 0.7 concatenate.15
  15.7 0.6 dynamic_slice.12
  16.3 1.3 compare_select_fusion
  17.6 1.4 select_reduce_fusion.1
  20.6 0.1 copy.36
  20.8 0.1 copy.37
  21.1 0.6 gather_fusion
  21.7 1.1 broadcast_select_fusion.ordered_ref
  22.9 0.6 maximum_bitcast_fusion.packed_ref
  23.5 39.5 %shard_map.185 = (bf16[4096,128]{1,0:T(8,128)(2,1)}, bf16[8,256,128]{2,1,0:T(8,128)(2,1)}) custom-call(bf16[8,256,256]{2,1,0:T(8,128)(2,1)} %broadcast_select_fusion.ordered_ref, bf16[256,128]{1,0:T(8,128)(2,1)} %maximum_bitcast_fusion.packed_ref), custom_call_target="tpu_custom_call" | custom-call | tf_op jit(solution)/shard_map/pallas_call | solution.py:660
  63.0 1.5 copy.57
  64.5 0.8 reshape_reshape_reshape.10
  65.4 1.0 reshape_reshape.6
  66.3 1.3 pad_add_fusion.lens_ref
  67.6 0.3 fusion
  67.9 0.6 fusion.44
  68.5 1.7 convolution_convert_fusion.3
  70.4 6.9 %shard_map.186 = bf16[512,64]{1,0:T(8,128)(2,1)S(1)} custom-call(s32[2]{0:T(128)S(1)} %pad_add_fusion.lens_ref, bf16[512,64]{1,0:T(8,128)(2,1)S(1)} %get-tuple-element.22.q_ref, bf16[4096,128]{1,0:T(8,128)(2,1)S(1)} %copy-done.1, bf16[512,64]{1,0:T(8,128)(2,1)S(1)} %get-tuple-element.21.kn_ref, bf16[512,64]{1,0:T(8,128)(2,1)S(1)} %get-tuple-element.20.vn_ref, ...), custom_call_target="tpu_custom_call" | custom-call | tf_op jit(solution)/shard_map/pallas_call | solution.py:381
  77.3 0.7 dynamic-slice_convert_fusion.refs_1_
  78.0 1.4 convolution_convert_fusion.2.refs_0_
  79.3 37.9 %shard_map.187 = (f32[32,1024]{1,0:T(8,128)}, bf16[512,1024]{1,0:T(8,128)(2,1)}) custom-call(bf16[512,1024]{1,0:T(8,128)(2,1)} %convolution_convert_fusion.2.refs_0_, f32[32,1024]{1,0:T(8,128)} %dynamic-slice_convert_fusion.refs_1_, f32[1,1024]{1,0:T(1,128)} %get-tuple-element.25.refs_2_), custom_call_target="tpu_custom_call" | custom-call | tf_op jit(solution)/shard_map/pallas_call | solution.py:314
  117.2 0.6 iota_compare_fusion.2
  117.9 3.3 %reshape.161 = bf16[8,100352]{1,0:T(8,128)(2,1)} reshape(bf16[802816]{0:T(1024)(128)(2,1)} %all-gather.3.cloned.1.call-done) | data formatting | bytes 3211264 | tf_op jit(solution)/shard_map/all_gather | solution.py:392
  121.1 1.7 fusion.41
  122.8 0.8 reshape_reshape_reshape.9
  123.6 0.2 reshape_reshape.7
  123.9 0.1 slice-done.2
  124.0 2.1 %reshape_reshape_reshape.11 = bf16[1024,352]{1,0:T(8,128)(2,1)} reshape(bf16[8,45056]{1,0:T(8,128)(2,1)S(1)} %slice-done.2) | data formatting | bytes 1441792 | tf_op jit(solution)/shard_map/reshape;reshape;reshape | solution.py:773
  126.1 1.9 convolution_convert_fusion.4
  128.0 2.0 fusion.45
  129.9 0.2 fusion.7
  130.1 2.6 %convolution_convert_fusion.1.refs_0_ = bf16[512,1024]{1,0:T(8,128)(2,1)} fusion(f32[512,512]{0,1:T(8,128)S(1)} %get-tuple-element.27, f32[512]{0:T(512)S(1)} %fusion.7, f32[512]{0:T(512)S(1)} %get-tuple-element.26, bf16[8,8,8,128]{3,2,1,0:T(8,128)(2,1)} %bitcast.76, bf16[1,512,2,1,64]{1,4,2,3,0:T(8,128)(2,1)S(1)} %bitcast.75), kind=kOutput, calls=%fused_computation.7 | convolution fusion | flops 102006784 | bytes 2297856 | tf_op jit(solution)/shard_map/dot_general | solution.py:770
  132.7 26.9 %shard_map.188 = (f32[32,1024]{1,0:T(8,128)}, bf16[512,1024]{1,0:T(8,128)(2,1)}) custom-call(bf16[512,1024]{1,0:T(8,128)(2,1)} %convolution_convert_fusion.1.refs_0_, f32[32,1024]{1,0:T(8,128)} %get-tuple-element.12.refs_1_, f32[1,1024]{1,0:T(1,128)} %get-tuple-element.23.refs_2_), custom_call_target="tpu_custom_call" | custom-call | tf_op jit(solution)/shard_map/pallas_call | solution.py:314
  159.6 2.0 %fusion.46 = f32[512,352]{0,1:T(8,128)S(1)} fusion(bf16[512,1024]{1,0:T(8,128)(2,1)} %get-tuple-element.13, bf16[1024,352]{1,0:T(8,128)(2,1)} %reshape_reshape_reshape.11), kind=kOutput, calls=%fused_computation.81 | convolution fusion | flops 369098752 | bytes 2490368 | tf_op jit(solution)/shard_map/dot_general | solution.py:773
  161.7 1.5 convolution_convert_fusion.refs_0_
  163.2 27.3 %shard_map.189 = (f32[32,1024]{1,0:T(8,128)}, bf16[512,1024]{1,0:T(8,128)(2,1)}) custom-call(bf16[512,1024]{1,0:T(8,128)(2,1)} %convolution_convert_fusion.refs_0_, f32[32,1024]{1,0:T(8,128)} %get-tuple-element.14.refs_1_, f32[1,1024]{1,0:T(1,128)} %get-tuple-element.23.refs_2_), custom_call_target="tpu_custom_call" | custom-call | tf_op jit(solution)/shard_map/pallas_call | solution.py:314
  190.5 2.3 %copy.64 = bf16[512,1024]{1,0:T(8,128)(2,1)} copy(bf16[512,1024]{1,0:T(8,128)(2,1)} %get-tuple-element.34) | data formatting | bytes 2097152
  192.8 1.0 copy.65
  (50 shorter events, 1.0 us)
Async XLA Ops:
  7.2 13.9 %copy-start = (bf16[8,256,256]{2,1,0:T(8,128)(2,1)S(1)}, bf16[8,256,256]{2,1,0:T(8,128)(2,1)}, u32[]{:S(2)}) copy-start(bf16[8,256,256]{2,1,0:T(8,128)(2,1)} %param.20) | copy-start | bytes 3145732
  7.2 8.5 %copy-start.9 = (s32[8]{0:T(128)S(1)}, s32[8]{0:T(128)}, u32[]{:S(2)}) copy-start(s32[8]{0:T(128)} %param.21) | copy-start | bytes 100
  7.2 9.1 %copy-start.10 = (s32[8]{0:T(128)S(1)}, s32[8]{0:T(128)}, u32[]{:S(2)}) copy-start(s32[8]{0:T(128)} %param.22) | copy-start | bytes 100
  7.2 10.4 %copy-start.12 = (s32[8]{0:T(128)S(1)}, s32[8]{0:T(128)}, u32[]{:S(2)}) copy-start(s32[8]{0:T(128)} %param.24) | copy-start | bytes 100
  7.2 10.4 %copy-start.11 = (s32[8]{0:T(128)S(1)}, s32[8]{0:T(128)}, u32[]{:S(2)}) copy-start(s32[8]{0:T(128)} %param.23) | copy-start | bytes 100
  7.2 13.4 %copy-start.6 = (bf16[128,64]{0,1:T(8,128)(2,1)S(1)}, bf16[128,64]{0,1:T(8,128)(2,1)}, u32[]{:S(2)}) copy-start(bf16[128,64]{0,1:T(8,128)(2,1)} %param.28) | copy-start | bytes 49156
  7.2 13.6 %copy-start.5 = (bf16[128,2,64]{0,2,1:T(8,128)(2,1)S(1)}, bf16[128,2,64]{0,2,1:T(8,128)(2,1)}, u32[]{:S(2)}) copy-start(bf16[128,2,64]{0,2,1:T(8,128)(2,1)} %param.29) | copy-start | bytes 98308
  7.2 110.6 %all-gather.3.cloned.1.call-start = ((), (), s32[]{:S(2)}) async-start(), calls=%async_computation | async-start | bytes 1806336 | tf_op jit(solution)/shard_map/all_gather | solution.py:392
  12.1 0.7 copy-start.4
  21.1 1.8 copy-start.7
  63.0 4.7 %copy-start.2 = (bf16[512,1024]{1,0:T(8,128)(2,1)S(1)}, bf16[512,1024]{1,0:T(8,128)(2,1)}, u32[]{:S(2)}) copy-start(bf16[512,1024]{1,0:T(8,128)(2,1)} %param.18) | copy-start | bytes 3145732
  64.5 3.5 %copy-start.8 = (f32[3,1024]{1,0:T(4,128)S(1)}, f32[3,1024]{1,0:T(4,128)}, u32[]{:S(2)}) copy-start(f32[3,1024]{1,0:T(4,128)} %param.27) | copy-start | bytes 36868
  68.5 1.9 copy-start.1
  121.1 1.7 slice-start
  122.8 1.2 slice-start.2
  123.6 2.4 %copy-start.3 = (bf16[1024,128]{1,0:T(8,128)(2,1)S(1)}, bf16[1024,128]{1,0:T(8,128)(2,1)}, u32[]{:S(2)}) copy-start(bf16[1024,128]{1,0:T(8,128)(2,1)} %reshape_reshape_reshape.9) | copy-start | bytes 786436
  132.7 29.0 %slice-start.1 = ((bf16[8,100352]{1,0:T(8,128)(2,1)}), bf16[8,22528]{1,0:T(8,128)(2,1)S(1)}, s32[]{:S(2)}) async-start(bf16[8,100352]{1,0:T(8,128)(2,1)} %reshape.161), calls=%async_computation.2 | async-start | bytes 720896 | tf_op jit(solution)/shard_map/slice | solution.py:397
Sparse Core Ops, SparseCore 0:
  12.9 65.6 all-gather.2

commit v11 on v10

--- a/solution.py
+++ b/solution.py
@@ -128,10 +128,10 @@
 def stage_kernel(n_blk, final, extra, *refs):
     if extra:
         (part_ref, resid_ref, gain_ref, packed_ref, res_out, full_ref, wts_ref,
-         recv_a, send_b, recv_b, sems, b_send, b_recv, ag_send, ag_recv, w_send, w_recv) = refs
+         recv_a, send_b, recv_b, x_send, x_recv, b_send, b_recv, ag_send, ag_recv, w_send, w_recv) = refs
     else:
         (part_ref, resid_ref, gain_ref, res_out, full_ref,
-         recv_a, send_b, recv_b, sems, b_send, b_recv, ag_send, ag_recv) = refs
+         recv_a, send_b, recv_b, x_send, x_recv, b_send, b_recv, ag_send, ag_recv) = refs
     me = lax.axis_index("blk")
     req = lax.axis_index("req")
     rows = resid_ref.shape[0]
@@ -151,16 +151,18 @@
         pl.semaphore_signal(barrier, inc=1, device_id=(peer, me), device_id_type=MESH_IDS)
     pl.semaphore_wait(barrier, n_grp + n_req - 1)
     sends = []
-    exchange = pltpu.make_async_remote_copy(
-        src_ref=part_ref.at[pl.ds(pl.multiple_of((1 - c) * half, half), half)],
-        dst_ref=recv_a,
-        send_sem=sems.at[0],
-        recv_sem=sems.at[1],
-        device_id=(req, partner),
-        device_id_type=MESH_IDS,
-    )
-    exchange.start()
-    sends.append(exchange)
+    for k in range(n_grp):
+        grp = lax.rem(g + 1 + k, n_grp)
+        exchange = pltpu.make_async_remote_copy(
+            src_ref=part_ref.at[pl.ds(pl.multiple_of((1 - c) * half + grp * rows, rows), rows)],
+            dst_ref=recv_a.at[grp],
+            send_sem=x_send.at[k],
+            recv_sem=x_recv.at[grp],
+            device_id=(req, partner),
+            device_id_type=MESH_IDS,
+        )
+        exchange.start()
+        sends.append(exchange)
     for k in range(1, n_req):
         peer = lax.rem(req + k, n_req)
         copy = pltpu.make_async_remote_copy(
@@ -173,28 +175,39 @@
         )
         copy.start()
         sends.append(copy)
-    exchange.wait_recv()
-    pair = part_ref[pl.ds(pl.multiple_of(c * half, half), half), :].astype(jnp.float32) + recv_a[
-        ...
-    ].astype(jnp.float32)
-    send_b[...] = pair.astype(send_b.dtype)
-    for k in range(1, n_grp):
-        grp = lax.rem(g + k, n_grp)
-        copy = pltpu.make_async_remote_copy(
-            src_ref=send_b.at[pl.ds(pl.multiple_of(grp * rows, rows), rows)],
-            dst_ref=recv_b.at[g],
-            send_sem=b_send.at[grp],
-            recv_sem=b_recv.at[g],
-            device_id=(req, grp * 2 + c),
-            device_id_type=MESH_IDS,
-        )
-        copy.start()
-        sends.append(copy)
-    total = send_b[pl.ds(pl.multiple_of(g * rows, rows), rows), :].astype(jnp.float32)
+    total = None
+    for k in range(n_grp):
+        grp = lax.rem(g + 1 + k, n_grp)
+        incoming = pltpu.make_async_remote_copy(
+            src_ref=part_ref.at[pl.ds(0, rows)],
+            dst_ref=recv_a.at[grp],
+            send_sem=x_send.at[k],
+            recv_sem=x_recv.at[grp],
+            device_id=(req, partner),
+            device_id_type=MESH_IDS,
+        )
+        incoming.wait_recv()
+        pair = part_ref[pl.ds(pl.multiple_of(c * half + grp * rows, rows), rows), :].astype(
+            jnp.float32
+        ) + recv_a[grp].astype(jnp.float32)
+        if k == n_grp - 1:
+            total = pair
+        else:
+            send_b[grp] = pair.astype(send_b.dtype)
+            copy = pltpu.make_async_remote_copy(
+                src_ref=send_b.at[grp],
+                dst_ref=recv_b.at[g],
+                send_sem=b_send.at[grp],
+                recv_sem=b_recv.at[g],
+                device_id=(req, grp * 2 + c),
+                device_id_type=MESH_IDS,
+            )
+            copy.start()
+            sends.append(copy)
     for k in range(1, n_grp):
         grp = lax.rem(g + n_grp - k, n_grp)
         incoming = pltpu.make_async_remote_copy(
-            src_ref=send_b.at[pl.ds(0, rows)],
+            src_ref=send_b.at[0],
             dst_ref=recv_b.at[grp],
             send_sem=b_send.at[grp],
             recv_sem=b_recv.at[grp],
@@ -296,10 +309,11 @@
     ]
     n_grp = n_blk // 2
     scratch = [
-        pltpu.VMEM((n_grp * rows, width), part.dtype),
-        pltpu.VMEM((n_grp * rows, width), part.dtype),
         pltpu.VMEM((n_grp, rows, width), part.dtype),
-        pltpu.SemaphoreType.DMA((2,)),
+        pltpu.VMEM((n_grp, rows, width), part.dtype),
+        pltpu.VMEM((n_grp, rows, width), part.dtype),
+        pltpu.SemaphoreType.DMA((n_grp,)),
+        pltpu.SemaphoreType.DMA((n_grp,)),
         pltpu.SemaphoreType.DMA((n_grp,)),
         pltpu.SemaphoreType.DMA((n_grp,)),
         pltpu.SemaphoreType.DMA((n_blk,)),

time: 201 us -> 200 us (level)
  no operation moved by 1% of the time
where the time goes in v11:
time: 200 us
  Pallas kernels  137 us (68%)
  local copies, waits for them, and re-layouts  24.6 us (12%)
  between operations  15.8 us (8%)
  matrix products  14.1 us (7%)
  other arithmetic  7.51 us (4%)
    pallas_call x3, Pallas kernels, blk_stage(): pl.pallas_call(functools.partial(stage_kernel, n_blk, final, extra), out_...  91 us
    pallas_call x1, Pallas kernels, prologue(): pl.pallas_call(functools.partial(prologue_kernel, n_req, n_blk), out_shap...  39.5 us
    unnamed x38, local copies, waits for them, and re-layouts  9.21 us
    pallas_call x1, Pallas kernels, self_attention(): pl.pallas_call(self_kernel, out_shape=jax.ShapeDtypeStruct((n_q, HD), jnp...  6.87 us
  transfers between devices with their start and end apart: 1, of which 0 were waited for; matrix products, arithmetic and copies ran while one was open for 10% of the time, Pallas kernels for 42%

profile of v11, /device:TPU:33, one launch (start us, length us, event | category | flops | bytes accessed | tf_op | source)
XLA Modules:
  0.0 199.5 jit_solution(16083379182992919888)
XLA Ops:
  7.3 0.9 copy.33
  8.3 0.9 copy.34
  9.3 1.0 copy.35
  10.3 0.2 reshape.135
  10.5 0.7 bitcast_dynamic-update-slice_fusion.1
  11.3 0.8 bitcast_dynamic-update-slice_fusion
  12.1 0.7 copy-done.4
  12.8 1.0 convolution_reduce_fusion
  13.8 0.5 slice.95
  14.3 0.6 pad_slice_fusion
  15.0 0.7 concatenate.15
  15.7 0.6 dynamic_slice.12
  16.3 1.3 compare_select_fusion
  17.6 1.4 select_reduce_fusion.1
  20.6 0.1 copy.36
  20.8 0.1 copy.37
  21.1 0.6 gather_fusion
  21.7 1.1 broadcast_select_fusion.ordered_ref
  22.9 0.6 maximum_bitcast_fusion.packed_ref
  23.5 39.5 %shard_map.185 = (bf16[4096,128]{1,0:T(8,128)(2,1)}, bf16[8,256,128]{2,1,0:T(8,128)(2,1)}) custom-call(bf16[8,256,256]{2,1,0:T(8,128)(2,1)} %broadcast_select_fusion.ordered_ref, bf16[256,128]{1,0:T(8,128)(2,1)} %maximum_bitcast_fusion.packed_ref), custom_call_target="tpu_custom_call" | custom-call | tf_op jit(solution)/shard_map/pallas_call | solution.py:674
  63.0 1.5 copy.57
  64.5 0.8 reshape_reshape_reshape.10
  65.4 1.0 reshape_reshape.6
  66.3 1.3 pad_add_fusion.lens_ref
  67.6 0.3 fusion
  67.9 0.6 fusion.44
  68.5 1.7 convolution_convert_fusion.3
  70.4 6.9 %shard_map.186 = bf16[512,64]{1,0:T(8,128)(2,1)S(1)} custom-call(s32[2]{0:T(128)S(1)} %pad_add_fusion.lens_ref, bf16[512,64]{1,0:T(8,128)(2,1)S(1)} %get-tuple-element.22.q_ref, bf16[4096,128]{1,0:T(8,128)(2,1)S(1)} %copy-done.1, bf16[512,64]{1,0:T(8,128)(2,1)S(1)} %get-tuple-element.21.kn_ref, bf16[512,64]{1,0:T(8,128)(2,1)S(1)} %get-tuple-element.20.vn_ref, ...), custom_call_target="tpu_custom_call" | custom-call | tf_op jit(solution)/shard_map/pallas_call | solution.py:395
  77.3 0.7 dynamic-slice_convert_fusion.refs_1_
  78.0 1.4 convolution_convert_fusion.2.refs_0_
  79.3 37.4 %shard_map.187 = (f32[32,1024]{1,0:T(8,128)}, bf16[512,1024]{1,0:T(8,128)(2,1)}) custom-call(bf16[512,1024]{1,0:T(8,128)(2,1)} %convolution_convert_fusion.2.refs_0_, f32[32,1024]{1,0:T(8,128)} %dynamic-slice_convert_fusion.refs_1_, f32[1,1024]{1,0:T(1,128)} %get-tuple-element.25.refs_2_), custom_call_target="tpu_custom_call" | custom-call | tf_op jit(solution)/shard_map/pallas_call | solution.py:328
  116.8 0.6 iota_compare_fusion.2
  117.4 3.3 %reshape.161 = bf16[8,100352]{1,0:T(8,128)(2,1)} reshape(bf16[802816]{0:T(1024)(128)(2,1)} %all-gather.3.cloned.1.call-done) | data formatting | bytes 3211264 | tf_op jit(solution)/shard_map/all_gather | solution.py:406
  120.7 1.7 fusion.41
  122.4 0.8 reshape_reshape_reshape.9
  123.2 0.2 reshape_reshape.7
  123.5 0.1 slice-done.2
  123.6 2.1 %reshape_reshape_reshape.11 = bf16[1024,352]{1,0:T(8,128)(2,1)} reshape(bf16[8,45056]{1,0:T(8,128)(2,1)S(1)} %slice-done.2) | data formatting | bytes 1441792 | tf_op jit(solution)/shard_map/reshape;reshape;reshape | solution.py:787
  125.7 1.9 convolution_convert_fusion.4
  127.5 2.0 fusion.45
  129.5 0.2 fusion.7
  129.7 2.6 %convolution_convert_fusion.1.refs_0_ = bf16[512,1024]{1,0:T(8,128)(2,1)} fusion(f32[512,512]{0,1:T(8,128)S(1)} %get-tuple-element.27, f32[512]{0:T(512)S(1)} %fusion.7, f32[512]{0:T(512)S(1)} %get-tuple-element.26, bf16[8,8,8,128]{3,2,1,0:T(8,128)(2,1)} %bitcast.76, bf16[1,512,2,1,64]{1,4,2,3,0:T(8,128)(2,1)S(1)} %bitcast.75), kind=kOutput, calls=%fused_computation.7 | convolution fusion | flops 102006784 | bytes 2297856 | tf_op jit(solution)/shard_map/dot_general | solution.py:784
  132.3 26.6 %shard_map.188 = (f32[32,1024]{1,0:T(8,128)}, bf16[512,1024]{1,0:T(8,128)(2,1)}) custom-call(bf16[512,1024]{1,0:T(8,128)(2,1)} %convolution_convert_fusion.1.refs_0_, f32[32,1024]{1,0:T(8,128)} %get-tuple-element.12.refs_1_, f32[1,1024]{1,0:T(1,128)} %get-tuple-element.23.refs_2_), custom_call_target="tpu_custom_call" | custom-call | tf_op jit(solution)/shard_map/pallas_call | solution.py:328
  158.9 2.0 %fusion.46 = f32[512,352]{0,1:T(8,128)S(1)} fusion(bf16[512,1024]{1,0:T(8,128)(2,1)} %get-tuple-element.13, bf16[1024,352]{1,0:T(8,128)(2,1)} %reshape_reshape_reshape.11), kind=kOutput, calls=%fused_computation.81 | convolution fusion | flops 369098752 | bytes 2490368 | tf_op jit(solution)/shard_map/dot_general | solution.py:787
  160.9 1.5 convolution_convert_fusion.refs_0_
  162.4 27.0 %shard_map.189 = (f32[32,1024]{1,0:T(8,128)}, bf16[512,1024]{1,0:T(8,128)(2,1)}) custom-call(bf16[512,1024]{1,0:T(8,128)(2,1)} %convolution_convert_fusion.refs_0_, f32[32,1024]{1,0:T(8,128)} %get-tuple-element.14.refs_1_, f32[1,1024]{1,0:T(1,128)} %get-tuple-element.23.refs_2_), custom_call_target="tpu_custom_call" | custom-call | tf_op jit(solution)/shard_map/pallas_call | solution.py:328
  189.4 2.3 %copy.64 = bf16[512,1024]{1,0:T(8,128)(2,1)} copy(bf16[512,1024]{1,0:T(8,128)(2,1)} %get-tuple-element.34) | data formatting | bytes 2097152
  191.7 1.0 copy.65
  (50 shorter events, 1.0 us)
Async XLA Ops:
  7.2 13.9 %copy-start = (bf16[8,256,256]{2,1,0:T(8,128)(2,1)S(1)}, bf16[8,256,256]{2,1,0:T(8,128)(2,1)}, u32[]{:S(2)}) copy-start(bf16[8,256,256]{2,1,0:T(8,128)(2,1)} %param.20) | copy-start | bytes 3145732
  7.2 8.5 %copy-start.9 = (s32[8]{0:T(128)S(1)}, s32[8]{0:T(128)}, u32[]{:S(2)}) copy-start(s32[8]{0:T(128)} %param.21) | copy-start | bytes 100
  7.2 9.1 %copy-start.10 = (s32[8]{0:T(128)S(1)}, s32[8]{0:T(128)}, u32[]{:S(2)}) copy-start(s32[8]{0:T(128)} %param.22) | copy-start | bytes 100
  7.2 10.4 %copy-start.12 = (s32[8]{0:T(128)S(1)}, s32[8]{0:T(128)}, u32[]{:S(2)}) copy-start(s32[8]{0:T(128)} %param.24) | copy-start | bytes 100
  7.2 10.4 %copy-start.11 = (s32[8]{0:T(128)S(1)}, s32[8]{0:T(128)}, u32[]{:S(2)}) copy-start(s32[8]{0:T(128)} %param.23) | copy-start | bytes 100
  7.2 13.4 %copy-start.6 = (bf16[128,64]{0,1:T(8,128)(2,1)S(1)}, bf16[128,64]{0,1:T(8,128)(2,1)}, u32[]{:S(2)}) copy-start(bf16[128,64]{0,1:T(8,128)(2,1)} %param.28) | copy-start | bytes 49156
  7.2 13.6 %copy-start.5 = (bf16[128,2,64]{0,2,1:T(8,128)(2,1)S(1)}, bf16[128,2,64]{0,2,1:T(8,128)(2,1)}, u32[]{:S(2)}) copy-start(bf16[128,2,64]{0,2,1:T(8,128)(2,1)} %param.29) | copy-start | bytes 98308
  7.2 110.2 %all-gather.3.cloned.1.call-start = ((), (), s32[]{:S(2)}) async-start(), calls=%async_computation | async-start | bytes 1806336 | tf_op jit(solution)/shard_map/all_gather | solution.py:406
  12.1 0.7 copy-start.4
  21.1 1.8 copy-start.7
  63.0 4.7 %copy-start.2 = (bf16[512,1024]{1,0:T(8,128)(2,1)S(1)}, bf16[512,1024]{1,0:T(8,128)(2,1)}, u32[]{:S(2)}) copy-start(bf16[512,1024]{1,0:T(8,128)(2,1)} %param.18) | copy-start | bytes 3145732
  64.5 3.5 %copy-start.8 = (f32[3,1024]{1,0:T(4,128)S(1)}, f32[3,1024]{1,0:T(4,128)}, u32[]{:S(2)}) copy-start(f32[3,1024]{1,0:T(4,128)} %param.27) | copy-start | bytes 36868
  68.5 1.9 copy-start.1
  120.7 1.7 slice-start
  122.4 1.2 slice-start.2
  123.2 2.4 %copy-start.3 = (bf16[1024,128]{1,0:T(8,128)(2,1)S(1)}, bf16[1024,128]{1,0:T(8,128)(2,1)}, u32[]{:S(2)}) copy-start(bf16[1024,128]{1,0:T(8,128)(2,1)} %reshape_reshape_reshape.9) | copy-start | bytes 786436
  132.3 28.6 %slice-start.1 = ((bf16[8,100352]{1,0:T(8,128)(2,1)}), bf16[8,22528]{1,0:T(8,128)(2,1)S(1)}, s32[]{:S(2)}) async-start(bf16[8,100352]{1,0:T(8,128)(2,1)} %reshape.161), calls=%async_computation.2 | async-start | bytes 720896 | tf_op jit(solution)/shard_map/slice | solution.py:411
Sparse Core Ops, SparseCore 0:
  12.9 65.6 all-gather.2

commit v12 on v11

--- a/solution.py
+++ b/solution.py
@@ -337,6 +337,40 @@
     )(*args)
 
 
+def cross_kernel(len_ref, normed_ref, enc_ref, wq_ref, wkv_ref, wo_ref, out_ref):
+    enc_len = len_ref[0]
+    queries = jnp.dot(normed_ref[...], wq_ref[...], preferred_element_type=jnp.float32).astype(
+        jnp.bfloat16
+    )
+    pair = jnp.dot(enc_ref[...], wkv_ref[...], preferred_element_type=jnp.float32).astype(
+        jnp.bfloat16
+    )
+    keys = pair[:, :HD]
+    values = pair[:, HD:]
+    scores = lax.dot_general(
+        queries, keys, (((1,), (1,)), ((), ())), preferred_element_type=jnp.float32
+    )
+    col = lax.broadcasted_iota(jnp.int32, scores.shape, 1)
+    scores = jnp.where(col < enc_len, scores, NEG_FILL)
+    top = jnp.max(scores, axis=1, keepdims=True)
+    weights = jnp.exp(scores - top)
+    weights = (weights / jnp.sum(weights, axis=1, keepdims=True)).astype(jnp.bfloat16)
+    context = jnp.dot(weights, values, preferred_element_type=jnp.float32).astype(jnp.bfloat16)
+    out_ref[...] = jnp.dot(context, wo_ref[...], preferred_element_type=jnp.float32).astype(
+        out_ref.dtype
+    )
+
+
+def cross_branch(normed, enc, wq, wkv, wo, enc_len):
+    vmem = pl.BlockSpec(memory_space=pltpu.VMEM)
+    return pl.pallas_call(
+        cross_kernel,
+        out_shape=jax.ShapeDtypeStruct((normed.shape[0], wo.shape[1]), jnp.bfloat16),
+        in_specs=[pl.BlockSpec(memory_space=pltpu.SMEM)] + [vmem] * 5,
+        out_specs=vmem,
+    )(enc_len.reshape(1).astype(jnp.int32), normed, enc, wq, wkv, wo)
+
+
 def self_kernel(lens_ref, q_ref, c_ref, kn_ref, vn_ref, g_ref, f_ref, o_ref):
     old_len = lens_ref[0]
     fresh_len = lens_ref[1]
@@ -769,19 +803,14 @@
     part = jnp.dot(context, wo_self, preferred_element_type=jnp.float32).astype(jnp.bfloat16)
     residual, normed = blk_stage(part, own_rows, norm_gain[1], False)
     wq_cross, wkv_cross, wo_cross, w_in, w_out = late_gathered
-    queries = (
-        jnp.dot(normed, wq_cross, preferred_element_type=jnp.float32)
-        .astype(jnp.bfloat16)
-        .reshape(req_dev, -1, heads_dev, HD)
-    )
-    cross_pair = wkv_cross.reshape(wkv_cross.shape[0], -1)
-    key_value = (
-        jnp.dot(encoder_out, cross_pair, preferred_element_type=jnp.float32)
-        .astype(jnp.bfloat16)
-        .reshape(req_dev, -1, 2, heads_dev, HD)
-    )
-    context = cross_attend(queries, key_value, slot_enc)
-    part = jnp.dot(context.reshape(-1, width_dev), wo_cross, preferred_element_type=jnp.float32)
+    part = cross_branch(
+        normed,
+        encoder_out,
+        wq_cross,
+        wkv_cross.reshape(wkv_cross.shape[0], -1),
+        wo_cross,
+        slot_enc[0],
+    )
     residual, normed = blk_stage(part.astype(jnp.bfloat16), residual, norm_gain[2], False)
     ff_dev = w_in.shape[2]
     gate_up = jnp.dot(normed, w_in.reshape(w_in.shape[0], -1), preferred_element_type=jnp.float32)

time: 200 us -> 200 us (level)
  matrix products: 14.1 us -> 7.45 us
  Pallas kernels: 137 us -> 143 us
    dot_general x3 -> x0, matrix products: 6.43 us -> none  [the longest x1 2.59 us: per_device(): jnp.dot(context.reshape(-1, width_dev), wo_cross, preferred_element_type=...]
    pallas_call x0 -> x1, Pallas kernels: none -> 5.45 us  [cross_branch(): pl.pallas_call(cross_kernel, out_shape=jax.ShapeDtypeStruct((normed.shape...]
    unnamed x38 -> x39, local copies, waits for them, and re-layouts: 9.21 us -> 9.88 us
where the time goes in v12:
time: 200 us; the launch traced here: 199 us
  Pallas kernels  143 us (72%)
  local copies, waits for them, and re-layouts  25.3 us (13%)
  between operations  15.8 us (8%)
  other arithmetic  7.99 us (4%)
  matrix products  7.45 us (4%)
    pallas_call x3, Pallas kernels, blk_stage(): pl.pallas_call(functools.partial(stage_kernel, n_blk, final, extra), out_...  91 us
    pallas_call x1, Pallas kernels, prologue(): pl.pallas_call(functools.partial(prologue_kernel, n_req, n_blk), out_shap...  39.5 us
    unnamed x39, local copies, waits for them, and re-layouts  9.88 us
    pallas_call x1, Pallas kernels, self_attention(): pl.pallas_call(self_kernel, out_shape=jax.ShapeDtypeStruct((n_q, HD), jnp...  6.88 us
    pallas_call x1, Pallas kernels, cross_branch(): pl.pallas_call(cross_kernel, out_shape=jax.ShapeDtypeStruct((normed.shape...  5.45 us
  transfers between devices with their start and end apart: 1, of which 0 were waited for; matrix products, arithmetic and copies ran while one was open for 10% of the time, Pallas kernels for 42%

profile of v12, /device:TPU:33, one launch (start us, length us, event | category | flops | bytes accessed | tf_op | source)
XLA Modules:
  0.0 199.5 jit_solution(4856968162576214158)
XLA Ops:
  7.3 0.9 copy.36
  8.3 0.9 copy.37
  9.2 0.1 reshape.93
  9.3 1.0 copy.38
  10.3 0.2 reshape.95
  10.5 0.7 bitcast_dynamic-update-slice_fusion.1
  11.3 0.8 bitcast_dynamic-update-slice_fusion
  12.1 0.7 copy-done.4
  12.8 1.0 convolution_reduce_fusion
  13.8 0.5 slice.85
  14.3 0.6 pad_slice_fusion
  15.0 0.7 concatenate.14
  15.7 0.7 dynamic_slice.12
  16.3 1.3 select_reduce_fusion.1
  19.1 1.3 compare_select_fusion
  20.6 0.1 copy.33
  20.9 0.1 copy.34
  21.0 0.1 reshape.85
  21.1 0.6 gather_fusion
  21.7 1.1 broadcast_select_fusion.ordered_ref
  22.9 0.6 maximum_bitcast_fusion.packed_ref
  23.5 39.5 %shard_map.185 = (bf16[4096,128]{1,0:T(8,128)(2,1)}, bf16[8,256,128]{2,1,0:T(8,128)(2,1)}) custom-call(bf16[8,256,256]{2,1,0:T(8,128)(2,1)} %broadcast_select_fusion.ordered_ref, bf16[256,128]{1,0:T(8,128)(2,1)} %maximum_bitcast_fusion.packed_ref), custom_call_target="tpu_custom_call" | custom-call | tf_op jit(solution)/shard_map/pallas_call | solution.py:708
  63.0 1.5 copy.54
  64.5 0.8 reshape_reshape_reshape.9
  65.4 1.0 reshape_reshape.6
  66.3 1.3 pad_add_fusion.lens_ref
  67.7 0.3 fusion
  68.0 0.6 fusion.36
  68.6 1.7 convolution_convert_fusion.2
  70.3 0.1 fusion.35
  70.4 6.9 %shard_map.186 = bf16[512,64]{1,0:T(8,128)(2,1)S(1)} custom-call(s32[2]{0:T(128)S(1)} %pad_add_fusion.lens_ref, bf16[512,64]{1,0:T(8,128)(2,1)S(1)} %get-tuple-element.22.q_ref, bf16[4096,128]{1,0:T(8,128)(2,1)S(1)} %copy-done.1, bf16[512,64]{1,0:T(8,128)(2,1)S(1)} %get-tuple-element.21.kn_ref, bf16[512,64]{1,0:T(8,128)(2,1)S(1)} %get-tuple-element.20.vn_ref, ...), custom_call_target="tpu_custom_call" | custom-call | tf_op jit(solution)/shard_map/pallas_call | solution.py:429
  77.3 0.7 dynamic-slice_convert_fusion.refs_1_
  78.0 1.4 convolution_convert_fusion.1.refs_0_
  79.4 37.4 %shard_map.187 = (f32[32,1024]{1,0:T(8,128)}, bf16[512,1024]{1,0:T(8,128)(2,1)}) custom-call(bf16[512,1024]{1,0:T(8,128)(2,1)} %convolution_convert_fusion.1.refs_0_, f32[32,1024]{1,0:T(8,128)} %dynamic-slice_convert_fusion.refs_1_, f32[1,1024]{1,0:T(1,128)} %get-tuple-element.25.refs_2_), custom_call_target="tpu_custom_call" | custom-call | tf_op jit(solution)/shard_map/pallas_call | solution.py:328
  116.8 1.3 select_reduce_fusion.2
  118.1 3.2 %reshape.109 = bf16[8,100352]{1,0:T(8,128)(2,1)} reshape(bf16[802816]{0:T(1024)(128)(2,1)} %all-gather.3.cloned.1.call-done) | data formatting | bytes 3211264 | tf_op jit(solution)/shard_map/all_gather | solution.py:440
  121.3 1.0 fusion.33
  122.4 0.8 reshape_reshape_reshape.10.wkv_ref
  123.2 0.7 copy.55
  123.9 1.0 reshape_reshape.7.wq_ref
  124.9 2.1 %reshape_reshape_reshape.11 = bf16[1024,352]{1,0:T(8,128)(2,1)} reshape(bf16[8,45056]{1,0:T(8,128)(2,1)S(1)} %slice-done.2) | data formatting | bytes 1441792 | tf_op jit(solution)/shard_map/reshape;reshape;reshape | solution.py:816
  126.9 5.4 %shard_map.188.refs_0_ = bf16[512,1024]{1,0:T(8,128)(2,1)} custom-call(s32[1]{0:T(128)} %bitcast.1.len_ref, bf16[512,1024]{1,0:T(8,128)(2,1)} %get-tuple-element.11.normed_ref, bf16[512,1024]{1,0:T(8,128)(2,1)} %enc_ref.1, bf16[1024,64]{1,0:T(8,128)(2,1)} %reshape_reshape.7.wq_ref, bf16[1024,128]{1,0:T(8,128)(2,1)} %reshape_reshape_reshape.10.wkv_ref, ...), custom_call_target="tpu_custom_call" | custom-call | tf_op jit(solution)/shard_map/pallas_call | solution.py:366
  132.4 26.6 %shard_map.189 = (f32[32,1024]{1,0:T(8,128)}, bf16[512,1024]{1,0:T(8,128)(2,1)}) custom-call(bf16[512,1024]{1,0:T(8,128)(2,1)} %shard_map.188.refs_0_, f32[32,1024]{1,0:T(8,128)} %get-tuple-element.12.refs_1_, f32[1,1024]{1,0:T(1,128)} %get-tuple-element.23.refs_2_), custom_call_target="tpu_custom_call" | custom-call | tf_op jit(solution)/shard_map/pallas_call | solution.py:328
  159.0 1.8 fusion.37
  160.8 1.5 convolution_convert_fusion.refs_0_
  162.3 27.1 %shard_map.190 = (f32[32,1024]{1,0:T(8,128)}, bf16[512,1024]{1,0:T(8,128)(2,1)}) custom-call(bf16[512,1024]{1,0:T(8,128)(2,1)} %convolution_convert_fusion.refs_0_, f32[32,1024]{1,0:T(8,128)} %get-tuple-element.14.refs_1_, f32[1,1024]{1,0:T(1,128)} %get-tuple-element.23.refs_2_), custom_call_target="tpu_custom_call" | custom-call | tf_op jit(solution)/shard_map/pallas_call | solution.py:328
  189.4 2.3 %copy.62 = bf16[512,1024]{1,0:T(8,128)(2,1)} copy(bf16[512,1024]{1,0:T(8,128)(2,1)} %get-tuple-element.30) | data formatting | bytes 2097152
  191.7 1.0 copy.63
  (48 shorter events, 0.7 us)
Async XLA Ops:
  7.2 13.9 %copy-start = (bf16[8,256,256]{2,1,0:T(8,128)(2,1)S(1)}, bf16[8,256,256]{2,1,0:T(8,128)(2,1)}, u32[]{:S(2)}) copy-start(bf16[8,256,256]{2,1,0:T(8,128)(2,1)} %param.20) | copy-start | bytes 3145732
  7.2 8.5 %copy-start.9 = (s32[8]{0:T(128)S(1)}, s32[8]{0:T(128)}, u32[]{:S(2)}) copy-start(s32[8]{0:T(128)} %param.21) | copy-start | bytes 100
  7.2 9.1 %copy-start.11 = (s32[8]{0:T(128)S(1)}, s32[8]{0:T(128)}, u32[]{:S(2)}) copy-start(s32[8]{0:T(128)} %param.23) | copy-start | bytes 100
  7.2 11.9 %copy-start.10 = (s32[8]{0:T(128)S(1)}, s32[8]{0:T(128)}, u32[]{:S(2)}) copy-start(s32[8]{0:T(128)} %param.22) | copy-start | bytes 100
  7.2 13.4 %copy-start.6 = (bf16[128,64]{0,1:T(8,128)(2,1)S(1)}, bf16[128,64]{0,1:T(8,128)(2,1)}, u32[]{:S(2)}) copy-start(bf16[128,64]{0,1:T(8,128)(2,1)} %param.28) | copy-start | bytes 49156
  7.2 13.6 %copy-start.5 = (bf16[128,2,64]{0,2,1:T(8,128)(2,1)S(1)}, bf16[128,2,64]{0,2,1:T(8,128)(2,1)}, u32[]{:S(2)}) copy-start(bf16[128,2,64]{0,2,1:T(8,128)(2,1)} %param.29) | copy-start | bytes 98308
  7.2 110.9 %all-gather.3.cloned.1.call-start = ((), (), s32[]{:S(2)}) async-start(), calls=%async_computation | async-start | bytes 1806336 | tf_op jit(solution)/shard_map/all_gather | solution.py:440
  12.1 0.7 copy-start.4
  21.1 1.8 copy-start.7
  63.0 4.7 %copy-start.3 = (bf16[512,1024]{1,0:T(8,128)(2,1)S(1)}, bf16[512,1024]{1,0:T(8,128)(2,1)}, u32[]{:S(2)}) copy-start(bf16[512,1024]{1,0:T(8,128)(2,1)} %param.18) | copy-start | bytes 3145732
  64.5 3.5 %copy-start.8 = (f32[3,1024]{1,0:T(4,128)S(1)}, f32[3,1024]{1,0:T(4,128)}, u32[]{:S(2)}) copy-start(f32[3,1024]{1,0:T(4,128)} %param.27) | copy-start | bytes 36868
  68.6 1.9 copy-start.1
  77.3 39.5 %copy-start.12 = (s32[8]{0:T(128)S(1)}, s32[8]{0:T(128)}, u32[]{:S(2)}) copy-start(s32[8]{0:T(128)} %param.24) | copy-start | bytes 100
  121.3 1.1 slice-start
  122.4 2.5 %slice-start.2 = ((bf16[8,100352]{1,0:T(8,128)(2,1)}), bf16[8,45056]{1,0:T(8,128)(2,1)S(1)}, s32[]{:S(2)}) async-start(bf16[8,100352]{1,0:T(8,128)(2,1)} %reshape.109), calls=%async_computation.3 | async-start | bytes 1441792 | tf_op jit(solution)/shard_map/slice | solution.py:445
  126.9 32.0 %copy-start.2 = (bf16[1024,352]{1,0:T(8,128)(2,1)S(1)}, bf16[1024,352]{1,0:T(8,128)(2,1)}, u32[]{:S(2)}) copy-start(bf16[1024,352]{1,0:T(8,128)(2,1)} %reshape_reshape_reshape.11) | copy-start | bytes 2162692
  132.4 28.4 %slice-start.1 = ((bf16[8,100352]{1,0:T(8,128)(2,1)}), bf16[8,22528]{1,0:T(8,128)(2,1)S(1)}, s32[]{:S(2)}) async-start(bf16[8,100352]{1,0:T(8,128)(2,1)} %reshape.109), calls=%async_computation.2 | async-start | bytes 720896 | tf_op jit(solution)/shard_map/slice | solution.py:445
Sparse Core Ops, SparseCore 0:
  12.9 65.4 all-gather.2

commit v13 on v11

--- a/solution.py
+++ b/solution.py
@@ -337,6 +337,92 @@
     )(*args)
 
 
+def cross_kernel(n_req, spans, len_ref, normed_ref, enc_ref, w_ref, out_ref):
+    enc_len = len_ref[0]
+    (q_at, q_len), (kv_at, kv_len), (o_at, o_len) = spans
+    nt = (((1,), (1,)), ((), ()))
+    width = w_ref.shape[2]
+    queries = None
+    pair = None
+    for r in range(n_req):
+        cols = slice(r * width, (r + 1) * width)
+        term = lax.dot_general(
+            normed_ref[:, cols], w_ref[r, q_at : q_at + q_len, :], nt,
+            preferred_element_type=jnp.float32,
+        )
+        queries = term if queries is None else queries + term
+        term = lax.dot_general(
+            enc_ref[:, cols], w_ref[r, kv_at : kv_at + kv_len, :], nt,
+            preferred_element_type=jnp.float32,
+        )
+        pair = term if pair is None else pair + term
+    queries = queries.astype(jnp.bfloat16)
+    pair = pair.astype(jnp.bfloat16)
+    keys = pair[:, :HD]
+    values = pair[:, HD:]
+    scores = lax.dot_general(queries, keys, nt, preferred_element_type=jnp.float32)
+    col = lax.broadcasted_iota(jnp.int32, scores.shape, 1)
+    scores = jnp.where(col < enc_len, scores, NEG_FILL)
+    top = jnp.max(scores, axis=1, keepdims=True)
+    weights = jnp.exp(scores - top)
+    weights = (weights / jnp.sum(weights, axis=1, keepdims=True)).astype(jnp.bfloat16)
+    context = jnp.dot(weights, values, preferred_element_type=jnp.float32).astype(jnp.bfloat16)
+    for r in range(n_req):
+        out_ref[:, r * width : (r + 1) * width] = jnp.dot(
+            context, w_ref[r, o_at : o_at + o_len, :], preferred_element_type=jnp.float32
+        ).astype(out_ref.dtype)
+
+
+def ffn_kernel(n_req, spans, normed_ref, w_ref, out_ref):
+    (i_at, i_len), (o_at, o_len) = spans
+    nt = (((1,), (1,)), ((), ()))
+    width = w_ref.shape[2]
+    ff_dev = o_len
+    gate_up = None
+    for r in range(n_req):
+        term = lax.dot_general(
+            normed_ref[:, r * width : (r + 1) * width], w_ref[r, i_at : i_at + i_len, :], nt,
+            preferred_element_type=jnp.float32,
+        )
+        gate_up = term if gate_up is None else gate_up + term
+    hidden = (jax.nn.gelu(gate_up[:, :ff_dev], approximate=True) * gate_up[:, ff_dev:]).astype(
+        jnp.bfloat16
+    )
+    for r in range(n_req):
+        out_ref[:, r * width : (r + 1) * width] = jnp.dot(
+            hidden, w_ref[r, o_at : o_at + o_len, :], preferred_element_type=jnp.float32
+        ).astype(out_ref.dtype)
+
+
+def block_spans(pieces):
+    spans, at = [], 0
+    for w, axis in pieces:
+        rows = w.size // w.shape[0] if axis == 0 else w.shape[0]
+        spans.append((at, rows))
+        at += rows
+    return spans
+
+
+def cross_branch(normed, enc, blocks, spans, enc_len):
+    vmem = pl.BlockSpec(memory_space=pltpu.VMEM)
+    return pl.pallas_call(
+        functools.partial(cross_kernel, blocks.shape[0], tuple(spans)),
+        out_shape=jax.ShapeDtypeStruct(normed.shape, jnp.bfloat16),
+        in_specs=[pl.BlockSpec(memory_space=pltpu.SMEM)] + [vmem] * 3,
+        out_specs=vmem,
+    )(enc_len.reshape(1).astype(jnp.int32), normed, enc, blocks)
+
+
+def ffn_branch(normed, blocks, spans):
+    vmem = pl.BlockSpec(memory_space=pltpu.VMEM)
+    return pl.pallas_call(
+        functools.partial(ffn_kernel, blocks.shape[0], tuple(spans)),
+        out_shape=jax.ShapeDtypeStruct(normed.shape, jnp.bfloat16),
+        in_specs=[vmem] * 2,
+        out_specs=vmem,
+    )(normed, blocks)
+
+
 def self_kernel(lens_ref, q_ref, c_ref, kn_ref, vn_ref, g_ref, f_ref, o_ref):
     old_len = lens_ref[0]
     fresh_len = lens_ref[1]
@@ -703,6 +789,15 @@
         shape[axis] *= n_req
         out.append(part.reshape(shape))
     return out
+
+
+def lane_pack(pieces):
+    blocks = []
+    for w, axis in pieces:
+        flat = w.reshape(w.shape[0], -1)
+        blocks.append(flat.T if axis == 0 else flat)
+    packed = jnp.concatenate(blocks, axis=0)
+    return lax.all_gather(packed, "req", axis=0, tiled=False)
 
 
 def per_device(
@@ -745,7 +840,7 @@
     cache_blk, whole = prologue(ordered, flat.reshape(-1, 128))
     cache_dec = cache_blk[None]
     gathered = unpack(whole, early)
-    late_gathered = pack_gather(late)
+    late_blocks = lane_pack(late)
     wq_self, wkv_self, wo_self = gathered
     n_blk = lax.axis_size("blk")
     rows_dev = new_states.shape[0] // n_blk
@@ -768,27 +863,10 @@
     )
     part = jnp.dot(context, wo_self, preferred_element_type=jnp.float32).astype(jnp.bfloat16)
     residual, normed = blk_stage(part, own_rows, norm_gain[1], False)
-    wq_cross, wkv_cross, wo_cross, w_in, w_out = late_gathered
-    queries = (
-        jnp.dot(normed, wq_cross, preferred_element_type=jnp.float32)
-        .astype(jnp.bfloat16)
-        .reshape(req_dev, -1, heads_dev, HD)
-    )
-    cross_pair = wkv_cross.reshape(wkv_cross.shape[0], -1)
-    key_value = (
-        jnp.dot(encoder_out, cross_pair, preferred_element_type=jnp.float32)
-        .astype(jnp.bfloat16)
-        .reshape(req_dev, -1, 2, heads_dev, HD)
-    )
-    context = cross_attend(queries, key_value, slot_enc)
-    part = jnp.dot(context.reshape(-1, width_dev), wo_cross, preferred_element_type=jnp.float32)
+    spans = block_spans(late)
+    part = cross_branch(normed, encoder_out, late_blocks, spans[:3], slot_enc[0])
     residual, normed = blk_stage(part.astype(jnp.bfloat16), residual, norm_gain[2], False)
-    ff_dev = w_in.shape[2]
-    gate_up = jnp.dot(normed, w_in.reshape(w_in.shape[0], -1), preferred_element_type=jnp.float32)
-    hidden = (jax.nn.gelu(gate_up[:, :ff_dev], approximate=True) * gate_up[:, ff_dev:]).astype(
-        jnp.bfloat16
-    )
-    part = jnp.dot(hidden, w_out, preferred_element_type=jnp.float32).astype(jnp.bfloat16)
+    part = ffn_branch(normed, late_blocks, spans[3:])
     _, layer_out = blk_stage(part, residual, norm_gain[2], True)
     return (layer_out, cache_dec)
 

time: 200 us -> 195 us (0.975)
  matrix products: 14.1 us -> 4.14 us
  Pallas kernels: 137 us -> 146 us
  local copies, waits for them, and re-layouts: 24.6 us -> 17.8 us
  other arithmetic: 7.51 us -> 9.93 us
    pallas_call x0 -> x2, Pallas kernels: none -> 10.5 us  [the longest x1 5.63 us: cross_branch(): pl.pallas_call(functools.partial(cross_kernel, blocks.shape[0], tuple(spa...]
    dot_general x5 -> x0, matrix products: 9.96 us -> none  [the longest x1 2.59 us: per_device(): jnp.dot(context.reshape(-1, width_dev), wo_cross, preferred_element_type=...]
    all_gather x1 -> x0, local copies, waits for them, and re-layouts: 3.25 us -> none  [pack_gather(): whole = lax.all_gather(flat, 'req', axis=0, tiled=False)]
    another operation x3 -> x0, local copies, waits for them, and re-layouts: 3.14 us -> none  [the longest x1 2.07 us: per_device(): w_in.reshape(w_in.shape[0], -1)]
    unnamed x38 -> x23, local copies, waits for them, and re-layouts: 9.21 us -> 10.3 us
  transfers between devices with their start and end apart: 1 -> 1, of which waited for: 0 -> 0; matrix products, arithmetic and copies ran while one was open for 10% -> 12% of each run, Pallas kernels for 42% -> 42%
where the time goes in v13:
time: 195 us; the launch traced here: 194 us
  Pallas kernels  146 us (75%)
  local copies, waits for them, and re-layouts  17.8 us (9%)
  between operations  15.6 us (8%)
  other arithmetic  9.93 us (5%)
  matrix products  4.14 us (2%)
    pallas_call x3, Pallas kernels, blk_stage(): pl.pallas_call(functools.partial(stage_kernel, n_blk, final, extra), out_...  90 us
    pallas_call x1, Pallas kernels, prologue(): pl.pallas_call(functools.partial(prologue_kernel, n_req, n_blk), out_shap...  39 us
    unnamed x23, local copies, waits for them, and re-layouts  10.3 us
    pallas_call x1, Pallas kernels, self_attention(): pl.pallas_call(self_kernel, out_shape=jax.ShapeDtypeStruct((n_q, HD), jnp...  6.83 us
    pallas_call x1, Pallas kernels, cross_branch(): pl.pallas_call(functools.partial(cross_kernel, blocks.shape[0], tuple(spa...  5.63 us
    pallas_call x1, Pallas kernels, ffn_branch(): pl.pallas_call(functools.partial(ffn_kernel, blocks.shape[0], tuple(spans...  4.86 us
  transfers between devices with their start and end apart: 1, of which 0 were waited for; matrix products, arithmetic and copies ran while one was open for 12% of the time, Pallas kernels for 42%

profile of v13, /device:TPU:33, one launch (start us, length us, event | category | flops | bytes accessed | tf_op | source)
XLA Modules:
  0.0 194.0 jit_solution(13779368059614503554)
XLA Ops:
  7.2 0.0 copy-start
  7.2 0.0 all-gather.3.cloned.1.call-start
  7.2 0.8 bitcast_dynamic-update-slice_fusion
  8.0 0.8 constant_dynamic-update-slice_fusion.3
  8.8 0.7 constant_dynamic-update-slice_fusion.2
  9.5 0.9 constant_dynamic-update-slice_fusion.1
  10.4 0.8 constant_dynamic-update-slice_fusion
  11.2 0.7 copy-done.3
  11.9 0.0 all-gather.3.cloned.1.call-update
  11.9 1.0 convolution_reduce_fusion
  13.0 0.5 slice.57
  13.5 0.6 concatenate.14
  14.1 0.7 pad_slice_fusion
  14.8 0.1 rev.3
  14.9 0.7 compare_and_fusion
  15.6 1.3 dynamic_slice.12
  16.9 2.0 %select_reduce_fusion.1 = s32[]{:T(128)} fusion(s32[8]{0:T(128)} %param.23, s32[]{:T(128)} %bitcast), kind=kLoop, calls=%fused_computation.34 | loop fusion | flops 23 | bytes 40 | tf_op jit(solution)/shard_map/reduce_sum | solution.py:31
  20.3 0.1 dynamic_slice.14
  20.4 0.1 slice.46
  20.4 1.9 %compare_select_fusion = (s32[8]{0:T(128)S(1)}, s32[]{:T(128)}) fusion(s32[8]{0:T(128)} %param.21, s32[8]{0:T(128)} %param.22, s32[]{:T(128)} %bitcast), kind=kLoop, calls=%fused_computation.29 | loop fusion | flops 47 | bytes 104 | tf_op jit(solution)/shard_map/jit(_take)/jit(_where)/select_n | solution.py:831
  22.4 0.9 copy.25
  23.3 0.1 reshape.64
  23.4 0.8 copy.24
  24.2 0.1 reshape.63
  24.3 0.6 gather_fusion
  24.9 1.1 broadcast_select_fusion.ordered_ref
  26.1 0.6 maximum_bitcast_fusion.packed_ref
  26.7 39.0 %shard_map.185 = (bf16[4096,128]{1,0:T(8,128)(2,1)}, bf16[8,256,128]{2,1,0:T(8,128)(2,1)}) custom-call(bf16[8,256,256]{2,1,0:T(8,128)(2,1)} %broadcast_select_fusion.ordered_ref, bf16[256,128]{1,0:T(8,128)(2,1)} %maximum_bitcast_fusion.packed_ref), custom_call_target="tpu_custom_call" | custom-call | tf_op jit(solution)/shard_map/pallas_call | solution.py:760
  65.8 1.5 copy.35
  67.2 0.0 copy-start.5
  67.3 1.0 reshape_reshape.3
  68.3 0.8 reshape_reshape_reshape.3
  69.1 1.3 pad_add_fusion.lens_ref
  70.4 0.3 fusion
  70.7 0.6 fusion.15
  71.3 1.7 convolution_convert_fusion.1
  73.0 0.1 fusion.14
  73.2 6.8 %shard_map.186 = bf16[512,64]{1,0:T(8,128)(2,1)S(1)} custom-call(s32[2]{0:T(128)S(1)} %pad_add_fusion.lens_ref, bf16[512,64]{1,0:T(8,128)(2,1)S(1)} %get-tuple-element.20.q_ref, bf16[4096,128]{1,0:T(8,128)(2,1)S(1)} %copy-done.1, bf16[512,64]{1,0:T(8,128)(2,1)S(1)} %get-tuple-element.19.kn_ref, bf16[512,64]{1,0:T(8,128)(2,1)S(1)} %get-tuple-element.18.vn_ref, ...), custom_call_target="tpu_custom_call" | custom-call | tf_op jit(solution)/shard_map/pallas_call | solution.py:481
  80.0 0.7 dynamic-slice_convert_fusion.refs_1_
  80.7 1.4 convolution_convert_fusion.refs_0_
  82.1 36.3 %shard_map.187 = (f32[32,1024]{1,0:T(8,128)}, bf16[512,1024]{1,0:T(8,128)(2,1)}) custom-call(bf16[512,1024]{1,0:T(8,128)(2,1)} %convolution_convert_fusion.refs_0_, f32[32,1024]{1,0:T(8,128)} %dynamic-slice_convert_fusion.refs_1_, f32[1,1024]{1,0:T(1,128)} %get-tuple-element.23.refs_2_), custom_call_target="tpu_custom_call" | custom-call | tf_op jit(solution)/shard_map/pallas_call | solution.py:328
  118.4 1.3 select_reduce_fusion.2
  119.6 5.6 %shard_map.188.refs_0_ = bf16[512,1024]{1,0:T(8,128)(2,1)} custom-call(s32[1]{0:T(128)} %bitcast.1.len_ref, bf16[512,1024]{1,0:T(8,128)(2,1)} %get-tuple-element.11.normed_ref, bf16[512,1024]{1,0:T(8,128)(2,1)} %enc_ref.1, bf16[8,784,128]{2,1,0:T(8,128)(2,1)} %bitcast.35), custom_call_target="tpu_custom_call" | custom-call | tf_op jit(solution)/shard_map/pallas_call | solution.py:408
  125.3 27.3 %shard_map.189 = (f32[32,1024]{1,0:T(8,128)}, bf16[512,1024]{1,0:T(8,128)(2,1)}) custom-call(bf16[512,1024]{1,0:T(8,128)(2,1)} %shard_map.188.refs_0_, f32[32,1024]{1,0:T(8,128)} %get-tuple-element.12.refs_1_, f32[1,1024]{1,0:T(1,128)} %get-tuple-element.21.refs_2_), custom_call_target="tpu_custom_call" | custom-call | tf_op jit(solution)/shard_map/pallas_call | solution.py:328
  152.5 4.9 %shard_map.190.refs_0_ = bf16[512,1024]{1,0:T(8,128)(2,1)} custom-call(bf16[512,1024]{1,0:T(8,128)(2,1)} %get-tuple-element.13.normed_ref, bf16[8,784,128]{2,1,0:T(8,128)(2,1)} %bitcast.36), custom_call_target="tpu_custom_call" | custom-call | tf_op jit(solution)/shard_map/pallas_call | solution.py:418
  157.4 26.5 %shard_map.191 = (f32[32,1024]{1,0:T(8,128)}, bf16[512,1024]{1,0:T(8,128)(2,1)}) custom-call(bf16[512,1024]{1,0:T(8,128)(2,1)} %shard_map.190.refs_0_, f32[32,1024]{1,0:T(8,128)} %get-tuple-element.14.refs_1_, f32[1,1024]{1,0:T(1,128)} %get-tuple-element.21.refs_2_), custom_call_target="tpu_custom_call" | custom-call | tf_op jit(solution)/shard_map/pallas_call | solution.py:328
  183.9 2.3 %copy.42 = bf16[512,1024]{1,0:T(8,128)(2,1)} copy(bf16[512,1024]{1,0:T(8,128)(2,1)} %get-tuple-element.28) | data formatting | bytes 2097152
  186.1 1.0 copy.43
  (17 shorter events, 0.1 us)
Async XLA Ops:
  7.2 17.1 %copy-start = (bf16[8,256,256]{2,1,0:T(8,128)(2,1)S(1)}, bf16[8,256,256]{2,1,0:T(8,128)(2,1)}, u32[]{:S(2)}) copy-start(bf16[8,256,256]{2,1,0:T(8,128)(2,1)} %param.20) | copy-start | bytes 3145732
  7.2 112.5 %all-gather.3.cloned.1.call-start = ((), (), s32[]{:S(2)}) async-start(), calls=%async_computation | async-start | bytes 1806336 | tf_op jit(solution)/shard_map/all_gather | solution.py:800
  11.2 0.7 copy-start.3
  24.3 1.8 copy-start.4
  65.7 4.7 %copy-start.2 = (bf16[512,1024]{1,0:T(8,128)(2,1)S(1)}, bf16[512,1024]{1,0:T(8,128)(2,1)}, u32[]{:S(2)}) copy-start(bf16[512,1024]{1,0:T(8,128)(2,1)} %param.18) | copy-start | bytes 3145732
  67.2 3.5 %copy-start.5 = (f32[3,1024]{1,0:T(4,128)S(1)}, f32[3,1024]{1,0:T(4,128)}, u32[]{:S(2)}) copy-start(f32[3,1024]{1,0:T(4,128)} %param.27) | copy-start | bytes 36868
  71.3 1.9 copy-start.1
  80.0 38.4 %copy-start.6 = (s32[8]{0:T(128)S(1)}, s32[8]{0:T(128)}, u32[]{:S(2)}) copy-start(s32[8]{0:T(128)} %param.24) | copy-start | bytes 100
Sparse Core Ops, SparseCore 0:
  12.0 65.6 all-gather.2

commit v14 on v13

--- a/solution.py
+++ b/solution.py
@@ -824,10 +824,10 @@
     heads_dev = H // blk_count
     width_dev = heads_dev * HD
     req_dev = cache_in.shape[0] // lax.axis_size("req")
-    own_slots = lax.dynamic_slice_in_dim(slot_order, lax.axis_index("req") * req_dev, req_dev, 0)
-    slot_new = pick_lengths(new_lengths, own_slots)
-    slot_old = pick_lengths(cache_lengths, own_slots)
-    slot_enc = pick_lengths(enc_lengths, own_slots)
+    own_slot = lax.dynamic_index_in_dim(slot_order, lax.axis_index("req"), 0, keepdims=False)
+    tables = jnp.stack([new_lengths, cache_lengths, enc_lengths])
+    picked = lax.dynamic_slice_in_dim(tables, own_slot, 1, 1)
+    slot_new, slot_old, slot_enc = picked[0], picked[1], picked[2]
     ordered = jnp.take(cache_in, slot_order, axis=0)
     onehot = (bucket_of[:, None] == jnp.arange(rel_bias.shape[0], dtype=jnp.int32)[None, :]).astype(
         jnp.float32

time: 195 us -> 194 us (level)
  other arithmetic: 9.93 us -> 6.07 us
    reduce_sum x2 -> x0, other arithmetic: 3.27 us -> none  [pick_lengths(): return jnp.sum(jnp.where(matches, table[None, :], 0), axis=1)]
    unnamed x23 -> x21, local copies, waits for them, and re-layouts: 10.3 us -> 10.3 us
  transfers between devices with their start and end apart: 1 -> 1, of which waited for: 0 -> 0; matrix products, arithmetic and copies ran while one was open for 12% -> 11% of each run, Pallas kernels for 42% -> 43%
where the time goes in v14:
time: 194 us; the launch traced here: 193 us
  Pallas kernels  147 us (76%)
  local copies, waits for them, and re-layouts  18.4 us (9%)
  between operations  17.5 us (9%)
  other arithmetic  6.07 us (3%)
  matrix products  4.14 us (2%)
    pallas_call x3, Pallas kernels, blk_stage(): pl.pallas_call(functools.partial(stage_kernel, n_blk, final, extra), out_...  90.8 us
    pallas_call x1, Pallas kernels, prologue(): pl.pallas_call(functools.partial(prologue_kernel, n_req, n_blk), out_shap...  39 us
    unnamed x21, local copies, waits for them, and re-layouts  10.3 us
    pallas_call x1, Pallas kernels, self_attention(): pl.pallas_call(self_kernel, out_shape=jax.ShapeDtypeStruct((n_q, HD), jnp...  6.83 us
    pallas_call x1, Pallas kernels, cross_branch(): pl.pallas_call(functools.partial(cross_kernel, blocks.shape[0], tuple(spa...  5.61 us
    pallas_call x1, Pallas kernels, ffn_branch(): pl.pallas_call(functools.partial(ffn_kernel, blocks.shape[0], tuple(spans...  4.87 us
  transfers between devices with their start and end apart: 1, of which 0 were waited for; matrix products, arithmetic and copies ran while one was open for 11% of the time, Pallas kernels for 43%

profile of v14, /device:TPU:33, one launch (start us, length us, event | category | flops | bytes accessed | tf_op | source)
XLA Modules:
  0.0 193.3 jit_solution(16319746026621339409)
XLA Ops:
  7.2 0.0 all-gather.3.cloned.1.call-start
  7.2 0.8 bitcast_dynamic-update-slice_fusion
  8.0 0.8 constant_dynamic-update-slice_fusion.3
  8.8 0.7 constant_dynamic-update-slice_fusion.2
  9.5 0.9 constant_dynamic-update-slice_fusion.1
  10.4 0.8 constant_dynamic-update-slice_fusion
  11.2 0.7 copy-done.3
  11.9 0.0 all-gather.3.cloned.1.call-update
  11.9 1.2 dynamic_slice.16
  14.5 1.0 convolution_reduce_fusion
  15.5 0.5 slice.69
  16.0 0.6 concatenate.14
  16.7 0.7 pad_slice_fusion
  17.3 0.7 compare_select_fusion
  18.0 0.7 compare_and_fusion
  19.3 0.7 pad_add_fusion
  20.0 0.1 constant_dynamic-slice_fusion.1
  20.1 0.6 fusion.16
  21.9 0.1 rev.3
  22.0 0.1 dynamic_slice.19
  22.1 0.1 slice.58
  22.2 0.9 copy.25
  23.1 0.1 reshape.56
  23.2 0.8 copy.24
  24.0 0.1 reshape.55
  24.2 0.6 gather_fusion
  24.8 1.1 broadcast_select_fusion.ordered_ref
  25.9 0.6 maximum_bitcast_fusion.packed_ref
  26.5 39.0 %shard_map.185 = (bf16[4096,128]{1,0:T(8,128)(2,1)}, bf16[8,256,128]{2,1,0:T(8,128)(2,1)}) custom-call(bf16[8,256,256]{2,1,0:T(8,128)(2,1)} %broadcast_select_fusion.ordered_ref, bf16[256,128]{1,0:T(8,128)(2,1)} %maximum_bitcast_fusion.packed_ref), custom_call_target="tpu_custom_call" | custom-call | tf_op jit(solution)/shard_map/pallas_call | solution.py:760
  65.6 1.5 copy.35
  67.1 1.0 reshape_reshape.3
  68.1 0.8 reshape_reshape_reshape.3
  68.9 1.3 pad_add_fusion.1.lens_ref
  70.2 0.3 fusion
  70.5 0.6 fusion.15
  71.1 1.7 convolution_convert_fusion.1
  72.9 0.1 fusion.14
  73.0 6.8 %shard_map.186 = bf16[512,64]{1,0:T(8,128)(2,1)S(1)} custom-call(s32[2]{0:T(128)S(1)} %pad_add_fusion.1.lens_ref, bf16[512,64]{1,0:T(8,128)(2,1)S(1)} %get-tuple-element.20.q_ref, bf16[4096,128]{1,0:T(8,128)(2,1)S(1)} %copy-done.1, bf16[512,64]{1,0:T(8,128)(2,1)S(1)} %get-tuple-element.19.kn_ref, bf16[512,64]{1,0:T(8,128)(2,1)S(1)} %get-tuple-element.18.vn_ref, ...), custom_call_target="tpu_custom_call" | custom-call | tf_op jit(solution)/shard_map/pallas_call | solution.py:481
  79.8 0.7 dynamic-slice_convert_fusion.refs_1_
  80.5 1.4 convolution_convert_fusion.refs_0_
  81.9 37.3 %shard_map.187 = (f32[32,1024]{1,0:T(8,128)}, bf16[512,1024]{1,0:T(8,128)(2,1)}) custom-call(bf16[512,1024]{1,0:T(8,128)(2,1)} %convolution_convert_fusion.refs_0_, f32[32,1024]{1,0:T(8,128)} %dynamic-slice_convert_fusion.refs_1_, f32[1,1024]{1,0:T(1,128)} %get-tuple-element.23.refs_2_), custom_call_target="tpu_custom_call" | custom-call | tf_op jit(solution)/shard_map/pallas_call | solution.py:328
  119.2 0.0 all-gather.3.cloned.1.call-done
  119.2 5.6 %shard_map.188.refs_0_ = bf16[512,1024]{1,0:T(8,128)(2,1)} custom-call(s32[1]{0:T(128)} %bitcast.4.len_ref, bf16[512,1024]{1,0:T(8,128)(2,1)} %get-tuple-element.11.normed_ref, bf16[512,1024]{1,0:T(8,128)(2,1)} %enc_ref.1, bf16[8,784,128]{2,1,0:T(8,128)(2,1)} %bitcast.40), custom_call_target="tpu_custom_call" | custom-call | tf_op jit(solution)/shard_map/pallas_call | solution.py:408
  124.8 26.6 %shard_map.189 = (f32[32,1024]{1,0:T(8,128)}, bf16[512,1024]{1,0:T(8,128)(2,1)}) custom-call(bf16[512,1024]{1,0:T(8,128)(2,1)} %shard_map.188.refs_0_, f32[32,1024]{1,0:T(8,128)} %get-tuple-element.12.refs_1_, f32[1,1024]{1,0:T(1,128)} %get-tuple-element.21.refs_2_), custom_call_target="tpu_custom_call" | custom-call | tf_op jit(solution)/shard_map/pallas_call | solution.py:328
  151.4 4.9 %shard_map.190.refs_0_ = bf16[512,1024]{1,0:T(8,128)(2,1)} custom-call(bf16[512,1024]{1,0:T(8,128)(2,1)} %get-tuple-element.13.normed_ref, bf16[8,784,128]{2,1,0:T(8,128)(2,1)} %bitcast.41), custom_call_target="tpu_custom_call" | custom-call | tf_op jit(solution)/shard_map/pallas_call | solution.py:418
  156.3 26.9 %shard_map.191 = (f32[32,1024]{1,0:T(8,128)}, bf16[512,1024]{1,0:T(8,128)(2,1)}) custom-call(bf16[512,1024]{1,0:T(8,128)(2,1)} %shard_map.190.refs_0_, f32[32,1024]{1,0:T(8,128)} %get-tuple-element.14.refs_1_, f32[1,1024]{1,0:T(1,128)} %get-tuple-element.21.refs_2_), custom_call_target="tpu_custom_call" | custom-call | tf_op jit(solution)/shard_map/pallas_call | solution.py:328
  183.2 2.3 %copy.42 = bf16[512,1024]{1,0:T(8,128)(2,1)} copy(bf16[512,1024]{1,0:T(8,128)(2,1)} %get-tuple-element.29) | data formatting | bytes 2097152
  185.5 1.0 copy.43
  (16 shorter events, 0.1 us)
Async XLA Ops:
  7.2 17.0 %copy-start = (bf16[8,256,256]{2,1,0:T(8,128)(2,1)S(1)}, bf16[8,256,256]{2,1,0:T(8,128)(2,1)}, u32[]{:S(2)}) copy-start(bf16[8,256,256]{2,1,0:T(8,128)(2,1)} %param.20) | copy-start | bytes 3145732
  7.2 112.0 %all-gather.3.cloned.1.call-start = ((), (), s32[]{:S(2)}) async-start(), calls=%async_computation | async-start | bytes 1806336 | tf_op jit(solution)/shard_map/all_gather | solution.py:800
  11.2 0.7 copy-start.3
  24.1 1.8 copy-start.4
  65.6 4.7 %copy-start.2 = (bf16[512,1024]{1,0:T(8,128)(2,1)S(1)}, bf16[512,1024]{1,0:T(8,128)(2,1)}, u32[]{:S(2)}) copy-start(bf16[512,1024]{1,0:T(8,128)(2,1)} %param.18) | copy-start | bytes 3145732
  67.1 3.5 %copy-start.5 = (f32[3,1024]{1,0:T(4,128)S(1)}, f32[3,1024]{1,0:T(4,128)}, u32[]{:S(2)}) copy-start(f32[3,1024]{1,0:T(4,128)} %param.27) | copy-start | bytes 36868
  71.1 1.9 copy-start.1
Sparse Core Ops, SparseCore 0:
  12.0 65.2 all-gather.2

commit v15 on v14

--- a/solution.py
+++ b/solution.py
@@ -839,8 +839,10 @@
     flat = jnp.concatenate([w.reshape(-1) for w, _ in early])
     cache_blk, whole = prologue(ordered, flat.reshape(-1, 128))
     cache_dec = cache_blk[None]
+    ffn_parts, _ = lax.optimization_barrier(((ff_in, ff_out), cache_blk))
+    ffn_blocks = lane_pack([(ffn_parts[0], 0), (ffn_parts[1], 1)])
     gathered = unpack(whole, early)
-    late_blocks = lane_pack(late)
+    cross_blocks = lane_pack(late[:3])
     wq_self, wkv_self, wo_self = gathered
     n_blk = lax.axis_size("blk")
     rows_dev = new_states.shape[0] // n_blk
@@ -864,9 +866,9 @@
     part = jnp.dot(context, wo_self, preferred_element_type=jnp.float32).astype(jnp.bfloat16)
     residual, normed = blk_stage(part, own_rows, norm_gain[1], False)
     spans = block_spans(late)
-    part = cross_branch(normed, encoder_out, late_blocks, spans[:3], slot_enc[0])
+    part = cross_branch(normed, encoder_out, cross_blocks, spans[:3], slot_enc[0])
     residual, normed = blk_stage(part.astype(jnp.bfloat16), residual, norm_gain[2], False)
-    part = ffn_branch(normed, late_blocks, spans[3:])
+    part = ffn_branch(normed, ffn_blocks, block_spans([(ff_in, 0), (ff_out, 1)]))
     _, layer_out = blk_stage(part, residual, norm_gain[2], True)
     return (layer_out, cache_dec)
 

time: 194 us -> 213 us (1.098)
  blocking collectives: 0 us -> 24.5 us
  local copies, waits for them, and re-layouts: 18.4 us -> 13.8 us
    all_gather x0 -> x1, blocking collectives: none -> 24.5 us  [lane_pack(): return lax.all_gather(packed, 'req', axis=0, tiled=False)]
    pallas_call x1, Pallas kernels: 39 us -> 30.6 us  [prologue(): pl.pallas_call(functools.partial(prologue_kernel, n_req, n_blk), out_shap...]
    pallas_call x3, Pallas kernels: 90.8 us -> 98.2 us  [blk_stage(): pl.pallas_call(functools.partial(stage_kernel, n_blk, final, extra), out_...]
    unnamed x21 -> x39, local copies, waits for them, and re-layouts: 10.3 us -> 7.02 us
  transfers between devices with their start and end apart: 1 -> 1, of which waited for: 0 -> 0; matrix products, arithmetic and copies ran while one was open for 11% -> 6% of each run, Pallas kernels for 43% -> 40%
where the time goes in v15:
time: 213 us; the launch traced here: 211 us
  Pallas kernels  145 us (68%)
  blocking collectives  24.5 us (12%)
  between operations  17.6 us (8%)
  local copies, waits for them, and re-layouts  13.8 us (6%)
  other arithmetic  6.28 us (3%)
  matrix products  2.97 us (1%)
    pallas_call x3, Pallas kernels, blk_stage(): pl.pallas_call(functools.partial(stage_kernel, n_blk, final, extra), out_...  98.2 us
    pallas_call x1, Pallas kernels, prologue(): pl.pallas_call(functools.partial(prologue_kernel, n_req, n_blk), out_shap...  30.6 us
    all_gather x1, blocking collectives, lane_pack(): return lax.all_gather(packed, 'req', axis=0, tiled=False)  24.5 us
    unnamed x39, local copies, waits for them, and re-layouts  7.02 us
    pallas_call x1, Pallas kernels, self_attention(): pl.pallas_call(self_kernel, out_shape=jax.ShapeDtypeStruct((n_q, HD), jnp...  6.76 us
    pallas_call x1, Pallas kernels, cross_branch(): pl.pallas_call(functools.partial(cross_kernel, blocks.shape[0], tuple(spa...  5.15 us
    pallas_call x1, Pallas kernels, ffn_branch(): pl.pallas_call(functools.partial(ffn_kernel, blocks.shape[0], tuple(spans...  4.68 us
  transfers between devices with their start and end apart: 1, of which 0 were waited for; matrix products, arithmetic and copies ran while one was open for 6% of the time, Pallas kernels for 40%

profile of v15, /device:TPU:33, one launch (start us, length us, event | category | flops | bytes accessed | tf_op | source)
XLA Modules:
  0.0 210.6 jit_solution(2841190202973311167)
XLA Ops:
  7.2 0.0 copy-start
  7.2 0.0 all-gather.4.cloned.1.call-start
  7.2 0.7 compare_select_fusion
  8.0 0.7 compare_and_fusion
  8.6 0.9 copy.25
  9.5 0.1 reshape.56
  9.6 0.8 copy.24
  10.4 0.1 reshape.55
  10.6 0.6 gather_fusion
  11.2 1.1 broadcast_select_fusion.ordered_ref
  12.3 0.0 copy-start.14
  12.4 0.6 maximum_bitcast_fusion.packed_ref
  13.0 30.6 %shard_map.185 = (bf16[4096,128]{1,0:T(8,128)(2,1)}, bf16[8,256,128]{2,1,0:T(8,128)(2,1)}) custom-call(bf16[8,256,256]{2,1,0:T(8,128)(2,1)} %broadcast_select_fusion.ordered_ref, bf16[256,128]{1,0:T(8,128)(2,1)} %maximum_bitcast_fusion.packed_ref), custom_call_target="tpu_custom_call" | custom-call | tf_op jit(solution)/shard_map/pallas_call | solution.py:760
  43.7 0.7 pad_maximum_fusion
  44.4 0.0 all-gather.4.cloned.1.call-update
  44.4 0.6 dynamic_slice.16
  47.0 0.1 constant_dynamic-slice_fusion.1
  47.1 0.5 fusion.16
  47.6 1.0 convolution_reduce_fusion
  48.6 0.6 slice.69
  49.2 0.7 pad_slice_fusion
  49.9 1.4 copy.35
  51.3 1.4 pad_add_fusion.1.lens_ref
  52.7 0.7 concatenate.17
  54.8 0.1 rev.3
  54.9 0.1 dynamic_slice.19
  55.0 0.1 slice.58
  55.1 1.0 reshape_reshape.3
  56.0 0.8 reshape_reshape_reshape.3
  56.9 0.3 fusion
  57.2 0.6 fusion.15
  57.8 0.0 copy-done.3
  57.8 0.1 copy-done.4
  57.9 0.6 convolution_convert_fusion.1
  58.5 0.1 fusion.14
  58.6 0.5 copy-done.1
  59.1 6.8 %shard_map.186 = bf16[512,64]{1,0:T(8,128)(2,1)S(1)} custom-call(s32[2]{0:T(128)S(1)} %pad_add_fusion.1.lens_ref, bf16[512,64]{1,0:T(8,128)(2,1)S(1)} %get-tuple-element.24.q_ref, bf16[4096,128]{1,0:T(8,128)(2,1)S(1)} %copy-done.1, bf16[512,64]{1,0:T(8,128)(2,1)S(1)} %get-tuple-element.23.kn_ref, bf16[512,64]{1,0:T(8,128)(2,1)S(1)} %get-tuple-element.22.vn_ref, ...), custom_call_target="tpu_custom_call" | custom-call | tf_op jit(solution)/shard_map/pallas_call | solution.py:481
  65.9 0.7 dynamic-slice_convert_fusion.refs_1_
  66.6 1.4 convolution_convert_fusion.refs_0_
  67.9 38.6 %shard_map.187 = (f32[32,1024]{1,0:T(8,128)}, bf16[512,1024]{1,0:T(8,128)(2,1)}) custom-call(bf16[512,1024]{1,0:T(8,128)(2,1)} %convolution_convert_fusion.refs_0_, f32[32,1024]{1,0:T(8,128)} %dynamic-slice_convert_fusion.refs_1_, f32[1,1024]{1,0:T(1,128)} %get-tuple-element.27.refs_2_), custom_call_target="tpu_custom_call" | custom-call | tf_op jit(solution)/shard_map/pallas_call | solution.py:328
  106.6 24.5 %all-gather = bf16[2048,128]{1,0:T(8,128)(2,1)} all-gather(bf16[256,128]{1,0:T(8,128)(2,1)S(1)} %pad_maximum_fusion.1), channel_id=2, replica_groups=mesh['req'=8,'blk'=16] {'req'}, dimensions={0}, use_global_device_ids=true | all-gather | bytes 589824 | tf_op jit(solution)/shard_map/all_gather | solution.py:800
  131.1 5.1 %shard_map.188.refs_0_ = bf16[512,1024]{1,0:T(8,128)(2,1)} custom-call(s32[1]{0:T(128)} %bitcast.4.len_ref, bf16[512,1024]{1,0:T(8,128)(2,1)} %get-tuple-element.13.normed_ref, bf16[512,1024]{1,0:T(8,128)(2,1)} %enc_ref.1, bf16[8,256,128]{2,1,0:T(8,128)(2,1)} %bitcast.42), custom_call_target="tpu_custom_call" | custom-call | tf_op jit(solution)/shard_map/pallas_call | solution.py:408
  136.2 33.2 %shard_map.189 = (f32[32,1024]{1,0:T(8,128)}, bf16[512,1024]{1,0:T(8,128)(2,1)}) custom-call(bf16[512,1024]{1,0:T(8,128)(2,1)} %shard_map.188.refs_0_, f32[32,1024]{1,0:T(8,128)} %get-tuple-element.14.refs_1_, f32[1,1024]{1,0:T(1,128)} %get-tuple-element.25.refs_2_), custom_call_target="tpu_custom_call" | custom-call | tf_op jit(solution)/shard_map/pallas_call | solution.py:328
  169.4 0.0 all-gather.4.cloned.1.call-done
  169.4 4.7 %shard_map.190.refs_0_ = bf16[512,1024]{1,0:T(8,128)(2,1)} custom-call(bf16[512,1024]{1,0:T(8,128)(2,1)} %get-tuple-element.15.normed_ref, bf16[8,528,128]{2,1,0:T(8,128)(2,1)} %bitcast.43), custom_call_target="tpu_custom_call" | custom-call | tf_op jit(solution)/shard_map/pallas_call | solution.py:418
  174.1 26.5 %shard_map.191 = (f32[32,1024]{1,0:T(8,128)}, bf16[512,1024]{1,0:T(8,128)(2,1)}) custom-call(bf16[512,1024]{1,0:T(8,128)(2,1)} %shard_map.190.refs_0_, f32[32,1024]{1,0:T(8,128)} %get-tuple-element.18.refs_1_, f32[1,1024]{1,0:T(1,128)} %get-tuple-element.25.refs_2_), custom_call_target="tpu_custom_call" | custom-call | tf_op jit(solution)/shard_map/pallas_call | solution.py:328
  200.6 2.3 %copy.38 = bf16[512,1024]{1,0:T(8,128)(2,1)} copy(bf16[512,1024]{1,0:T(8,128)(2,1)} %get-tuple-element.33) | data formatting | bytes 2097152
  202.8 1.0 copy.39
  (36 shorter events, 0.1 us)
Async XLA Ops:
  7.2 3.4 %copy-start = (bf16[8,256,256]{2,1,0:T(8,128)(2,1)S(1)}, bf16[8,256,256]{2,1,0:T(8,128)(2,1)}, u32[]{:S(2)}) copy-start(bf16[8,256,256]{2,1,0:T(8,128)(2,1)} %param.20) | copy-start | bytes 3145732
  7.2 162.2 %all-gather.4.cloned.1.call-start = ((), (), s32[]{:S(2)}) async-start(), calls=%async_computation | async-start | bytes 1216512 | tf_op jit(solution)/shard_map/all_gather | solution.py:800
  11.2 1.2 copy-start.8
  12.3 31.3 %copy-start.5 = (bf16[128,2,176]{0,2,1:T(8,128)(2,1)S(1)}, bf16[128,2,176]{0,2,1:T(8,128)(2,1)}, u32[]{:S(2)}) copy-start(bf16[128,2,176]{0,2,1:T(8,128)(2,1)} %param.34) | copy-start | bytes 270340
  12.3 31.4 %copy-start.6 = (bf16[176,128]{1,0:T(8,128)(2,1)S(1)}, bf16[176,128]{1,0:T(8,128)(2,1)}, u32[]{:S(2)}) copy-start(bf16[176,128]{1,0:T(8,128)(2,1)} %param.35) | copy-start | bytes 135172
  12.3 32.1 %copy-start.16 = (s32[8]{0:T(128)S(1)}, s32[8]{0:T(128)}, u32[]{:S(2)}) copy-start(s32[8]{0:T(128)} %param.21) | copy-start | bytes 100
  12.3 34.6 %copy-start.12 = (s32[8]{0:T(128)S(1)}, s32[8]{0:T(128)}, u32[]{:S(2)}) copy-start(s32[8]{0:T(128)} %param.24) | copy-start | bytes 100
  12.3 34.6 %copy-start.13 = (s32[8]{0:T(128)S(1)}, s32[8]{0:T(128)}, u32[]{:S(2)}) copy-start(s32[8]{0:T(128)} %param.23) | copy-start | bytes 100
  12.3 34.6 %copy-start.14 = (s32[8]{0:T(128)S(1)}, s32[8]{0:T(128)}, u32[]{:S(2)}) copy-start(s32[8]{0:T(128)} %param.22) | copy-start | bytes 100
  12.4 35.2 %copy-start.15 = (s32[4608]{0:T(1024)S(1)}, s32[4608]{0:T(1024)}, u32[]{:S(2)}) copy-start(s32[4608]{0:T(1024)} %param.25) | copy-start | bytes 55300
  51.3 5.6 %copy-start.2 = (bf16[512,1024]{1,0:T(8,128)(2,1)S(1)}, bf16[512,1024]{1,0:T(8,128)(2,1)}, u32[]{:S(2)}) copy-start(bf16[512,1024]{1,0:T(8,128)(2,1)} %param.18) | copy-start | bytes 3145732
  54.8 2.4 %copy-start.11 = (f32[3,1024]{1,0:T(4,128)S(1)}, f32[3,1024]{1,0:T(4,128)}, u32[]{:S(2)}) copy-start(f32[3,1024]{1,0:T(4,128)} %param.27) | copy-start | bytes 36868
  56.9 1.0 copy-start.3
  56.9 1.0 copy-start.4
  57.9 1.2 copy-start.1
  66.6 40.0 %copy-start.7 = (bf16[128,2,64]{0,2,1:T(8,128)(2,1)S(1)}, bf16[128,2,64]{0,2,1:T(8,128)(2,1)}, u32[]{:S(2)}) copy-start(bf16[128,2,64]{0,2,1:T(8,128)(2,1)} %param.32) | copy-start | bytes 98308
  66.6 40.0 %copy-start.9 = (bf16[64,128]{1,0:T(8,128)(2,1)S(1)}, bf16[64,128]{1,0:T(8,128)(2,1)}, u32[]{:S(2)}) copy-start(bf16[64,128]{1,0:T(8,128)(2,1)} %param.33) | copy-start | bytes 49156
  66.6 40.0 %copy-start.10 = (bf16[128,64]{0,1:T(8,128)(2,1)S(1)}, bf16[128,64]{0,1:T(8,128)(2,1)}, u32[]{:S(2)}) copy-start(bf16[128,64]{0,1:T(8,128)(2,1)} %param.31) | copy-start | bytes 49156
Sparse Core Ops, SparseCore 0:
  44.5 48.5 all-gather.3

commit v16 on v14

--- a/solution.py
+++ b/solution.py
@@ -487,6 +487,88 @@
     )(lens, q, cache_blk, k_new, v_new, g, f)
 
 
+def self_full_kernel(n_req, spans, lens_ref, x_ref, gain_ref, w_ref, c_ref, g_ref, f_ref, o_ref, ctx_ref):
+    old_len = lens_ref[0]
+    fresh_len = lens_ref[1]
+    (q_at, q_len), (kv_at, kv_len), (o_at, o_len) = spans
+    nt = (((1,), (1,)), ((), ()))
+    width = w_ref.shape[2]
+    x = x_ref[...].astype(jnp.float32)
+    mean_square = jnp.mean(x * x, axis=-1, keepdims=True)
+    normed = (x * lax.rsqrt(mean_square + EPSILON) * gain_ref[...]).astype(jnp.bfloat16)
+    queries = None
+    pair = None
+    for r in range(n_req):
+        cols = slice(r * width, (r + 1) * width)
+        term = lax.dot_general(
+            normed[:, cols], w_ref[r, q_at : q_at + q_len, :], nt,
+            preferred_element_type=jnp.float32,
+        )
+        queries = term if queries is None else queries + term
+        term = lax.dot_general(
+            normed[:, cols], w_ref[r, kv_at : kv_at + kv_len, :], nt,
+            preferred_element_type=jnp.float32,
+        )
+        pair = term if pair is None else pair + term
+    queries = queries.astype(jnp.bfloat16)
+    pair = pair.astype(jnp.bfloat16)
+    k_new = pair[:, :HD]
+    v_new = pair[:, HD:]
+    n_q = x_ref.shape[0]
+    n_ctx = c_ref.shape[0]
+    wide_old = n_ctx + TQ
+    wide_new = n_q + TQ
+    k_old = c_ref[:, :HD]
+    v_old = c_ref[:, HD:]
+    for t in range(n_q // TQ):
+        q = queries[t * TQ : (t + 1) * TQ, :]
+        start = n_q - TQ - t * TQ
+        s_old = lax.dot_general(q, k_old, nt, preferred_element_type=jnp.float32)
+        line = jnp.broadcast_to(g_ref[:, start : start + wide_old], (TQ, wide_old))
+        bias = pltpu.roll(line, wide_old - (TQ - 1), 1, stride=1, stride_axis=0)[:, :n_ctx]
+        col = lax.broadcasted_iota(jnp.int32, (TQ, n_ctx), 1)
+        s_old = jnp.where(col < old_len, s_old + bias, NEG_FILL)
+        s_new = lax.dot_general(q, k_new, nt, preferred_element_type=jnp.float32)
+        line = jnp.broadcast_to(f_ref[:, start : start + wide_new], (TQ, wide_new))
+        bias = pltpu.roll(line, wide_new - (TQ - 1), 1, stride=1, stride_axis=0)[:, :n_q]
+        row = lax.broadcasted_iota(jnp.int32, (TQ, n_q), 0) + t * TQ
+        col = lax.broadcasted_iota(jnp.int32, (TQ, n_q), 1)
+        s_new = jnp.where((col <= row) & (col < fresh_len), s_new + bias, NEG_FILL)
+        top = jnp.maximum(
+            jnp.max(s_old, axis=1, keepdims=True), jnp.max(s_new, axis=1, keepdims=True)
+        )
+        p_old = jnp.exp(s_old - top)
+        p_new = jnp.exp(s_new - top)
+        total = jnp.sum(p_old, axis=1, keepdims=True) + jnp.sum(p_new, axis=1, keepdims=True)
+        w_old = (p_old / total).astype(jnp.bfloat16)
+        w_new = (p_new / total).astype(jnp.bfloat16)
+        out = jnp.dot(w_old, v_old, preferred_element_type=jnp.float32) + jnp.dot(
+            w_new, v_new, preferred_element_type=jnp.float32
+        )
+        ctx_ref[t * TQ : (t + 1) * TQ, :] = out.astype(jnp.bfloat16)
+    context = ctx_ref[...]
+    for r in range(n_req):
+        o_ref[:, r * width : (r + 1) * width] = jnp.dot(
+            context, w_ref[r, o_at : o_at + o_len, :], preferred_element_type=jnp.float32
+        ).astype(o_ref.dtype)
+
+
+def self_branch(states, gain, blocks, spans, cache_blk, line, old_len, fresh_len):
+    n_q = states.shape[0]
+    n_ctx = cache_blk.shape[0]
+    g, f = bias_lines(line, old_len, n_q, n_ctx)
+    lens = jnp.stack([old_len, fresh_len]).astype(jnp.int32)
+    vmem = pl.BlockSpec(memory_space=pltpu.VMEM)
+    return pl.pallas_call(
+        functools.partial(self_full_kernel, blocks.shape[0], tuple(spans)),
+        out_shape=jax.ShapeDtypeStruct(states.shape, jnp.bfloat16),
+        in_specs=[pl.BlockSpec(memory_space=pltpu.SMEM)] + [vmem] * 6,
+        out_specs=vmem,
+        scratch_shapes=[pltpu.VMEM((n_q, HD), jnp.bfloat16)],
+        compiler_params=pltpu.CompilerParams(vmem_limit_bytes=48 * 1024 * 1024),
+    )(lens, states, gain[None, :], blocks, cache_blk, g, f)
+
+
 def pack_gather(pieces):
     flat = jnp.concatenate([w.reshape(-1) for w, _ in pieces])
     whole = lax.all_gather(flat, "req", axis=0, tiled=False)
@@ -836,32 +918,28 @@
     bias_dist = jnp.dot(onehot, own_bias, precision=lax.Precision.HIGHEST).T
     early = [(self_q, 0), (self_kv, 0), (self_out, 1)]
     late = [(cross_q, 0), (cross_kv, 0), (cross_out, 1), (ff_in, 0), (ff_out, 1)]
-    flat = jnp.concatenate([w.reshape(-1) for w, _ in early])
-    cache_blk, whole = prologue(ordered, flat.reshape(-1, 128))
+    blocks = []
+    for w, axis in early:
+        two_d = w.reshape(w.shape[0], -1)
+        blocks.append(two_d.T if axis == 0 else two_d)
+    cache_blk, early_blocks = prologue(ordered, jnp.concatenate(blocks, axis=0))
     cache_dec = cache_blk[None]
-    gathered = unpack(whole, early)
     late_blocks = lane_pack(late)
-    wq_self, wkv_self, wo_self = gathered
     n_blk = lax.axis_size("blk")
     rows_dev = new_states.shape[0] // n_blk
     own_rows = lax.dynamic_slice_in_dim(
         new_states, chunk_of(lax.axis_index("blk"), n_blk) * rows_dev, rows_dev, 0
     ).astype(jnp.float32)
-    normed = rms_rows(new_states.astype(jnp.float32), norm_gain[0])
-    self_cat = jnp.concatenate([wq_self, wkv_self.reshape(wkv_self.shape[0], -1)], axis=1)
-    projected = jnp.dot(normed, self_cat, preferred_element_type=jnp.float32).astype(
-        jnp.bfloat16
-    )
-    context = self_attention(
-        projected[:, :HD],
-        cache_dec[0],
-        projected[:, HD : 2 * HD],
-        projected[:, 2 * HD :],
+    part = self_branch(
+        new_states,
+        norm_gain[0],
+        early_blocks,
+        block_spans(early),
+        cache_blk,
         bias_dist[0],
         slot_old[0],
         slot_new[0],
     )
-    part = jnp.dot(context, wo_self, preferred_element_type=jnp.float32).astype(jnp.bfloat16)
     residual, normed = blk_stage(part, own_rows, norm_gain[1], False)
     spans = block_spans(late)
     part = cross_branch(normed, encoder_out, late_blocks, spans[:3], slot_enc[0])

time: 194 us -> 189 us (0.974)
  matrix products: 4.14 us -> 1.04 us
  local copies, waits for them, and re-layouts: 18.4 us -> 16.3 us
  Pallas kernels: 147 us -> 149 us
    dot_general x2 -> x0, matrix products: 3.11 us -> none  [the longest x1 1.73 us: per_device(): jnp.dot(normed, self_cat, preferred_element_type=jnp.float32)]
    unnamed x21 -> x30, local copies, waits for them, and re-layouts: 10.3 us -> 10.4 us
  transfers between devices with their start and end apart: 1 -> 1, of which waited for: 0 -> 0; matrix products, arithmetic and copies ran while one was open for 11% -> 6% of each run, Pallas kernels for 43% -> 45%
where the time goes in v16:
time: 189 us; the launch traced here: 188 us
  Pallas kernels  149 us (79%)
  between operations  17.3 us (9%)
  local copies, waits for them, and re-layouts  16.3 us (9%)
  other arithmetic  4.99 us (3%)
    pallas_call x3, Pallas kernels, blk_stage(): pl.pallas_call(functools.partial(stage_kernel, n_blk, final, extra), out_...  91.3 us
    pallas_call x1, Pallas kernels, prologue(): pl.pallas_call(functools.partial(prologue_kernel, n_req, n_blk), out_shap...  39 us
    unnamed x30, local copies, waits for them, and re-layouts  10.4 us
    pallas_call x1, Pallas kernels, self_branch(): pl.pallas_call(functools.partial(self_full_kernel, blocks.shape[0], tuple...  7.76 us
    pallas_call x1, Pallas kernels, cross_branch(): pl.pallas_call(functools.partial(cross_kernel, blocks.shape[0], tuple(spa...  5.59 us
    pallas_call x1, Pallas kernels, ffn_branch(): pl.pallas_call(functools.partial(ffn_kernel, blocks.shape[0], tuple(spans...  4.86 us
  transfers between devices with their start and end apart: 1, of which 0 were waited for; matrix products, arithmetic and copies ran while one was open for 6% of the time, Pallas kernels for 45%

profile of v16, /device:TPU:33, one launch (start us, length us, event | category | flops | bytes accessed | tf_op | source)
XLA Modules:
  0.0 188.3 jit_solution(11677417565075851387)
XLA Ops:
  7.2 0.0 copy-start
  7.2 0.0 all-gather.3.cloned.1.call-start
  7.2 0.8 bitcast_dynamic-update-slice_fusion
  8.0 0.8 constant_dynamic-update-slice_fusion.3
  8.8 0.7 constant_dynamic-update-slice_fusion.2
  9.5 0.9 constant_dynamic-update-slice_fusion.1
  10.5 0.8 constant_dynamic-update-slice_fusion
  11.3 0.7 copy-done.6
  11.9 0.0 all-gather.3.cloned.1.call-update
  12.0 1.2 dynamic_slice.16
  15.2 0.7 pad_add_fusion
  15.9 0.1 constant_dynamic-slice_fusion.1
  15.9 0.5 fusion.2
  17.6 1.0 convolution_reduce_fusion
  18.6 0.5 slice.40
  19.2 0.6 concatenate.10
  19.8 0.1 rev.3
  19.9 0.1 dynamic_slice.19
  20.0 0.7 pad_slice_fusion
  20.7 0.1 slice.35
  20.8 0.7 compare_select_fusion
  21.4 0.0 copy-done
  21.4 0.6 gather_fusion
  22.0 0.0 copy-done.7
  22.1 0.0 copy-done.8
  22.1 0.0 copy-done.9
  22.1 0.6 pad_maximum_fusion.packed_ref
  22.7 0.0 copy-done.11
  22.7 0.0 copy-start.10
  22.7 0.0 copy-start.4
  22.8 1.1 broadcast_select_fusion.ordered_ref
  23.9 39.0 %shard_map.185 = (bf16[4096,128]{1,0:T(8,128)(2,1)}, bf16[8,256,128]{2,1,0:T(8,128)(2,1)}) custom-call(bf16[8,256,256]{2,1,0:T(8,128)(2,1)} %broadcast_select_fusion.ordered_ref, bf16[256,128]{1,0:T(8,128)(2,1)} %pad_maximum_fusion.packed_ref), custom_call_target="tpu_custom_call" | custom-call | tf_op jit(solution)/shard_map/pallas_call | solution.py:842
  62.9 1.2 pad_add_fusion.1.lens_ref
  64.1 0.6 fusion.1
  64.7 1.2 copy-done.1
  65.9 1.0 copy-done.5
  67.0 7.8 %shard_map.186.refs_0_ = bf16[512,1024]{1,0:T(8,128)(2,1)S(1)} custom-call(s32[2]{0:T(128)S(1)} %pad_add_fusion.1.lens_ref, bf16[512,1024]{1,0:T(8,128)(2,1)S(1)} %copy-done.4, f32[1,1024]{1,0:T(1,128)S(1)} %get-tuple-element.17.gain_ref, bf16[8,256,128]{2,1,0:T(8,128)(2,1)S(1)} %copy-done.5, bf16[4096,128]{1,0:T(8,128)(2,1)S(1)} %copy-done.1, ...), custom_call_target="tpu_custom_call" | custom-call | tf_op jit(solution)/shard_map/pallas_call | solution.py:562
  74.7 0.0 copy-start.3
  74.7 1.0 copy-done.3
  75.7 0.7 dynamic-slice_convert_fusion.refs_1_
  76.4 37.9 %shard_map.187 = (f32[32,1024]{1,0:T(8,128)}, bf16[512,1024]{1,0:T(8,128)(2,1)}) custom-call(bf16[512,1024]{1,0:T(8,128)(2,1)} %copy-done.3, f32[32,1024]{1,0:T(8,128)} %dynamic-slice_convert_fusion.refs_1_, f32[1,1024]{1,0:T(1,128)} %get-tuple-element.18.refs_2_), custom_call_target="tpu_custom_call" | custom-call | tf_op jit(solution)/shard_map/pallas_call | solution.py:328
  114.2 0.0 all-gather.3.cloned.1.call-done
  114.3 5.6 %shard_map.188.refs_0_ = bf16[512,1024]{1,0:T(8,128)(2,1)} custom-call(s32[1]{0:T(128)} %bitcast.4.len_ref, bf16[512,1024]{1,0:T(8,128)(2,1)} %get-tuple-element.11.normed_ref, bf16[512,1024]{1,0:T(8,128)(2,1)} %enc_ref.1, bf16[8,784,128]{2,1,0:T(8,128)(2,1)} %bitcast.28), custom_call_target="tpu_custom_call" | custom-call | tf_op jit(solution)/shard_map/pallas_call | solution.py:408
  119.9 26.5 %shard_map.189 = (f32[32,1024]{1,0:T(8,128)}, bf16[512,1024]{1,0:T(8,128)(2,1)}) custom-call(bf16[512,1024]{1,0:T(8,128)(2,1)} %shard_map.188.refs_0_, f32[32,1024]{1,0:T(8,128)} %get-tuple-element.12.refs_1_, f32[1,1024]{1,0:T(1,128)} %get-tuple-element.16.refs_2_), custom_call_target="tpu_custom_call" | custom-call | tf_op jit(solution)/shard_map/pallas_call | solution.py:328
  146.4 4.9 %shard_map.190.refs_0_ = bf16[512,1024]{1,0:T(8,128)(2,1)} custom-call(bf16[512,1024]{1,0:T(8,128)(2,1)} %get-tuple-element.13.normed_ref, bf16[8,784,128]{2,1,0:T(8,128)(2,1)} %bitcast.29), custom_call_target="tpu_custom_call" | custom-call | tf_op jit(solution)/shard_map/pallas_call | solution.py:418
  151.3 26.9 %shard_map.191 = (f32[32,1024]{1,0:T(8,128)}, bf16[512,1024]{1,0:T(8,128)(2,1)}) custom-call(bf16[512,1024]{1,0:T(8,128)(2,1)} %shard_map.190.refs_0_, f32[32,1024]{1,0:T(8,128)} %get-tuple-element.14.refs_1_, f32[1,1024]{1,0:T(1,128)} %get-tuple-element.16.refs_2_), custom_call_target="tpu_custom_call" | custom-call | tf_op jit(solution)/shard_map/pallas_call | solution.py:328
  178.2 2.3 %copy.26 = bf16[512,1024]{1,0:T(8,128)(2,1)} copy(bf16[512,1024]{1,0:T(8,128)(2,1)} %get-tuple-element.24) | data formatting | bytes 2097152
  180.5 1.0 copy.27
  (14 shorter events, 0.0 us)
Async XLA Ops:
  7.2 14.3 %copy-start = (bf16[8,256,256]{2,1,0:T(8,128)(2,1)S(1)}, bf16[8,256,256]{2,1,0:T(8,128)(2,1)}, u32[]{:S(2)}) copy-start(bf16[8,256,256]{2,1,0:T(8,128)(2,1)} %param.20) | copy-start | bytes 3145732
  7.2 107.1 %all-gather.3.cloned.1.call-start = ((), (), s32[]{:S(2)}) async-start(), calls=%async_computation | async-start | bytes 1806336 | tf_op jit(solution)/shard_map/all_gather | solution.py:882
  8.0 14.0 %copy-start.7 = (bf16[128,2,64]{0,2,1:T(8,128)(2,1)S(1)}, bf16[128,2,64]{0,2,1:T(8,128)(2,1)}, u32[]{:S(2)}) copy-start(bf16[128,2,64]{0,2,1:T(8,128)(2,1)} %param.29) | copy-start | bytes 98308
  8.0 14.0 %copy-start.8 = (bf16[64,128]{1,0:T(8,128)(2,1)S(1)}, bf16[64,128]{1,0:T(8,128)(2,1)}, u32[]{:S(2)}) copy-start(bf16[64,128]{1,0:T(8,128)(2,1)} %param.30) | copy-start | bytes 49156
  8.0 14.0 %copy-start.9 = (bf16[128,64]{0,1:T(8,128)(2,1)S(1)}, bf16[128,64]{0,1:T(8,128)(2,1)}, u32[]{:S(2)}) copy-start(bf16[128,64]{0,1:T(8,128)(2,1)} %param.28) | copy-start | bytes 49156
  9.5 13.2 %copy-start.11 = (s32[8]{0:T(128)S(1)}, s32[8]{0:T(128)}, u32[]{:S(2)}) copy-start(s32[8]{0:T(128)} %param.21) | copy-start | bytes 100
  11.3 0.7 copy-start.6
  22.7 41.4 %copy-start.10 = (f32[3,1024]{1,0:T(4,128)S(1)}, f32[3,1024]{1,0:T(4,128)}, u32[]{:S(2)}) copy-start(f32[3,1024]{1,0:T(4,128)} %param.27) | copy-start | bytes 36868
  22.7 41.9 %copy-start.4 = (bf16[512,1024]{1,0:T(8,128)(2,1)S(1)}, bf16[512,1024]{1,0:T(8,128)(2,1)}, u32[]{:S(2)}) copy-start(bf16[512,1024]{1,0:T(8,128)(2,1)} %x_ref.1) | copy-start | bytes 3145732
  64.7 1.2 copy-start.1
  65.9 1.0 copy-start.5
  74.7 1.0 copy-start.3
  151.3 29.2 %copy-start.2 = (bf16[4096,128]{1,0:T(8,128)(2,1)S(1)}, bf16[4096,128]{1,0:T(8,128)(2,1)}, u32[]{:S(2)}) copy-start(bf16[4096,128]{1,0:T(8,128)(2,1)} %get-tuple-element.10.c_ref) | copy-start | bytes 3145732
Sparse Core Ops, SparseCore 0:
  12.1 65.7 all-gather.2

commit v17 on v16

--- a/solution.py
+++ b/solution.py
@@ -338,7 +338,7 @@
 
 
 def cross_kernel(n_req, spans, len_ref, normed_ref, enc_ref, w_ref, out_ref):
-    enc_len = len_ref[0]
+    enc_len = len_ref[2]
     (q_at, q_len), (kv_at, kv_len), (o_at, o_len) = spans
     nt = (((1,), (1,)), ((), ()))
     width = w_ref.shape[2]
@@ -410,7 +410,7 @@
         out_shape=jax.ShapeDtypeStruct(normed.shape, jnp.bfloat16),
         in_specs=[pl.BlockSpec(memory_space=pltpu.SMEM)] + [vmem] * 3,
         out_specs=vmem,
-    )(enc_len.reshape(1).astype(jnp.int32), normed, enc, blocks)
+    )(enc_len, normed, enc, blocks)
 
 
 def ffn_branch(normed, blocks, spans):
@@ -488,8 +488,8 @@
 
 
 def self_full_kernel(n_req, spans, lens_ref, x_ref, gain_ref, w_ref, c_ref, g_ref, f_ref, o_ref, ctx_ref):
-    old_len = lens_ref[0]
-    fresh_len = lens_ref[1]
+    fresh_len = lens_ref[0]
+    old_len = lens_ref[1]
     (q_at, q_len), (kv_at, kv_len), (o_at, o_len) = spans
     nt = (((1,), (1,)), ((), ()))
     width = w_ref.shape[2]
@@ -553,11 +553,10 @@
         ).astype(o_ref.dtype)
 
 
-def self_branch(states, gain, blocks, spans, cache_blk, line, old_len, fresh_len):
+def self_branch(states, gain, blocks, spans, cache_blk, line, lens):
     n_q = states.shape[0]
     n_ctx = cache_blk.shape[0]
-    g, f = bias_lines(line, old_len, n_q, n_ctx)
-    lens = jnp.stack([old_len, fresh_len]).astype(jnp.int32)
+    g, f = bias_lines(line, lens[1], n_q, n_ctx)
     vmem = pl.BlockSpec(memory_space=pltpu.VMEM)
     return pl.pallas_call(
         functools.partial(self_full_kernel, blocks.shape[0], tuple(spans)),
@@ -909,7 +908,7 @@
     own_slot = lax.dynamic_index_in_dim(slot_order, lax.axis_index("req"), 0, keepdims=False)
     tables = jnp.stack([new_lengths, cache_lengths, enc_lengths])
     picked = lax.dynamic_slice_in_dim(tables, own_slot, 1, 1)
-    slot_new, slot_old, slot_enc = picked[0], picked[1], picked[2]
+    lens = picked.reshape(-1).astype(jnp.int32)
     ordered = jnp.take(cache_in, slot_order, axis=0)
     onehot = (bucket_of[:, None] == jnp.arange(rel_bias.shape[0], dtype=jnp.int32)[None, :]).astype(
         jnp.float32
@@ -937,12 +936,11 @@
         block_spans(early),
         cache_blk,
         bias_dist[0],
-        slot_old[0],
-        slot_new[0],
+        lens,
     )
     residual, normed = blk_stage(part, own_rows, norm_gain[1], False)
     spans = block_spans(late)
-    part = cross_branch(normed, encoder_out, late_blocks, spans[:3], slot_enc[0])
+    part = cross_branch(normed, encoder_out, late_blocks, spans[:3], lens)
     residual, normed = blk_stage(part.astype(jnp.bfloat16), residual, norm_gain[2], False)
     part = ffn_branch(normed, late_blocks, spans[3:])
     _, layer_out = blk_stage(part, residual, norm_gain[2], True)

time: 189 us -> 188 us (level)
    unnamed x30 -> x32, local copies, waits for them, and re-layouts: 10.4 us -> 10.4 us
  transfers between devices with their start and end apart: 1 -> 1, of which waited for: 0 -> 0; matrix products, arithmetic and copies ran while one was open for 6% -> 5% of each run, Pallas kernels for 45% -> 45%
where the time goes in v17:
time: 188 us; the launch traced here: 187 us
  Pallas kernels  148 us (79%)
  between operations  17.5 us (9%)
  local copies, waits for them, and re-layouts  16.4 us (9%)
  other arithmetic  3.83 us (2%)
    pallas_call x3, Pallas kernels, blk_stage(): pl.pallas_call(functools.partial(stage_kernel, n_blk, final, extra), out_...  91.8 us
    pallas_call x1, Pallas kernels, prologue(): pl.pallas_call(functools.partial(prologue_kernel, n_req, n_blk), out_shap...  38.9 us
    unnamed x32, local copies, waits for them, and re-layouts  10.4 us
    pallas_call x1, Pallas kernels, self_branch(): pl.pallas_call(functools.partial(self_full_kernel, blocks.shape[0], tuple...  7.76 us
    pallas_call x1, Pallas kernels, cross_branch(): pl.pallas_call(functools.partial(cross_kernel, blocks.shape[0], tuple(spa...  4.99 us
    pallas_call x1, Pallas kernels, ffn_branch(): pl.pallas_call(functools.partial(ffn_kernel, blocks.shape[0], tuple(spans...  4.87 us
  transfers between devices with their start and end apart: 1, of which 0 were waited for; matrix products, arithmetic and copies ran while one was open for 5% of the time, Pallas kernels for 45%

profile of v17, /device:TPU:33, one launch (start us, length us, event | category | flops | bytes accessed | tf_op | source)
XLA Modules:
  0.0 187.1 jit_solution(15192557172221772285)
XLA Ops:
  7.2 0.0 copy-start
  7.2 0.0 all-gather.3.cloned.1.call-start
  7.2 0.8 bitcast_dynamic-update-slice_fusion
  8.0 0.8 constant_dynamic-update-slice_fusion.3
  8.8 0.7 constant_dynamic-update-slice_fusion.2
  9.5 0.9 constant_dynamic-update-slice_fusion.1
  10.5 0.8 constant_dynamic-update-slice_fusion
  11.3 0.7 copy-done.7
  11.9 0.0 all-gather.3.cloned.1.call-update
  12.0 1.2 dynamic_slice.16
  15.2 0.7 pad_add_fusion
  15.9 0.2 fusion.1
  16.0 0.5 slice.26
  17.9 1.0 convolution_reduce_fusion
  18.9 0.5 slice.33
  19.4 0.6 concatenate.10
  20.1 0.1 rev.3
  20.2 0.1 dynamic_slice.19
  20.3 0.7 pad_slice_fusion
  20.9 0.1 slice.28
  21.0 0.7 compare_select_fusion
  21.7 0.0 copy-done
  21.7 0.6 gather_fusion
  22.3 0.0 copy-done.8
  22.3 0.0 copy-done.9
  22.3 0.0 copy-done.10
  22.3 0.7 pad_maximum_fusion.packed_ref
  23.0 0.0 copy-done.12
  23.0 0.0 copy-start.11
  23.0 0.0 copy-start.4
  23.0 1.1 broadcast_select_fusion.ordered_ref
  24.2 38.9 %shard_map.185 = (bf16[4096,128]{1,0:T(8,128)(2,1)}, bf16[8,256,128]{2,1,0:T(8,128)(2,1)}) custom-call(bf16[8,256,256]{2,1,0:T(8,128)(2,1)} %broadcast_select_fusion.ordered_ref, bf16[256,128]{1,0:T(8,128)(2,1)} %pad_maximum_fusion.packed_ref), custom_call_target="tpu_custom_call" | custom-call | tf_op jit(solution)/shard_map/pallas_call | solution.py:841
  63.1 0.6 fusion.2
  63.7 0.0 copy-done.4
  63.7 1.2 copy-done.1
  64.9 1.0 copy-done.5
  65.9 7.8 %shard_map.186.refs_0_ = bf16[512,1024]{1,0:T(8,128)(2,1)S(1)} custom-call(s32[3]{0:T(128)S(1)} %get-tuple-element.16.lens_ref.len_ref, bf16[512,1024]{1,0:T(8,128)(2,1)S(1)} %copy-done.4, f32[1,1024]{1,0:T(1,128)S(1)} %get-tuple-element.19.gain_ref, bf16[8,256,128]{2,1,0:T(8,128)(2,1)S(1)} %copy-done.5, bf16[4096,128]{1,0:T(8,128)(2,1)S(1)} %copy-done.1, ...), custom_call_target="tpu_custom_call" | custom-call | tf_op jit(solution)/shard_map/pallas_call | solution.py:561
  73.7 0.0 copy-start.3
  73.7 1.0 copy-done.3
  74.7 0.7 dynamic-slice_convert_fusion.refs_1_
  75.4 38.0 %shard_map.187 = (f32[32,1024]{1,0:T(8,128)}, bf16[512,1024]{1,0:T(8,128)(2,1)}) custom-call(bf16[512,1024]{1,0:T(8,128)(2,1)} %copy-done.3, f32[32,1024]{1,0:T(8,128)} %dynamic-slice_convert_fusion.refs_1_, f32[1,1024]{1,0:T(1,128)} %get-tuple-element.20.refs_2_), custom_call_target="tpu_custom_call" | custom-call | tf_op jit(solution)/shard_map/pallas_call | solution.py:328
  113.4 0.0 all-gather.3.cloned.1.call-done
  113.4 5.0 %shard_map.188.refs_0_ = bf16[512,1024]{1,0:T(8,128)(2,1)} custom-call(s32[3]{0:T(128)} %copy-done.6, bf16[512,1024]{1,0:T(8,128)(2,1)} %get-tuple-element.11.normed_ref, bf16[512,1024]{1,0:T(8,128)(2,1)} %enc_ref.1, bf16[8,784,128]{2,1,0:T(8,128)(2,1)} %bitcast.25), custom_call_target="tpu_custom_call" | custom-call | tf_op jit(solution)/shard_map/pallas_call | solution.py:408
  118.4 26.4 %shard_map.189 = (f32[32,1024]{1,0:T(8,128)}, bf16[512,1024]{1,0:T(8,128)(2,1)}) custom-call(bf16[512,1024]{1,0:T(8,128)(2,1)} %shard_map.188.refs_0_, f32[32,1024]{1,0:T(8,128)} %get-tuple-element.12.refs_1_, f32[1,1024]{1,0:T(1,128)} %get-tuple-element.18.refs_2_), custom_call_target="tpu_custom_call" | custom-call | tf_op jit(solution)/shard_map/pallas_call | solution.py:328
  144.9 4.9 %shard_map.190.refs_0_ = bf16[512,1024]{1,0:T(8,128)(2,1)} custom-call(bf16[512,1024]{1,0:T(8,128)(2,1)} %get-tuple-element.13.normed_ref, bf16[8,784,128]{2,1,0:T(8,128)(2,1)} %bitcast.26), custom_call_target="tpu_custom_call" | custom-call | tf_op jit(solution)/shard_map/pallas_call | solution.py:418
  149.7 27.3 %shard_map.191 = (f32[32,1024]{1,0:T(8,128)}, bf16[512,1024]{1,0:T(8,128)(2,1)}) custom-call(bf16[512,1024]{1,0:T(8,128)(2,1)} %shard_map.190.refs_0_, f32[32,1024]{1,0:T(8,128)} %get-tuple-element.14.refs_1_, f32[1,1024]{1,0:T(1,128)} %get-tuple-element.18.refs_2_), custom_call_target="tpu_custom_call" | custom-call | tf_op jit(solution)/shard_map/pallas_call | solution.py:328
  177.0 2.3 %copy.26 = bf16[512,1024]{1,0:T(8,128)(2,1)} copy(bf16[512,1024]{1,0:T(8,128)(2,1)} %get-tuple-element.23) | data formatting | bytes 2097152
  179.3 1.0 copy.27
  (15 shorter events, 0.0 us)
Async XLA Ops:
  7.2 14.5 %copy-start = (bf16[8,256,256]{2,1,0:T(8,128)(2,1)S(1)}, bf16[8,256,256]{2,1,0:T(8,128)(2,1)}, u32[]{:S(2)}) copy-start(bf16[8,256,256]{2,1,0:T(8,128)(2,1)} %param.20) | copy-start | bytes 3145732
  7.2 106.2 %all-gather.3.cloned.1.call-start = ((), (), s32[]{:S(2)}) async-start(), calls=%async_computation | async-start | bytes 1806336 | tf_op jit(solution)/shard_map/all_gather | solution.py:881
  8.0 14.3 %copy-start.8 = (bf16[128,2,64]{0,2,1:T(8,128)(2,1)S(1)}, bf16[128,2,64]{0,2,1:T(8,128)(2,1)}, u32[]{:S(2)}) copy-start(bf16[128,2,64]{0,2,1:T(8,128)(2,1)} %param.29) | copy-start | bytes 98308
  8.0 14.3 %copy-start.9 = (bf16[64,128]{1,0:T(8,128)(2,1)S(1)}, bf16[64,128]{1,0:T(8,128)(2,1)}, u32[]{:S(2)}) copy-start(bf16[64,128]{1,0:T(8,128)(2,1)} %param.30) | copy-start | bytes 49156
  8.0 14.3 %copy-start.10 = (bf16[128,64]{0,1:T(8,128)(2,1)S(1)}, bf16[128,64]{0,1:T(8,128)(2,1)}, u32[]{:S(2)}) copy-start(bf16[128,64]{0,1:T(8,128)(2,1)} %param.28) | copy-start | bytes 49156
  9.5 13.5 %copy-start.12 = (s32[8]{0:T(128)S(1)}, s32[8]{0:T(128)}, u32[]{:S(2)}) copy-start(s32[8]{0:T(128)} %param.21) | copy-start | bytes 100
  11.3 0.7 copy-start.7
  16.0 47.6 %copy-start.6 = (s32[3]{0:T(128)}, s32[3]{0:T(128)S(1)}, u32[]{:S(2)}) copy-start(s32[3]{0:T(128)S(1)} %get-tuple-element.16.lens_ref.len_ref) | copy-start | bytes 40
  23.0 40.1 %copy-start.11 = (f32[3,1024]{1,0:T(4,128)S(1)}, f32[3,1024]{1,0:T(4,128)}, u32[]{:S(2)}) copy-start(f32[3,1024]{1,0:T(4,128)} %param.27) | copy-start | bytes 36868
  23.0 40.7 %copy-start.4 = (bf16[512,1024]{1,0:T(8,128)(2,1)S(1)}, bf16[512,1024]{1,0:T(8,128)(2,1)}, u32[]{:S(2)}) copy-start(bf16[512,1024]{1,0:T(8,128)(2,1)} %x_ref.1) | copy-start | bytes 3145732
  63.7 1.2 copy-start.1
  64.9 1.0 copy-start.5
  73.7 1.0 copy-start.3
  149.7 29.6 %copy-start.2 = (bf16[4096,128]{1,0:T(8,128)(2,1)S(1)}, bf16[4096,128]{1,0:T(8,128)(2,1)}, u32[]{:S(2)}) copy-start(bf16[4096,128]{1,0:T(8,128)(2,1)} %get-tuple-element.10.c_ref) | copy-start | bytes 3145732
Sparse Core Ops, SparseCore 0:
  12.1 65.2 all-gather.2

commit v18 on v17

--- a/solution.py
+++ b/solution.py
@@ -487,7 +487,11 @@
     )(lens, q, cache_blk, k_new, v_new, g, f)
 
 
-def self_full_kernel(n_req, spans, lens_ref, x_ref, gain_ref, w_ref, c_ref, g_ref, f_ref, o_ref, ctx_ref):
+def self_full_kernel(n_req, spans, lens_ref, x_ref, gain_ref, w_hbm, c_hbm, g_ref, f_ref, o_ref, ctx_ref, w_ref, c_ref, sems):
+    w_copy = pltpu.make_async_copy(w_hbm, w_ref, sems.at[0])
+    c_copy = pltpu.make_async_copy(c_hbm, c_ref, sems.at[1])
+    w_copy.start()
+    c_copy.start()
     fresh_len = lens_ref[0]
     old_len = lens_ref[1]
     (q_at, q_len), (kv_at, kv_len), (o_at, o_len) = spans
@@ -496,6 +500,7 @@
     x = x_ref[...].astype(jnp.float32)
     mean_square = jnp.mean(x * x, axis=-1, keepdims=True)
     normed = (x * lax.rsqrt(mean_square + EPSILON) * gain_ref[...]).astype(jnp.bfloat16)
+    w_copy.wait()
     queries = None
     pair = None
     for r in range(n_req):
@@ -518,6 +523,7 @@
     n_ctx = c_ref.shape[0]
     wide_old = n_ctx + TQ
     wide_new = n_q + TQ
+    c_copy.wait()
     k_old = c_ref[:, :HD]
     v_old = c_ref[:, HD:]
     for t in range(n_q // TQ):
@@ -561,9 +567,16 @@
     return pl.pallas_call(
         functools.partial(self_full_kernel, blocks.shape[0], tuple(spans)),
         out_shape=jax.ShapeDtypeStruct(states.shape, jnp.bfloat16),
-        in_specs=[pl.BlockSpec(memory_space=pltpu.SMEM)] + [vmem] * 6,
+        in_specs=[pl.BlockSpec(memory_space=pltpu.SMEM), vmem, vmem]
+        + [pl.BlockSpec(memory_space=pl.ANY)] * 2
+        + [vmem] * 2,
         out_specs=vmem,
-        scratch_shapes=[pltpu.VMEM((n_q, HD), jnp.bfloat16)],
+        scratch_shapes=[
+            pltpu.VMEM((n_q, HD), jnp.bfloat16),
+            pltpu.VMEM(blocks.shape, blocks.dtype),
+            pltpu.VMEM(cache_blk.shape, cache_blk.dtype),
+            pltpu.SemaphoreType.DMA((2,)),
+        ],
         compiler_params=pltpu.CompilerParams(vmem_limit_bytes=48 * 1024 * 1024),
     )(lens, states, gain[None, :], blocks, cache_blk, g, f)
 

time: 188 us -> 188 us (level)
  no operation moved by 1% of the time
where the time goes in v18:
time: 188 us
  Pallas kernels  149 us (79%)
  between operations  17.5 us (9%)
  local copies, waits for them, and re-layouts  16.4 us (9%)
  other arithmetic  3.83 us (2%)
    pallas_call x3, Pallas kernels, blk_stage(): pl.pallas_call(functools.partial(stage_kernel, n_blk, final, extra), out_...  91.7 us
    pallas_call x1, Pallas kernels, prologue(): pl.pallas_call(functools.partial(prologue_kernel, n_req, n_blk), out_shap...  38.9 us
    unnamed x32, local copies, waits for them, and re-layouts  10.4 us
    pallas_call x1, Pallas kernels, self_branch(): pl.pallas_call(functools.partial(self_full_kernel, blocks.shape[0], tuple...  8.3 us
    pallas_call x1, Pallas kernels, cross_branch(): pl.pallas_call(functools.partial(cross_kernel, blocks.shape[0], tuple(spa...  4.99 us
    pallas_call x1, Pallas kernels, ffn_branch(): pl.pallas_call(functools.partial(ffn_kernel, blocks.shape[0], tuple(spans...  4.86 us
  transfers between devices with their start and end apart: 1, of which 0 were waited for; matrix products, arithmetic and copies ran while one was open for 5% of the time, Pallas kernels for 45%

profile of v18, /device:TPU:33, one launch (start us, length us, event | category | flops | bytes accessed | tf_op | source)
XLA Modules:
  0.0 187.6 jit_solution(18314610641184814823)
XLA Ops:
  7.2 0.0 copy-start
  7.2 0.0 all-gather.3.cloned.1.call-start
  7.2 0.8 bitcast_dynamic-update-slice_fusion
  8.0 0.8 constant_dynamic-update-slice_fusion.3
  8.8 0.7 constant_dynamic-update-slice_fusion.2
  9.5 0.9 constant_dynamic-update-slice_fusion.1
  10.5 0.8 constant_dynamic-update-slice_fusion
  11.3 0.7 copy-done.7
  11.9 0.0 all-gather.3.cloned.1.call-update
  12.0 1.2 dynamic_slice.16
  15.2 0.7 pad_add_fusion
  15.9 0.2 fusion.1
  16.0 0.5 slice.26
  17.9 1.0 convolution_reduce_fusion
  18.9 0.5 slice.33
  19.4 0.6 concatenate.10
  20.1 0.1 rev.3
  20.2 0.1 dynamic_slice.19
  20.3 0.7 pad_slice_fusion
  20.9 0.1 slice.28
  21.0 0.7 compare_select_fusion
  21.7 0.0 copy-done
  21.7 0.6 gather_fusion
  22.3 0.0 copy-done.8
  22.3 0.0 copy-done.9
  22.3 0.7 pad_maximum_fusion.packed_ref
  23.0 0.0 copy-done.12
  23.0 0.0 copy-start.11
  23.0 0.0 copy-start.4
  23.0 1.1 broadcast_select_fusion.ordered_ref
  24.2 38.9 %shard_map.185 = (bf16[4096,128]{1,0:T(8,128)(2,1)}, bf16[8,256,128]{2,1,0:T(8,128)(2,1)}) custom-call(bf16[8,256,256]{2,1,0:T(8,128)(2,1)} %broadcast_select_fusion.ordered_ref, bf16[256,128]{1,0:T(8,128)(2,1)} %pad_maximum_fusion.packed_ref), custom_call_target="tpu_custom_call" | custom-call | tf_op jit(solution)/shard_map/pallas_call | solution.py:854
  63.1 0.6 fusion.2
  63.7 0.0 copy-done.4
  63.7 1.2 copy-done.1
  64.9 1.0 copy-done.5
  65.9 8.3 %shard_map.186.refs_0_ = bf16[512,1024]{1,0:T(8,128)(2,1)S(1)} custom-call(s32[3]{0:T(128)S(1)} %get-tuple-element.16.lens_ref.len_ref, bf16[512,1024]{1,0:T(8,128)(2,1)S(1)} %copy-done.4, f32[1,1024]{1,0:T(1,128)S(1)} %get-tuple-element.19.gain_ref, bf16[8,256,128]{2,1,0:T(8,128)(2,1)S(1)} %copy-done.5, bf16[4096,128]{1,0:T(8,128)(2,1)S(1)} %copy-done.1, ...), custom_call_target="tpu_custom_call" | custom-call | tf_op jit(solution)/shard_map/pallas_call | solution.py:567
  74.3 0.0 copy-start.3
  74.3 1.0 copy-done.3
  75.2 0.7 dynamic-slice_convert_fusion.refs_1_
  75.9 38.0 %shard_map.187 = (f32[32,1024]{1,0:T(8,128)}, bf16[512,1024]{1,0:T(8,128)(2,1)}) custom-call(bf16[512,1024]{1,0:T(8,128)(2,1)} %copy-done.3, f32[32,1024]{1,0:T(8,128)} %dynamic-slice_convert_fusion.refs_1_, f32[1,1024]{1,0:T(1,128)} %get-tuple-element.20.refs_2_), custom_call_target="tpu_custom_call" | custom-call | tf_op jit(solution)/shard_map/pallas_call | solution.py:328
  113.9 0.0 all-gather.3.cloned.1.call-done
  114.0 5.0 %shard_map.188.refs_0_ = bf16[512,1024]{1,0:T(8,128)(2,1)} custom-call(s32[3]{0:T(128)} %copy-done.6, bf16[512,1024]{1,0:T(8,128)(2,1)} %get-tuple-element.11.normed_ref, bf16[512,1024]{1,0:T(8,128)(2,1)} %enc_ref.1, bf16[8,784,128]{2,1,0:T(8,128)(2,1)} %bitcast.25), custom_call_target="tpu_custom_call" | custom-call | tf_op jit(solution)/shard_map/pallas_call | solution.py:408
  118.9 26.4 %shard_map.189 = (f32[32,1024]{1,0:T(8,128)}, bf16[512,1024]{1,0:T(8,128)(2,1)}) custom-call(bf16[512,1024]{1,0:T(8,128)(2,1)} %shard_map.188.refs_0_, f32[32,1024]{1,0:T(8,128)} %get-tuple-element.12.refs_1_, f32[1,1024]{1,0:T(1,128)} %get-tuple-element.18.refs_2_), custom_call_target="tpu_custom_call" | custom-call | tf_op jit(solution)/shard_map/pallas_call | solution.py:328
  145.4 4.9 %shard_map.190.refs_0_ = bf16[512,1024]{1,0:T(8,128)(2,1)} custom-call(bf16[512,1024]{1,0:T(8,128)(2,1)} %get-tuple-element.13.normed_ref, bf16[8,784,128]{2,1,0:T(8,128)(2,1)} %bitcast.26), custom_call_target="tpu_custom_call" | custom-call | tf_op jit(solution)/shard_map/pallas_call | solution.py:418
  150.3 27.3 %shard_map.191 = (f32[32,1024]{1,0:T(8,128)}, bf16[512,1024]{1,0:T(8,128)(2,1)}) custom-call(bf16[512,1024]{1,0:T(8,128)(2,1)} %shard_map.190.refs_0_, f32[32,1024]{1,0:T(8,128)} %get-tuple-element.14.refs_1_, f32[1,1024]{1,0:T(1,128)} %get-tuple-element.18.refs_2_), custom_call_target="tpu_custom_call" | custom-call | tf_op jit(solution)/shard_map/pallas_call | solution.py:328
  177.5 2.3 %copy.26 = bf16[512,1024]{1,0:T(8,128)(2,1)} copy(bf16[512,1024]{1,0:T(8,128)(2,1)} %get-tuple-element.23) | data formatting | bytes 2097152
  179.8 0.0 copy-done.2
  179.8 1.0 copy.27
  (15 shorter events, 0.0 us)
Async XLA Ops:
  7.2 14.5 %copy-start = (bf16[8,256,256]{2,1,0:T(8,128)(2,1)S(1)}, bf16[8,256,256]{2,1,0:T(8,128)(2,1)}, u32[]{:S(2)}) copy-start(bf16[8,256,256]{2,1,0:T(8,128)(2,1)} %param.20) | copy-start | bytes 3145732
  7.2 106.8 %all-gather.3.cloned.1.call-start = ((), (), s32[]{:S(2)}) async-start(), calls=%async_computation | async-start | bytes 1806336 | tf_op jit(solution)/shard_map/all_gather | solution.py:894
  8.0 14.3 %copy-start.8 = (bf16[128,2,64]{0,2,1:T(8,128)(2,1)S(1)}, bf16[128,2,64]{0,2,1:T(8,128)(2,1)}, u32[]{:S(2)}) copy-start(bf16[128,2,64]{0,2,1:T(8,128)(2,1)} %param.29) | copy-start | bytes 98308
  8.0 14.3 %copy-start.9 = (bf16[64,128]{1,0:T(8,128)(2,1)S(1)}, bf16[64,128]{1,0:T(8,128)(2,1)}, u32[]{:S(2)}) copy-start(bf16[64,128]{1,0:T(8,128)(2,1)} %param.30) | copy-start | bytes 49156
  8.0 14.3 %copy-start.10 = (bf16[128,64]{0,1:T(8,128)(2,1)S(1)}, bf16[128,64]{0,1:T(8,128)(2,1)}, u32[]{:S(2)}) copy-start(bf16[128,64]{0,1:T(8,128)(2,1)} %param.28) | copy-start | bytes 49156
  9.5 13.5 %copy-start.12 = (s32[8]{0:T(128)S(1)}, s32[8]{0:T(128)}, u32[]{:S(2)}) copy-start(s32[8]{0:T(128)} %param.21) | copy-start | bytes 100
  11.3 0.7 copy-start.7
  16.0 47.6 %copy-start.6 = (s32[3]{0:T(128)}, s32[3]{0:T(128)S(1)}, u32[]{:S(2)}) copy-start(s32[3]{0:T(128)S(1)} %get-tuple-element.16.lens_ref.len_ref) | copy-start | bytes 40
  23.0 40.1 %copy-start.11 = (f32[3,1024]{1,0:T(4,128)S(1)}, f32[3,1024]{1,0:T(4,128)}, u32[]{:S(2)}) copy-start(f32[3,1024]{1,0:T(4,128)} %param.27) | copy-start | bytes 36868
  23.0 40.7 %copy-start.4 = (bf16[512,1024]{1,0:T(8,128)(2,1)S(1)}, bf16[512,1024]{1,0:T(8,128)(2,1)}, u32[]{:S(2)}) copy-start(bf16[512,1024]{1,0:T(8,128)(2,1)} %x_ref.1) | copy-start | bytes 3145732
  63.7 1.2 copy-start.1
  64.9 1.0 copy-start.5
  74.3 1.0 copy-start.3
  150.3 29.5 %copy-start.2 = (bf16[4096,128]{1,0:T(8,128)(2,1)S(1)}, bf16[4096,128]{1,0:T(8,128)(2,1)}, u32[]{:S(2)}) copy-start(bf16[4096,128]{1,0:T(8,128)(2,1)} %get-tuple-element.10.c_hbm) | copy-start | bytes 3145732
Sparse Core Ops, SparseCore 0:
  12.1 65.2 all-gather.2

commit v19 on v17

--- a/solution.py
+++ b/solution.py
@@ -332,7 +332,9 @@
         out_specs=tuple([vmem] * len(outs)),
         scratch_shapes=scratch,
         compiler_params=pltpu.CompilerParams(
-            collective_id=5 if extra else (4 if final else 3), has_side_effects=True
+            collective_id=5 if extra else (4 if final else 3),
+            has_side_effects=True,
+            vmem_limit_bytes=16 * 1024 * 1024,
         ),
     )(*args)
 
@@ -410,6 +412,7 @@
         out_shape=jax.ShapeDtypeStruct(normed.shape, jnp.bfloat16),
         in_specs=[pl.BlockSpec(memory_space=pltpu.SMEM)] + [vmem] * 3,
         out_specs=vmem,
+        compiler_params=pltpu.CompilerParams(vmem_limit_bytes=16 * 1024 * 1024),
     )(enc_len, normed, enc, blocks)
 
 
@@ -420,6 +423,7 @@
         out_shape=jax.ShapeDtypeStruct(normed.shape, jnp.bfloat16),
         in_specs=[vmem] * 2,
         out_specs=vmem,
+        compiler_params=pltpu.CompilerParams(vmem_limit_bytes=16 * 1024 * 1024),
     )(normed, blocks)
 
 
@@ -483,7 +487,7 @@
         out_shape=jax.ShapeDtypeStruct((n_q, HD), jnp.bfloat16),
         in_specs=[pl.BlockSpec(memory_space=pltpu.SMEM)] + [vmem] * 6,
         out_specs=vmem,
-        compiler_params=pltpu.CompilerParams(vmem_limit_bytes=48 * 1024 * 1024),
+        compiler_params=pltpu.CompilerParams(vmem_limit_bytes=24 * 1024 * 1024),
     )(lens, q, cache_blk, k_new, v_new, g, f)
 
 
@@ -564,7 +568,7 @@
         in_specs=[pl.BlockSpec(memory_space=pltpu.SMEM)] + [vmem] * 6,
         out_specs=vmem,
         scratch_shapes=[pltpu.VMEM((n_q, HD), jnp.bfloat16)],
-        compiler_params=pltpu.CompilerParams(vmem_limit_bytes=48 * 1024 * 1024),
+        compiler_params=pltpu.CompilerParams(vmem_limit_bytes=24 * 1024 * 1024),
     )(lens, states, gain[None, :], blocks, cache_blk, g, f)
 
 

time: 188 us -> 174 us (0.926)
  Pallas kernels: 148 us -> 137 us
    pallas_call x3, Pallas kernels: 91.8 us -> 85.4 us  [blk_stage(): pl.pallas_call(functools.partial(stage_kernel, n_blk, final, extra), out_...]
    pallas_call x1, Pallas kernels: 4.87 us -> 2.15 us  [ffn_branch(): pl.pallas_call(functools.partial(ffn_kernel, blocks.shape[0], tuple(spans...]
    pallas_call x1, Pallas kernels: 4.99 us -> 2.48 us  [cross_branch(): pl.pallas_call(functools.partial(cross_kernel, blocks.shape[0], tuple(spa...]
    unnamed x32 -> x34, local copies, waits for them, and re-layouts: 10.4 us -> 9.55 us
  transfers between devices with their start and end apart: 1 -> 1, of which waited for: 0 -> 0; matrix products, arithmetic and copies ran while one was open for 5% -> 5% of each run, Pallas kernels for 45% -> 47%
where the time goes in v19:
time: 174 us; the launch traced here: 173 us
  Pallas kernels  137 us (79%)
  between operations  17.5 us (10%)
  local copies, waits for them, and re-layouts  15 us (9%)
  other arithmetic  3.15 us (2%)
    pallas_call x3, Pallas kernels, blk_stage(): pl.pallas_call(functools.partial(stage_kernel, n_blk, final, extra), out_...  85.4 us
    pallas_call x1, Pallas kernels, prologue(): pl.pallas_call(functools.partial(prologue_kernel, n_req, n_blk), out_shap...  38.9 us
    unnamed x34, local copies, waits for them, and re-layouts  9.55 us
    pallas_call x1, Pallas kernels, self_branch(): pl.pallas_call(functools.partial(self_full_kernel, blocks.shape[0], tuple...  7.77 us
  transfers between devices with their start and end apart: 1, of which 0 were waited for; matrix products, arithmetic and copies ran while one was open for 5% of the time, Pallas kernels for 47%

profile of v19, /device:TPU:33, one launch (start us, length us, event | category | flops | bytes accessed | tf_op | source)
XLA Modules:
  0.0 173.5 jit_solution(7338502754617893031)
XLA Ops:
  7.2 0.0 copy-start
  7.2 0.0 all-gather.3.cloned.1.call-start
  7.2 0.8 bitcast_dynamic-update-slice_fusion
  8.0 0.8 constant_dynamic-update-slice_fusion.3
  8.8 0.7 constant_dynamic-update-slice_fusion.2
  9.5 0.9 constant_dynamic-update-slice_fusion.1
  10.5 0.8 constant_dynamic-update-slice_fusion
  11.3 0.7 copy-done.8
  11.9 0.0 all-gather.3.cloned.1.call-update
  12.0 1.2 dynamic_slice.16
  15.2 0.7 pad_add_fusion
  15.9 0.2 fusion.1
  16.0 0.5 slice.26
  17.9 1.0 convolution_reduce_fusion
  18.9 0.5 slice.33
  19.4 0.6 concatenate.10
  20.1 0.1 rev.3
  20.2 0.1 dynamic_slice.19
  20.3 0.7 pad_slice_fusion
  20.9 0.1 slice.28
  21.0 0.7 compare_select_fusion
  21.7 0.0 copy-done
  21.7 0.6 gather_fusion
  22.3 0.0 copy-done.9
  22.3 0.0 copy-done.10
  22.3 0.0 copy-done.11
  22.3 0.6 pad_maximum_fusion.packed_ref
  23.0 0.0 copy-done.13
  23.0 0.0 copy-start.12
  23.0 0.0 copy-start.5
  23.0 1.1 broadcast_select_fusion.ordered_ref
  24.1 38.9 %shard_map.185 = (bf16[4096,128]{1,0:T(8,128)(2,1)}, bf16[8,256,128]{2,1,0:T(8,128)(2,1)}) custom-call(bf16[8,256,256]{2,1,0:T(8,128)(2,1)} %broadcast_select_fusion.ordered_ref, bf16[256,128]{1,0:T(8,128)(2,1)} %pad_maximum_fusion.packed_ref), custom_call_target="tpu_custom_call" | custom-call | tf_op jit(solution)/shard_map/pallas_call | solution.py:845
  63.0 0.0 copy-done.12
  63.1 1.2 copy-done.3
  64.3 1.0 copy-done.7
  65.3 7.8 %shard_map.186.refs_0_ = bf16[512,1024]{1,0:T(8,128)(2,1)S(1)} custom-call(s32[3]{0:T(128)S(1)} %get-tuple-element.16.lens_ref.len_ref, bf16[512,1024]{1,0:T(8,128)(2,1)S(1)} %copy-done.5, f32[1,1024]{1,0:T(1,128)S(1)} %get-tuple-element.19.gain_ref, bf16[8,256,128]{2,1,0:T(8,128)(2,1)S(1)} %copy-done.7, bf16[4096,128]{1,0:T(8,128)(2,1)S(1)} %copy-done.3, ...), custom_call_target="tpu_custom_call" | custom-call | tf_op jit(solution)/shard_map/pallas_call | solution.py:565
  73.1 0.0 copy-start.6
  73.1 35.6 %shard_map.187 = (f32[32,1024]{1,0:T(8,128)S(1)}, bf16[512,1024]{1,0:T(8,128)(2,1)S(1)}) custom-call(bf16[512,1024]{1,0:T(8,128)(2,1)S(1)} %shard_map.186.refs_0_, f32[32,1024]{1,0:T(8,128)S(1)} %dynamic-slice_convert_fusion.refs_1_, f32[1,1024]{1,0:T(1,128)S(1)} %get-tuple-element.20.refs_2_), custom_call_target="tpu_custom_call" | custom-call | tf_op jit(solution)/shard_map/pallas_call | solution.py:328
  108.8 0.0 all-gather.3.cloned.1.call-done
  108.8 1.4 copy-done.1
  110.2 2.5 %shard_map.188.refs_0_ = bf16[512,1024]{1,0:T(8,128)(2,1)S(1)} custom-call(s32[3]{0:T(128)S(1)} %get-tuple-element.16.lens_ref.len_ref, bf16[512,1024]{1,0:T(8,128)(2,1)S(1)} %get-tuple-element.11.normed_ref, bf16[512,1024]{1,0:T(8,128)(2,1)S(1)} %copy-done.6, bf16[8,784,128]{2,1,0:T(8,128)(2,1)S(1)} %bitcast.23), custom_call_target="tpu_custom_call" | custom-call | tf_op jit(solution)/shard_map/pallas_call | solution.py:410
  112.7 24.6 %shard_map.189 = (f32[32,1024]{1,0:T(8,128)S(1)}, bf16[512,1024]{1,0:T(8,128)(2,1)S(1)}) custom-call(bf16[512,1024]{1,0:T(8,128)(2,1)S(1)} %shard_map.188.refs_0_, f32[32,1024]{1,0:T(8,128)S(1)} %get-tuple-element.12.refs_1_, f32[1,1024]{1,0:T(1,128)S(1)} %get-tuple-element.18.refs_2_), custom_call_target="tpu_custom_call" | custom-call | tf_op jit(solution)/shard_map/pallas_call | solution.py:328
  137.3 2.1 %shard_map.190.refs_0_ = bf16[512,1024]{1,0:T(8,128)(2,1)S(1)} custom-call(bf16[512,1024]{1,0:T(8,128)(2,1)S(1)} %get-tuple-element.13.normed_ref, bf16[8,784,128]{2,1,0:T(8,128)(2,1)S(1)} %bitcast.24), custom_call_target="tpu_custom_call" | custom-call | tf_op jit(solution)/shard_map/pallas_call | solution.py:421
  139.5 0.0 copy-start.4
  139.5 25.2 %shard_map.191 = (f32[32,1024]{1,0:T(8,128)}, bf16[512,1024]{1,0:T(8,128)(2,1)S(1)}) custom-call(bf16[512,1024]{1,0:T(8,128)(2,1)S(1)} %shard_map.190.refs_0_, f32[32,1024]{1,0:T(8,128)S(1)} %get-tuple-element.14.refs_1_, f32[1,1024]{1,0:T(1,128)S(1)} %get-tuple-element.18.refs_2_), custom_call_target="tpu_custom_call" | custom-call | tf_op jit(solution)/shard_map/pallas_call | solution.py:328
  164.7 1.0 copy.26
  165.7 0.0 copy-done.4
  165.7 1.0 copy.27
  (17 shorter events, 0.1 us)
Async XLA Ops:
  7.2 14.5 %copy-start = (bf16[8,256,256]{2,1,0:T(8,128)(2,1)S(1)}, bf16[8,256,256]{2,1,0:T(8,128)(2,1)}, u32[]{:S(2)}) copy-start(bf16[8,256,256]{2,1,0:T(8,128)(2,1)} %param.20) | copy-start | bytes 3145732
  7.2 101.6 %all-gather.3.cloned.1.call-start = ((), (), s32[]{:S(2)}) async-start(), calls=%async_computation | async-start | bytes 1806336 | tf_op jit(solution)/shard_map/all_gather | solution.py:885
  8.0 14.3 %copy-start.9 = (bf16[128,2,64]{0,2,1:T(8,128)(2,1)S(1)}, bf16[128,2,64]{0,2,1:T(8,128)(2,1)}, u32[]{:S(2)}) copy-start(bf16[128,2,64]{0,2,1:T(8,128)(2,1)} %param.29) | copy-start | bytes 98308
  8.0 14.3 %copy-start.10 = (bf16[64,128]{1,0:T(8,128)(2,1)S(1)}, bf16[64,128]{1,0:T(8,128)(2,1)}, u32[]{:S(2)}) copy-start(bf16[64,128]{1,0:T(8,128)(2,1)} %param.30) | copy-start | bytes 49156
  8.0 14.3 %copy-start.11 = (bf16[128,64]{0,1:T(8,128)(2,1)S(1)}, bf16[128,64]{0,1:T(8,128)(2,1)}, u32[]{:S(2)}) copy-start(bf16[128,64]{0,1:T(8,128)(2,1)} %param.28) | copy-start | bytes 49156
  9.5 13.4 %copy-start.13 = (s32[8]{0:T(128)S(1)}, s32[8]{0:T(128)}, u32[]{:S(2)}) copy-start(s32[8]{0:T(128)} %param.21) | copy-start | bytes 100
  11.3 0.7 copy-start.8
  23.0 40.1 %copy-start.12 = (f32[3,1024]{1,0:T(4,128)S(1)}, f32[3,1024]{1,0:T(4,128)}, u32[]{:S(2)}) copy-start(f32[3,1024]{1,0:T(4,128)} %param.27) | copy-start | bytes 36868
  23.0 40.1 %copy-start.5 = (bf16[512,1024]{1,0:T(8,128)(2,1)S(1)}, bf16[512,1024]{1,0:T(8,128)(2,1)}, u32[]{:S(2)}) copy-start(bf16[512,1024]{1,0:T(8,128)(2,1)} %x_ref.1) | copy-start | bytes 3145732
  63.1 1.2 copy-start.3
  64.3 1.0 copy-start.7
  73.1 35.7 %copy-start.6 = (bf16[512,1024]{1,0:T(8,128)(2,1)S(1)}, bf16[512,1024]{1,0:T(8,128)(2,1)}, u32[]{:S(2)}) copy-start(bf16[512,1024]{1,0:T(8,128)(2,1)} %enc_ref.1) | copy-start | bytes 3145732
  108.8 1.4 copy-start.1
  110.2 27.1 %copy-start.2 = (bf16[6272,128]{1,0:T(8,128)(2,1)S(1)}, bf16[6272,128]{1,0:T(8,128)(2,1)}, u32[]{:S(2)}) copy-start(bf16[6272,128]{1,0:T(8,128)(2,1)} %all-gather.3.cloned.1.call-done) | copy-start | bytes 4816900
  139.5 26.2 %copy-start.4 = (bf16[4096,128]{1,0:T(8,128)(2,1)S(1)}, bf16[4096,128]{1,0:T(8,128)(2,1)}, u32[]{:S(2)}) copy-start(bf16[4096,128]{1,0:T(8,128)(2,1)} %get-tuple-element.10.c_ref) | copy-start | bytes 3145732
Sparse Core Ops, SparseCore 0:
  12.1 65.4 all-gather.2

commit v20 on v19

--- a/solution.py
+++ b/solution.py
@@ -857,7 +857,9 @@
             pltpu.SemaphoreType.DMA((n_blk,)),
             pltpu.SemaphoreType.DMA((1,)),
         ],
-        compiler_params=pltpu.CompilerParams(has_side_effects=True),
+        compiler_params=pltpu.CompilerParams(
+            has_side_effects=True, vmem_limit_bytes=32 * 1024 * 1024
+        ),
     )(ordered, packed)
 
 

time: 174 us -> 172 us (0.989)
  Pallas kernels: 137 us -> 135 us
  local copies, waits for them, and re-layouts: 15 us -> 16.8 us
    unnamed x34 -> x36, local copies, waits for them, and re-layouts: 9.55 us -> 11.3 us
  transfers between devices with their start and end apart: 1 -> 1, of which waited for: 0 -> 0; matrix products, arithmetic and copies ran while one was open for 5% -> 4% of each run, Pallas kernels for 47% -> 47%
where the time goes in v20:
time: 172 us; the launch traced here: 171 us
  Pallas kernels  135 us (78%)
  between operations  17.5 us (10%)
  local copies, waits for them, and re-layouts  16.8 us (10%)
    pallas_call x3, Pallas kernels, blk_stage(): pl.pallas_call(functools.partial(stage_kernel, n_blk, final, extra), out_...  84.4 us
    pallas_call x1, Pallas kernels, prologue(): pl.pallas_call(functools.partial(prologue_kernel, n_req, n_blk), out_shap...  37.7 us
    unnamed x36, local copies, waits for them, and re-layouts  11.3 us
    pallas_call x1, Pallas kernels, self_branch(): pl.pallas_call(functools.partial(self_full_kernel, blocks.shape[0], tuple...  7.78 us
  transfers between devices with their start and end apart: 1, of which 0 were waited for; matrix products, arithmetic and copies ran while one was open for 4% of the time, Pallas kernels for 47%

profile of v20, /device:TPU:33, one launch (start us, length us, event | category | flops | bytes accessed | tf_op | source)
XLA Modules:
  0.0 171.5 jit_solution(17764152235063595447)
XLA Ops:
  7.2 0.0 copy-start
  7.2 0.0 all-gather.3.cloned.1.call-start
  7.2 0.8 bitcast_dynamic-update-slice_fusion
  8.0 0.8 constant_dynamic-update-slice_fusion.3
  8.8 0.7 constant_dynamic-update-slice_fusion.2
  9.5 0.9 constant_dynamic-update-slice_fusion.1
  10.5 0.8 constant_dynamic-update-slice_fusion
  11.3 0.7 copy-done.9
  11.9 0.0 all-gather.3.cloned.1.call-update
  12.0 1.2 dynamic_slice.16
  15.2 0.7 pad_add_fusion
  15.9 0.2 fusion.1
  16.0 0.5 slice.26
  17.9 1.0 convolution_reduce_fusion
  18.9 0.5 slice.33
  19.4 0.6 concatenate.10
  20.1 0.1 rev.3
  20.2 0.1 dynamic_slice.19
  20.3 0.7 pad_slice_fusion
  20.9 0.1 slice.28
  21.0 0.7 compare_select_fusion
  21.7 0.0 copy-done
  21.7 0.6 gather_fusion
  22.3 0.0 copy-done.10
  22.3 0.0 copy-done.11
  22.3 0.0 copy-done.12
  22.4 0.0 copy-start.13
  22.4 0.0 copy-start.3
  22.4 0.2 broadcast_select_fusion.ordered_ref
  22.6 37.7 %shard_map.185 = (bf16[4096,128]{1,0:T(8,128)(2,1)S(1)}, bf16[8,256,128]{2,1,0:T(8,128)(2,1)S(1)}) custom-call(bf16[8,256,256]{2,1,0:T(8,128)(2,1)S(1)} %broadcast_select_fusion.ordered_ref, bf16[256,128]{1,0:T(8,128)(2,1)S(1)} %pad_maximum_fusion.packed_ref), custom_call_target="tpu_custom_call" | custom-call | tf_op jit(solution)/shard_map/pallas_call | solution.py:845
  60.3 0.0 copy-start.7
  60.3 0.8 copy-done.7
  61.1 0.0 copy-done.3
  61.1 0.0 copy-start.8
  61.1 1.0 copy-done.8
  62.1 7.8 %shard_map.186.refs_0_ = bf16[512,1024]{1,0:T(8,128)(2,1)S(1)} custom-call(s32[3]{0:T(128)S(1)} %get-tuple-element.16.lens_ref.len_ref, bf16[512,1024]{1,0:T(8,128)(2,1)S(1)} %copy-done.3, f32[1,1024]{1,0:T(1,128)S(1)} %get-tuple-element.19.gain_ref, bf16[8,256,128]{2,1,0:T(8,128)(2,1)S(1)} %copy-done.8, bf16[4096,128]{1,0:T(8,128)(2,1)S(1)} %get-tuple-element.10.c_ref, ...), custom_call_target="tpu_custom_call" | custom-call | tf_op jit(solution)/shard_map/pallas_call | solution.py:565
  69.9 0.0 copy-start.4
  70.0 34.8 %shard_map.187 = (f32[32,1024]{1,0:T(8,128)S(1)}, bf16[512,1024]{1,0:T(8,128)(2,1)S(1)}) custom-call(bf16[512,1024]{1,0:T(8,128)(2,1)S(1)} %shard_map.186.refs_0_, f32[32,1024]{1,0:T(8,128)S(1)} %dynamic-slice_convert_fusion.refs_1_, f32[1,1024]{1,0:T(1,128)S(1)} %get-tuple-element.20.refs_2_), custom_call_target="tpu_custom_call" | custom-call | tf_op jit(solution)/shard_map/pallas_call | solution.py:328
  104.7 0.0 copy-start.5
  104.8 1.0 copy-done.5
  105.7 1.4 copy-done.1
  107.1 1.2 copy-done.6
  108.4 2.5 %shard_map.188.refs_0_ = bf16[512,1024]{1,0:T(8,128)(2,1)S(1)} custom-call(s32[3]{0:T(128)S(1)} %get-tuple-element.16.lens_ref.len_ref, bf16[512,1024]{1,0:T(8,128)(2,1)S(1)} %copy-done.6, bf16[512,1024]{1,0:T(8,128)(2,1)S(1)} %copy-done.4, bf16[8,784,128]{2,1,0:T(8,128)(2,1)S(1)} %bitcast.23), custom_call_target="tpu_custom_call" | custom-call | tf_op jit(solution)/shard_map/pallas_call | solution.py:410
  110.9 23.9 %shard_map.189 = (f32[32,1024]{1,0:T(8,128)S(1)}, bf16[512,1024]{1,0:T(8,128)(2,1)S(1)}) custom-call(bf16[512,1024]{1,0:T(8,128)(2,1)S(1)} %shard_map.188.refs_0_, f32[32,1024]{1,0:T(8,128)S(1)} %get-tuple-element.12.refs_1_, f32[1,1024]{1,0:T(1,128)S(1)} %get-tuple-element.18.refs_2_), custom_call_target="tpu_custom_call" | custom-call | tf_op jit(solution)/shard_map/pallas_call | solution.py:328
  134.8 2.2 %shard_map.190.refs_0_ = bf16[512,1024]{1,0:T(8,128)(2,1)S(1)} custom-call(bf16[512,1024]{1,0:T(8,128)(2,1)S(1)} %get-tuple-element.13.normed_ref, bf16[8,784,128]{2,1,0:T(8,128)(2,1)S(1)} %bitcast.24), custom_call_target="tpu_custom_call" | custom-call | tf_op jit(solution)/shard_map/pallas_call | solution.py:421
  137.0 25.7 %shard_map.191 = (f32[32,1024]{1,0:T(8,128)}, bf16[512,1024]{1,0:T(8,128)(2,1)S(1)}) custom-call(bf16[512,1024]{1,0:T(8,128)(2,1)S(1)} %shard_map.190.refs_0_, f32[32,1024]{1,0:T(8,128)S(1)} %get-tuple-element.14.refs_1_, f32[1,1024]{1,0:T(1,128)S(1)} %get-tuple-element.18.refs_2_), custom_call_target="tpu_custom_call" | custom-call | tf_op jit(solution)/shard_map/pallas_call | solution.py:328
  162.7 1.0 copy.26
  163.7 1.0 copy.27
  (19 shorter events, 0.1 us)
Async XLA Ops:
  7.2 14.5 %copy-start = (bf16[8,256,256]{2,1,0:T(8,128)(2,1)S(1)}, bf16[8,256,256]{2,1,0:T(8,128)(2,1)}, u32[]{:S(2)}) copy-start(bf16[8,256,256]{2,1,0:T(8,128)(2,1)} %param.20) | copy-start | bytes 3145732
  7.2 98.5 %all-gather.3.cloned.1.call-start = ((), (), s32[]{:S(2)}) async-start(), calls=%async_computation | async-start | bytes 1806336 | tf_op jit(solution)/shard_map/all_gather | solution.py:887
  8.0 14.3 %copy-start.10 = (bf16[128,2,64]{0,2,1:T(8,128)(2,1)S(1)}, bf16[128,2,64]{0,2,1:T(8,128)(2,1)}, u32[]{:S(2)}) copy-start(bf16[128,2,64]{0,2,1:T(8,128)(2,1)} %param.29) | copy-start | bytes 98308
  8.0 14.3 %copy-start.11 = (bf16[64,128]{1,0:T(8,128)(2,1)S(1)}, bf16[64,128]{1,0:T(8,128)(2,1)}, u32[]{:S(2)}) copy-start(bf16[64,128]{1,0:T(8,128)(2,1)} %param.30) | copy-start | bytes 49156
  8.0 14.3 %copy-start.12 = (bf16[128,64]{0,1:T(8,128)(2,1)S(1)}, bf16[128,64]{0,1:T(8,128)(2,1)}, u32[]{:S(2)}) copy-start(bf16[128,64]{0,1:T(8,128)(2,1)} %param.28) | copy-start | bytes 49156
  9.5 12.8 %copy-start.14 = (s32[8]{0:T(128)S(1)}, s32[8]{0:T(128)}, u32[]{:S(2)}) copy-start(s32[8]{0:T(128)} %param.21) | copy-start | bytes 100
  11.3 0.7 copy-start.9
  22.4 38.7 %copy-start.13 = (f32[3,1024]{1,0:T(4,128)S(1)}, f32[3,1024]{1,0:T(4,128)}, u32[]{:S(2)}) copy-start(f32[3,1024]{1,0:T(4,128)} %param.27) | copy-start | bytes 36868
  22.4 38.7 %copy-start.3 = (bf16[512,1024]{1,0:T(8,128)(2,1)S(1)}, bf16[512,1024]{1,0:T(8,128)(2,1)}, u32[]{:S(2)}) copy-start(bf16[512,1024]{1,0:T(8,128)(2,1)} %x_ref.1) | copy-start | bytes 3145732
  60.3 0.8 copy-start.7
  61.1 1.0 copy-start.8
  69.9 35.8 %copy-start.4 = (bf16[512,1024]{1,0:T(8,128)(2,1)S(1)}, bf16[512,1024]{1,0:T(8,128)(2,1)}, u32[]{:S(2)}) copy-start(bf16[512,1024]{1,0:T(8,128)(2,1)} %enc_ref.1) | copy-start | bytes 3145732
  104.7 1.0 copy-start.5
  105.7 1.4 copy-start.1
  107.1 1.2 copy-start.6
  108.4 26.4 %copy-start.2 = (bf16[6272,128]{1,0:T(8,128)(2,1)S(1)}, bf16[6272,128]{1,0:T(8,128)(2,1)}, u32[]{:S(2)}) copy-start(bf16[6272,128]{1,0:T(8,128)(2,1)} %all-gather.3.cloned.1.call-done) | copy-start | bytes 4816900
Sparse Core Ops, SparseCore 0:
  12.1 68.6 all-gather.2
